TPU v7x, 128 devices: a whole 4x4x4 slice. The times are simulated.
128 devices in a mesh: seq: 4 (over x), tensor: 32 (over z, y, core).
Axes of the slice: x: 4, y: 4, z: 4, core: 2. Of those that a mesh axis runs over, the one named last changes fastest.
Arguments:
- states: bfloat16 [64, 2048], P('tensor'), may hold values from -6 to 6
- attn_gain: bfloat16 [2048], replicated, may hold values from 0.5 to 1.5
- w_qkv: bfloat16 [2048, 3, 2048], P(None, None, 'tensor'), may hold values from -0.125 to 0.125
- w_out: bfloat16 [2048, 2048], P('tensor'), may hold values from -0.125 to 0.125
- mlp_gain: bfloat16 [2048], replicated, may hold values from 0.5 to 1.5
- w_gate_up: bfloat16 [2048, 2, 8192], P(None, None, 'tensor'), may hold values from -0.125 to 0.125
- w_down: bfloat16 [8192, 2048], P('tensor'), may hold values from -0.0625 to 0.0625
- key_cache: bfloat16 [64, 2048, 4096], P('tensor', None, 'seq')
- value_cache: bfloat16 [64, 2048, 4096], P('tensor', None, 'seq')
- sink_keys: bfloat16 [64, 2048, 4], P('tensor'), may hold values from -8 to 8
- sink_values: bfloat16 [64, 2048, 4], P('tensor'), may hold values from -6 to 6
- cache_len: int32 [64], replicated, may hold values from 1 to 4096, as said below
- slot_mask: int32 [64, 4096], P('tensor', 'seq'), may hold values 0 or 1
- slot_pos: int32 [64, 4096], P('tensor', 'seq'), may hold values from 0 to 8191
- new_pos: int32 [64], replicated, may hold values from 4096 to 8191
Outputs:
- out_states: bfloat16 [64, 2048], P('tensor')
- new_keys: bfloat16 [64, 2048], P(None, 'tensor')
- new_values: bfloat16 [64, 2048], P(None, 'tensor')
Inputs may be any that keep to these rules, and one draw needn't show every extreme that they name: `cache_len`: at least one request has all 4096 slots filled in every draw.
All inputs are finite; a program needn't handle non-finite values. No bound on the sum of `slot_mask` on one device may be relied on, other than what follows from the above.
Results may differ from a plain program's by a relative error of at most 0.02.
The roundings to bfloat16 on the way count: a program that leaves them out, or rounds other values in their place, can miss the bound.
Values may be sent and summed in bfloat16 or wider, within the bound.
A program may use at most 64 MiB of HBM per device.

v0:
```python
import jax
import jax.numpy as jnp
from jax import lax
from jax.sharding import PartitionSpec as P

HEAD_SIZE = 64
WINDOW = 4096


NEG = -1e30


def rms_norm(values, gain):
    meansq = jnp.mean(values * values, axis=-1, keepdims=True)
    return (values * lax.rsqrt(meansq + 1e-05) * gain.astype(jnp.float32)).astype(jnp.bfloat16)


def rotary(tensor, cosine, sine):
    half = tensor.shape[-1] // 2
    turned = jnp.concatenate([-tensor[..., half:], tensor[..., :half]], axis=-1)
    return tensor * cosine + turned * sine


def undo_round(weights):
    rounded = lax.optimization_barrier(weights.astype(jnp.bfloat16))
    return rounded.astype(jnp.float32)


def per_device(
    states,
    attn_gain,
    w_qkv,
    w_out,
    mlp_gain,
    w_gate_up,
    w_down,
    key_cache,
    value_cache,
    sink_keys,
    sink_values,
    cache_len,
    slot_mask,
    slot_pos,
    new_pos,
):
    rows = states.shape[0]
    width = states.shape[1]
    row_start = lax.axis_index("tensor") * rows
    floats = states.astype(jnp.float32)
    normed = rms_norm(floats, attn_gain)
    lanes = w_qkv.shape[2]
    heads_here = lanes // HEAD_SIZE
    qkv_matrix = w_qkv.reshape(width, 3 * lanes)
    projected = jnp.dot(
        lax.all_gather(normed, "tensor", axis=0, tiled=True),
        qkv_matrix,
        preferred_element_type=jnp.float32,
    )
    batch = projected.shape[0]
    projected = projected.reshape(batch, 3, heads_here, HEAD_SIZE)
    half = HEAD_SIZE // 2
    inverse = jnp.exp(
        -jnp.log(jnp.float32(130000.0)) * jnp.arange(half, dtype=jnp.float32) * (2.0 / HEAD_SIZE)
    )
    angle = new_pos.astype(jnp.float32)[:, None] * inverse[None, :]
    angle = jnp.concatenate([angle, angle], axis=-1)[:, None, :]
    cosine = jnp.cos(angle)
    sine = jnp.sin(angle)
    queries_all = rotary(projected[:, 0], cosine, sine).astype(jnp.bfloat16)
    keys_all = rotary(projected[:, 1], cosine, sine).astype(jnp.bfloat16)
    values_all = projected[:, 2].astype(jnp.bfloat16)
    stacked = jnp.stack([queries_all, keys_all, values_all], axis=1)
    mine = lax.all_to_all(stacked, "tensor", split_axis=0, concat_axis=2, tiled=True)
    queries = mine[:, 0]
    keys_new = mine[:, 1]
    values_new = mine[:, 2]
    all_heads = queries.shape[1]
    own_len = lax.dynamic_slice_in_dim(cache_len, row_start, rows, 0)
    own_pos = lax.dynamic_slice_in_dim(new_pos, row_start, rows, 0)
    window_here = key_cache.shape[2]
    seq_index = lax.axis_index("seq")
    slots = seq_index * window_here + jnp.arange(window_here, dtype=jnp.int32)
    live = (slots[None, :] < own_len[:, None]) & (slot_mask == 1)
    live = live & (slot_pos < own_pos[:, None]) & (own_pos[:, None] - slot_pos < WINDOW)
    live = live[:, None, :]
    first_shard = seq_index == 0
    kwin = key_cache.reshape(rows, all_heads, HEAD_SIZE, window_here)
    vwin = value_cache.reshape(rows, all_heads, HEAD_SIZE, window_here)
    sink_key_rows = sink_keys.reshape(rows, all_heads, HEAD_SIZE, sink_keys.shape[2])
    vsink = sink_values.reshape(rows, all_heads, HEAD_SIZE, sink_values.shape[2])
    score_win = (
        jnp.einsum("bhd,bhds->bhs", queries, kwin, preferred_element_type=jnp.float32) * 0.125
    )
    score_win = jnp.where(live, score_win, NEG)
    score_sink = (
        jnp.einsum("bhd,bhds->bhs", queries, sink_key_rows, preferred_element_type=jnp.float32)
        * 0.125
    )
    score_sink = jnp.where(first_shard, score_sink, NEG)
    score_new = jnp.sum(queries.astype(jnp.float32) * keys_new.astype(jnp.float32), axis=-1) * 0.125
    score_new = jnp.where(first_shard, score_new, NEG)
    local_top = jnp.maximum(
        jnp.maximum(jnp.max(score_win, axis=-1), jnp.max(score_sink, axis=-1)), score_new
    )
    top = lax.pmax(local_top, "seq")
    weight_win = jnp.where(live, jnp.exp(score_win - top[..., None]), 0.0)
    weight_sink = jnp.where(first_shard, jnp.exp(score_sink - top[..., None]), 0.0)
    weight_new = jnp.where(first_shard, jnp.exp(score_new - top), 0.0)
    total = jnp.sum(weight_win, axis=-1) + jnp.sum(weight_sink, axis=-1) + weight_new
    mixture = jnp.einsum(
        "bhs,bhds->bhd", weight_win.astype(jnp.bfloat16), vwin, preferred_element_type=jnp.float32
    )
    mixture = mixture + jnp.einsum(
        "bhs,bhds->bhd", weight_sink.astype(jnp.bfloat16), vsink, preferred_element_type=jnp.float32
    )
    mixture = mixture + undo_round(weight_new)[..., None] * values_new.astype(jnp.float32)
    total, mixture = (total, mixture)
    total, mixture = lax.psum((total, mixture), "seq")
    attended_own = (mixture / total[..., None]).astype(jnp.bfloat16)
    attended = lax.all_to_all(
        attended_own, "tensor", split_axis=1, concat_axis=0, tiled=True
    ).reshape(batch, lanes)
    units = w_gate_up.shape[2]
    gate_matrix = w_gate_up.reshape(width, 2 * units)
    block = attended
    projected_out = lax.psum_scatter(
        jnp.dot(block, w_out, preferred_element_type=jnp.float32).astype(jnp.bfloat16),
        "tensor",
        scatter_dimension=0,
        tiled=True,
    ).astype(jnp.float32)
    resid_part = (floats + projected_out).astype(jnp.bfloat16)
    normed2 = rms_norm(resid_part.astype(jnp.float32), mlp_gain)
    gate_up = jnp.dot(
        lax.all_gather(normed2, "tensor", axis=0, tiled=True),
        gate_matrix,
        preferred_element_type=jnp.float32,
    )
    hidden = (jax.nn.silu(gate_up[:, :units]) * gate_up[:, units:]).astype(jnp.bfloat16)
    block = hidden
    mlp_out = lax.psum_scatter(
        jnp.dot(block, w_down, preferred_element_type=jnp.float32).astype(jnp.bfloat16),
        "tensor",
        scatter_dimension=0,
        tiled=True,
    ).astype(jnp.float32)
    out_states = (resid_part.astype(jnp.float32) + mlp_out).astype(jnp.bfloat16)
    return (out_states, keys_all.reshape(batch, lanes), values_all.reshape(batch, lanes))


def solution(mesh):
    in_specs = (
        P("tensor", None),
        P(),
        P(None, None, "tensor"),
        P("tensor", None),
        P(),
        P(None, None, "tensor"),
        P("tensor", None),
        P("tensor", None, "seq"),
        P("tensor", None, "seq"),
        P("tensor", None, None),
        P("tensor", None, None),
        P(),
        P("tensor", "seq"),
        P("tensor", "seq"),
        P(),
    )
    out_specs = (P("tensor", None), P(None, "tensor"), P(None, "tensor"))
    return jax.shard_map(
        per_device, mesh=mesh, in_specs=in_specs, out_specs=out_specs, check_vma=False
    )
```

profile of v0, /device:TPU:1, one launch (start us, length us, event | category | flops | bytes accessed | tf_op | source)
XLA Modules:
  0.0 340.4 jit_solution(10589366295930931641)
XLA Ops:
  7.2 0.9 fusion.36
  9.6 27.6 %all-gather = bf16[32,2,2048]{2,1,0:T(2,128)(2,1)S(1)} all-gather(bf16[1,2,2048]{2,1,0:T(2,128)(2,1)S(1)} %fusion.48), channel_id=1, replica_groups=mesh['seq'=4,'tensor'=32] {'tensor'}, dimensions={0}, use_global_device_ids=true | all-gather | bytes 270336 | tf_op jit(solution)/shard_map/all_gather | solution.py:55
  37.3 1.5 convolution_bitcast_fusion
  41.1 5.1 %all-to-all-start = ((bf16[32,2,192]{2,1,0:T(2,128)(2,1)}), bf16[32,2,192]{2,1,0:T(2,128)(2,1)S(1)}, u32[]{:S(2)}, u32[]{:S(2)}) async-start(bf16[32,2,192]{2,1,0:T(2,128)(2,1)} %reshape.332), calls=%async_computation | async-start | bytes 65536 | tf_op jit(solution)/shard_map/all_to_all | solution.py:73
  47.7 0.8 compare_and_fusion
  48.5 0.9 reshape.310
  49.4 0.9 reshape.312
  50.2 3.2 all-to-all-done
  54.1 4.6 %fusion.34 = f32[2,32,1,1024]{3,2,1,0:T(1,128)S(1)} fusion(bf16[2,32,64,1024]{3,2,1,0:T(8,128)(2,1)} %bitcast.148, bf16[2,32,64,1]{2,0,1,3:T(2,128)(2,1)S(1)} %slice_bitcast_fusion.7), kind=kOutput, calls=%fused_computation.51 | convolution fusion | flops 8388608 | bytes 8658944 | tf_op jit(solution)/shard_map/bhd,bhds->bhs/dot_general | solution.py:92
  58.9 8.5 %pmax.7 = f32[2,32]{1,0:T(2,128)S(1)} all-reduce(f32[2,32]{1,0:T(2,128)S(1)} %maximum_maximum_fusion), channel_id=1, replica_groups=mesh['seq'=4,'tensor'=32] {'seq'}, use_global_device_ids=true, to_apply=%region_4.5 | all-reduce | flops 64 | bytes 512 | tf_op jit(solution)/shard_map/pmax | solution.py:105
  67.8 5.7 %fusion.2 = f32[2,32,1,64]{3,2,1,0:T(1,128)S(1)} fusion(bf16[2,32,64,1024]{3,2,1,0:T(8,128)(2,1)} %bitcast.157, bf16[2,32,1024,1]{2,1,0,3:T(8,128)(2,1)S(1)} %get-tuple-element.23), kind=kOutput, calls=%fused_computation.6 | convolution fusion | flops 8388608 | bytes 8536064 | tf_op jit(solution)/shard_map/bhs,bhds->bhd/dot_general | solution.py:110
  73.8 11.2 %all-reduce.2 = (f32[2,32,64]{2,0,1:T(2,128)S(1)}, f32[2,32]{1,0:T(2,128)S(1)}) all-reduce(f32[2,32,64]{2,0,1:T(2,128)S(1)} %fusion.30, f32[2,32]{1,0:T(2,128)S(1)} %get-tuple-element.36), channel_id=1, replica_groups=mesh['seq'=4,'tensor'=32] {'seq'}, use_global_device_ids=true, to_apply=%region_5.6 | all-reduce | flops 4160 | bytes 33280 | tf_op jit(solution)/shard_map/psum | solution.py:118
  85.8 9.7 %all-to-all-start.1 = ((bf16[2,32,64]{2,0,1:T(2,128)(2,1)}), bf16[2,32,64]{2,0,1:T(2,128)(2,1)S(1)}, u32[]{:S(2)}, u32[]{:S(2)}) async-start(bf16[2,32,64]{2,0,1:T(2,128)(2,1)} %divide_convert_fusion), calls=%async_computation.1 | async-start | bytes 32768 | tf_op jit(solution)/shard_map/all_to_all | solution.py:120
  95.5 6.8 %all-to-all-done.1 = bf16[2,32,64]{2,0,1:T(2,128)(2,1)S(1)} async-done(((bf16[2,32,64]{2,0,1:T(2,128)(2,1)}), bf16[2,32,64]{2,0,1:T(2,128)(2,1)S(1)}, u32[]{:S(2)}, u32[]{:S(2)}) %all-to-all-start.1) | async-done | bytes 8224 | tf_op jit(solution)/shard_map/all_to_all | solution.py:120
  102.3 0.9 convolution_convert_fusion.1
  104.0 2.0 copy.75
  107.3 94.1 %all-reduce.6.cloned.1.call-done = bf16[64,2048]{1,0:T(8,128)(2,1)} async-done(((bf16[64,2048]{1,0:T(8,128)(2,1)}), bf16[64,2048]{1,0:T(8,128)(2,1)}) %all-reduce.6.cloned.1.call-update) | async-done | bytes 262160
  201.4 0.9 fusion.40
  202.4 27.7 %all-gather.1 = bf16[32,2,2048]{2,1,0:T(2,128)(2,1)} all-gather(bf16[1,2,2048]{2,1,0:T(2,128)(2,1)S(1)} %fusion.47), channel_id=1, replica_groups=mesh['seq'=4,'tensor'=32] {'tensor'}, dimensions={0}, use_global_device_ids=true | all-gather | bytes 270336 | tf_op jit(solution)/shard_map/all_gather | solution.py:135
  230.1 1.1 reshape.320
  231.7 1.0 convolution_convert_fusion
  232.7 0.8 fusion.28
  234.2 98.0 %all-reduce.8.cloned.1.call-done = bf16[64,2048]{1,0:T(8,128)(2,1)} async-done(((bf16[64,2048]{1,0:T(8,128)(2,1)}), bf16[64,2048]{1,0:T(8,128)(2,1)}) %all-reduce.8.cloned.1.call-update) | async-done | bytes 262160
  332.2 1.4 fusion.43
  (59 shorter events, 10.4 us)
Async XLA Ops:
  7.2 224.5 %copy-start = (bf16[256,2048]{1,0:T(8,128)(2,1)S(1)}, bf16[256,2048]{1,0:T(8,128)(2,1)}, u32[]{:S(2)}) copy-start(bf16[256,2048]{1,0:T(8,128)(2,1)} %param.21) | copy-start | bytes 3145732
  41.1 12.3 %all-to-all-start = ((bf16[32,2,192]{2,1,0:T(2,128)(2,1)}), bf16[32,2,192]{2,1,0:T(2,128)(2,1)S(1)}, u32[]{:S(2)}, u32[]{:S(2)}) async-start(bf16[32,2,192]{2,1,0:T(2,128)(2,1)} %reshape.332), calls=%async_computation | async-start | bytes 65536 | tf_op jit(solution)/shard_map/all_to_all | solution.py:73
  58.7 36.8 %copy-start.3 = (bf16[2048]{0:T(1024)(128)(2,1)S(1)}, bf16[2048]{0:T(1024)(128)(2,1)}, u32[]{:S(2)}) copy-start(bf16[2048]{0:T(1024)(128)(2,1)} %param.19) | copy-start | bytes 12292
  58.7 43.6 %copy-start.1 = (bf16[64,2048]{1,0:T(8,128)(2,1)S(1)}, bf16[64,2048]{1,0:T(8,128)(2,1)}, u32[]{:S(2)}) copy-start(bf16[64,2048]{1,0:T(8,128)(2,1)} %param.18) | copy-start | bytes 786436
  58.7 47.4 %copy-start.4 = (u32[128]{0:T(128)S(1)}, u32[128]{0:T(128)}, u32[]{:S(2)}) copy-start(u32[128]{0:T(128)} %constant.53) | copy-start | bytes 1540
  58.7 142.7 %copy-start.2 = (bf16[2,2048]{1,0:T(2,128)(2,1)S(1)}, bf16[2,2048]{1,0:T(2,128)(2,1)}, u32[]{:S(2)}) copy-start(bf16[2,2048]{1,0:T(2,128)(2,1)} %param.15) | copy-start | bytes 24580
  85.8 16.5 %all-to-all-start.1 = ((bf16[2,32,64]{2,0,1:T(2,128)(2,1)}), bf16[2,32,64]{2,0,1:T(2,128)(2,1)S(1)}, u32[]{:S(2)}, u32[]{:S(2)}) async-start(bf16[2,32,64]{2,0,1:T(2,128)(2,1)} %divide_convert_fusion), calls=%async_computation.1 | async-start | bytes 32768 | tf_op jit(solution)/shard_map/all_to_all | solution.py:120
  95.5 106.0 %all-reduce.6.cloned.1.call-start = ((), (), s32[]{:S(2)}) async-start(), calls=%async_computation.2 | async-start | bytes 524288
  103.3 229.0 %all-reduce.8.cloned.1.call-start = ((), (), s32[]{:S(2)}) async-start(), calls=%async_computation.3 | async-start | bytes 524288
Sparse Core Ops, SparseCore 0:
  103.4 97.9 all-reduce.5
  232.8 99.3 all-reduce.7
where the time goes:
time: 341 us; the launch traced here: 340 us
  waiting for transfers between devices  202 us (59%)
  blocking collectives  75 us (22%)
  between operations  14.9 us (4%)
  starting transfers between devices  14.8 us (4%)
  matrix products  14.5 us (4%)
  local copies, waits for them, and re-layouts  9.84 us (3%)
  other arithmetic  9.15 us (3%)
    unnamed x4, waiting for transfers between devices  192 us
    all_gather x1, blocking collectives, per_device(): lax.all_gather(normed2, 'tensor', axis=0, tiled=True)  27.7 us
    all_gather x1, blocking collectives, per_device(): lax.all_gather(normed, 'tensor', axis=0, tiled=True)  27.6 us
    psum x1, blocking collectives, per_device(): total, mixture = lax.psum((total, mixture), 'seq')  11.2 us
    all_to_all x1, starting transfers between devices, per_device(): lax.all_to_all(attended_own, 'tensor', split_axis=1, concat_axis=0, tiled...  9.66 us
    pmax x1, blocking collectives, per_device(): top = lax.pmax(local_top, 'seq')  8.48 us
  transfers between devices with their start and end apart: 4, of which 4 were waited for; matrix products, arithmetic and copies ran while one was open for 3% of the time, Pallas kernels for 0%

commit v1 on v0

--- a/solution.py
+++ b/solution.py
@@ -1,6 +1,10 @@
+import functools
+
 import jax
 import jax.numpy as jnp
 from jax import lax
+from jax.experimental import pallas as pl
+from jax.experimental.pallas import tpu as pltpu
 from jax.sharding import PartitionSpec as P
 
 HEAD_SIZE = 64
@@ -8,6 +12,7 @@
 
 
 NEG = -1e30
+MESH_ID = pl.DeviceIdType.MESH
 
 
 def rms_norm(values, gain):
@@ -24,6 +29,77 @@
 def undo_round(weights):
     rounded = lax.optimization_barrier(weights.astype(jnp.bfloat16))
     return rounded.astype(jnp.float32)
+
+
+def _exchange_kernel(n, axis, gather, x_ref, y_ref, send_sem, recv_sem, local_sem):
+    me = lax.axis_index(axis)
+    barrier = pltpu.get_barrier_semaphore()
+
+    def greet(d, carry):
+        peer = lax.rem(me + d, n)
+        pl.semaphore_signal(barrier, 1, device_id={axis: peer}, device_id_type=MESH_ID)
+        return carry
+
+    lax.fori_loop(1, n, greet, 0)
+    pl.semaphore_wait(barrier, n - 1)
+
+    def source(j):
+        return x_ref if gather else x_ref.at[j]
+
+    def outgoing(d):
+        j = lax.rem(me + d, n)
+        return pltpu.make_async_remote_copy(
+            src_ref=source(j),
+            dst_ref=y_ref.at[me],
+            send_sem=send_sem.at[j],
+            recv_sem=recv_sem.at[me],
+            device_id={axis: j},
+            device_id_type=MESH_ID,
+        )
+
+    def incoming(d):
+        k = lax.rem(me + n - d, n)
+        return pltpu.make_async_remote_copy(
+            src_ref=source(k),
+            dst_ref=y_ref.at[k],
+            send_sem=send_sem.at[k],
+            recv_sem=recv_sem.at[k],
+            device_id={axis: k},
+            device_id_type=MESH_ID,
+        )
+
+    local = pltpu.make_async_copy(source(me), y_ref.at[me], local_sem)
+    local.start()
+
+    def start(d, carry):
+        outgoing(d).start()
+        return carry
+
+    lax.fori_loop(1, n, start, 0)
+
+    def finish(d, carry):
+        outgoing(d).wait_send()
+        incoming(d).wait_recv()
+        return carry
+
+    lax.fori_loop(1, n, finish, 0)
+    local.wait()
+
+
+def exchange(x, axis, n, cid, gather=False):
+    piece = x.shape if gather else x.shape[1:]
+    return pl.pallas_call(
+        functools.partial(_exchange_kernel, n, axis, gather),
+        out_shape=jax.ShapeDtypeStruct((n,) + tuple(piece), x.dtype),
+        in_specs=[pl.BlockSpec(memory_space=pl.ANY)],
+        out_specs=pl.BlockSpec(memory_space=pl.ANY),
+        scratch_shapes=[
+            pltpu.SemaphoreType.DMA((n,)),
+            pltpu.SemaphoreType.DMA((n,)),
+            pltpu.SemaphoreType.DMA(()),
+        ],
+        compiler_params=pltpu.CompilerParams(collective_id=cid, has_side_effects=True),
+    )(x)
 
 
 def per_device(
@@ -42,6 +118,8 @@
     slot_mask,
     slot_pos,
     new_pos,
+    tn,
+    sn,
 ):
     rows = states.shape[0]
     width = states.shape[1]
@@ -51,11 +129,8 @@
     lanes = w_qkv.shape[2]
     heads_here = lanes // HEAD_SIZE
     qkv_matrix = w_qkv.reshape(width, 3 * lanes)
-    projected = jnp.dot(
-        lax.all_gather(normed, "tensor", axis=0, tiled=True),
-        qkv_matrix,
-        preferred_element_type=jnp.float32,
-    )
+    normed_all = exchange(normed, "tensor", tn, 0, gather=True).reshape(tn * rows, width)
+    projected = jnp.dot(normed_all, qkv_matrix, preferred_element_type=jnp.float32)
     batch = projected.shape[0]
     projected = projected.reshape(batch, 3, heads_here, HEAD_SIZE)
     half = HEAD_SIZE // 2
@@ -70,7 +145,8 @@
     keys_all = rotary(projected[:, 1], cosine, sine).astype(jnp.bfloat16)
     values_all = projected[:, 2].astype(jnp.bfloat16)
     stacked = jnp.stack([queries_all, keys_all, values_all], axis=1)
-    mine = lax.all_to_all(stacked, "tensor", split_axis=0, concat_axis=2, tiled=True)
+    mine = exchange(stacked.reshape(tn, rows, 3, heads_here, HEAD_SIZE), "tensor", tn, 1)
+    mine = jnp.transpose(mine, (1, 2, 0, 3, 4)).reshape(rows, 3, tn * heads_here, HEAD_SIZE)
     queries = mine[:, 0]
     keys_new = mine[:, 1]
     values_new = mine[:, 2]
@@ -102,10 +178,9 @@
     local_top = jnp.maximum(
         jnp.maximum(jnp.max(score_win, axis=-1), jnp.max(score_sink, axis=-1)), score_new
     )
-    top = lax.pmax(local_top, "seq")
-    weight_win = jnp.where(live, jnp.exp(score_win - top[..., None]), 0.0)
-    weight_sink = jnp.where(first_shard, jnp.exp(score_sink - top[..., None]), 0.0)
-    weight_new = jnp.where(first_shard, jnp.exp(score_new - top), 0.0)
+    weight_win = jnp.where(live, jnp.exp(score_win - local_top[..., None]), 0.0)
+    weight_sink = jnp.where(first_shard, jnp.exp(score_sink - local_top[..., None]), 0.0)
+    weight_new = jnp.where(first_shard, jnp.exp(score_new - local_top), 0.0)
     total = jnp.sum(weight_win, axis=-1) + jnp.sum(weight_sink, axis=-1) + weight_new
     mixture = jnp.einsum(
         "bhs,bhds->bhd", weight_win.astype(jnp.bfloat16), vwin, preferred_element_type=jnp.float32
@@ -114,36 +189,29 @@
         "bhs,bhds->bhd", weight_sink.astype(jnp.bfloat16), vsink, preferred_element_type=jnp.float32
     )
     mixture = mixture + undo_round(weight_new)[..., None] * values_new.astype(jnp.float32)
-    total, mixture = (total, mixture)
-    total, mixture = lax.psum((total, mixture), "seq")
+    packed = jnp.concatenate([mixture, total[..., None], local_top[..., None]], axis=-1)
+    parts = exchange(packed, "seq", sn, 2, gather=True)
+    part_top = parts[..., HEAD_SIZE + 1]
+    top = jnp.max(part_top, axis=0)
+    scale = jnp.exp(part_top - top[None])
+    total = jnp.sum(parts[..., HEAD_SIZE] * scale, axis=0)
+    mixture = jnp.sum(parts[..., :HEAD_SIZE] * scale[..., None], axis=0)
     attended_own = (mixture / total[..., None]).astype(jnp.bfloat16)
-    attended = lax.all_to_all(
-        attended_own, "tensor", split_axis=1, concat_axis=0, tiled=True
-    ).reshape(batch, lanes)
+    to_send = jnp.transpose(attended_own.reshape(rows, tn, lanes), (1, 0, 2))
+    attended = exchange(to_send, "tensor", tn, 3).reshape(batch, lanes)
     units = w_gate_up.shape[2]
     gate_matrix = w_gate_up.reshape(width, 2 * units)
-    block = attended
-    projected_out = lax.psum_scatter(
-        jnp.dot(block, w_out, preferred_element_type=jnp.float32).astype(jnp.bfloat16),
-        "tensor",
-        scatter_dimension=0,
-        tiled=True,
-    ).astype(jnp.float32)
+    partial_out = jnp.dot(attended, w_out, preferred_element_type=jnp.float32).astype(jnp.bfloat16)
+    pieces = exchange(partial_out.reshape(tn, rows, width), "tensor", tn, 4)
+    projected_out = jnp.sum(pieces.astype(jnp.float32), axis=0)
     resid_part = (floats + projected_out).astype(jnp.bfloat16)
     normed2 = rms_norm(resid_part.astype(jnp.float32), mlp_gain)
-    gate_up = jnp.dot(
-        lax.all_gather(normed2, "tensor", axis=0, tiled=True),
-        gate_matrix,
-        preferred_element_type=jnp.float32,
-    )
+    normed2_all = exchange(normed2, "tensor", tn, 5, gather=True).reshape(tn * rows, width)
+    gate_up = jnp.dot(normed2_all, gate_matrix, preferred_element_type=jnp.float32)
     hidden = (jax.nn.silu(gate_up[:, :units]) * gate_up[:, units:]).astype(jnp.bfloat16)
-    block = hidden
-    mlp_out = lax.psum_scatter(
-        jnp.dot(block, w_down, preferred_element_type=jnp.float32).astype(jnp.bfloat16),
-        "tensor",
-        scatter_dimension=0,
-        tiled=True,
-    ).astype(jnp.float32)
+    partial_down = jnp.dot(hidden, w_down, preferred_element_type=jnp.float32).astype(jnp.bfloat16)
+    pieces = exchange(partial_down.reshape(tn, rows, width), "tensor", tn, 6)
+    mlp_out = jnp.sum(pieces.astype(jnp.float32), axis=0)
     out_states = (resid_part.astype(jnp.float32) + mlp_out).astype(jnp.bfloat16)
     return (out_states, keys_all.reshape(batch, lanes), values_all.reshape(batch, lanes))
 
@@ -167,6 +235,7 @@
         P(),
     )
     out_specs = (P("tensor", None), P(None, "tensor"), P(None, "tensor"))
+    body = functools.partial(per_device, tn=mesh.shape["tensor"], sn=mesh.shape["seq"])
     return jax.shard_map(
-        per_device, mesh=mesh, in_specs=in_specs, out_specs=out_specs, check_vma=False
-    )
+        body, mesh=mesh, in_specs=in_specs, out_specs=out_specs, check_vma=False
+    )

time: 341 us -> 112 us (0.33)
  waiting for transfers between devices: 202 us -> 0 us
  blocking collectives: 75 us -> 0 us
  Pallas kernels: 0 us -> 69.7 us
  starting transfers between devices: 14.8 us -> 0 us
  between operations: 14.9 us -> 0.93 us
  other arithmetic: 9.15 us -> 15.3 us
    unnamed x4 -> x0, waiting for transfers between devices: 192 us -> none
    pallas_call x0 -> x7, Pallas kernels: none -> 69.7 us  [exchange(): pl.pallas_call(functools.partial(_exchange_kernel, n, axis, gather), out_...]
    all_gather x2 -> x0, blocking collectives: 55.4 us -> none  [the longest x1 27.7 us: per_device(): lax.all_gather(normed2, 'tensor', axis=0, tiled=True)]
    all_to_all x2 -> x0, starting transfers between devices: 14.7 us -> none  [the longest x1 9.66 us: per_device(): lax.all_to_all(attended_own, 'tensor', split_axis=1, concat_axis=0, tiled...]
    psum x1 -> x0, blocking collectives: 11.2 us -> none  [per_device(): total, mixture = lax.psum((total, mixture), 'seq')]
    all_to_all x2 -> x0, waiting for transfers between devices: 10 us -> none  [the longest x1 6.79 us: per_device(): lax.all_to_all(attended_own, 'tensor', split_axis=1, concat_axis=0, tiled...]
    pmax x1 -> x0, blocking collectives: 8.48 us -> none  [per_device(): top = lax.pmax(local_top, 'seq')]
    unnamed x18 -> x9, local copies, waits for them, and re-layouts: 6.02 us -> 1.86 us
  transfers between devices with their start and end apart: 4 -> 0, of which waited for: 4 -> 0; matrix products, arithmetic and copies ran while one was open for 3% -> 0% of each run, Pallas kernels for 0% -> 0%
where the time goes in v1:
time: 112 us; the launch traced here: 111 us
  Pallas kernels  69.7 us (62%)
  other arithmetic  15.3 us (14%)
  matrix products  14.3 us (13%)
  local copies, waits for them, and re-layouts  10.9 us (10%)
    pallas_call x7, Pallas kernels, exchange(): pl.pallas_call(functools.partial(_exchange_kernel, n, axis, gather), out_...  69.7 us
    dot_general x1, matrix products, per_device(): jnp.einsum('bhs,bhds->bhd', weight_win.astype(jnp.bfloat16), vwin, prefer...  5.86 us
    dot_general x1, matrix products, per_device(): jnp.einsum('bhd,bhds->bhs', queries, kwin, preferred_element_type=jnp.flo...  4.58 us

profile of v1, /device:TPU:1, one launch (start us, length us, event | category | flops | bytes accessed | tf_op | source)
XLA Modules:
  0.0 111.1 jit_solution(16026237712887815471)
XLA Ops:
  5.2 1.4 %fusion.40.x_ref = bf16[2,2048]{1,0:T(2,128)(2,1)} fusion(bf16[2,2048]{1,0:T(2,128)(2,1)} %param.15, f32[2]{0:T(128)S(1)} %add_rsqrt_fusion.1, f32[2048]{0:T(1024)S(1)} %convert_element_type.100), kind=kLoop, calls=%fused_computation.69 | loop fusion | flops 16384 | bytes 24584 | tf_op jit(solution)/shard_map/convert_element_type | solution.py:20
  7.3 0.9 reshape.396
  8.2 0.9 reshape.398
  9.1 14.7 %shard_map.166 = bf16[32,2,2048]{2,1,0:T(2,128)(2,1)} custom-call(bf16[2,2048]{1,0:T(2,128)(2,1)} %fusion.40.x_ref), custom_call_target="tpu_custom_call" | custom-call | tf_op jit(solution)/shard_map/pallas_call | solution.py:91
  23.8 1.0 reshape.406
  24.8 1.5 %fusion = f32[64,3,64]{0,2,1:T(8,128)S(1)} fusion(bf16[64,2048,1]{1,0,2:T(8,128)(2,1)S(1)} %reshape.406, bf16[2048,3,64]{0,2,1:T(8,128)(2,1)} %param.17), kind=kOutput, calls=%fused_computation.2 | convolution fusion | flops 50331648 | bytes 1097728 | tf_op jit(solution)/shard_map/dot_general | solution.py:133
  29.2 9.1 %shard_map.167 = bf16[32,2,3,1,64]{4,3,2,1,0:T(2,128)(2,1)} custom-call(bf16[32,2,3,1,64]{4,3,2,1,0:T(2,128)(2,1)} %pad_maximum_fusion.x_ref), custom_call_target="tpu_custom_call" | custom-call | tf_op jit(solution)/shard_map/pallas_call | solution.py:91
  38.3 0.9 copy.128
  39.6 4.6 %fusion.36 = f32[2,32,1,1024]{3,2,1,0:T(1,128)S(1)} fusion(bf16[2,32,64,1024]{3,2,1,0:T(8,128)(2,1)} %bitcast.117, bf16[2,32,64,1]{2,1,0,3:T(8,128)(2,1)S(1)} %slice_bitcast_fusion.7), kind=kOutput, calls=%fused_computation.59 | convolution fusion | flops 8388608 | bytes 8658944 | tf_op jit(solution)/shard_map/bhd,bhds->bhs/dot_general | solution.py:168
  44.6 5.9 %fusion.3 = f32[2,32,1,64]{3,2,1,0:T(1,128)S(1)} fusion(bf16[2,32,64,1024]{3,2,1,0:T(8,128)(2,1)} %bitcast.137, bf16[2,32,1024,1]{2,1,0,3:T(8,128)(2,1)S(1)} %get-tuple-element.27), kind=kOutput, calls=%fused_computation.8 | convolution fusion | flops 8388608 | bytes 8536064 | tf_op jit(solution)/shard_map/bhs,bhds->bhd/dot_general | solution.py:185
  51.9 5.7 %shard_map.168 = f32[4,2,32,66]{3,2,1,0:T(8,128)} custom-call(f32[2,32,66]{2,1,0:T(8,128)} %pad_maximum_fusion.2.x_ref), custom_call_target="tpu_custom_call" | custom-call | tf_op jit(solution)/shard_map/pallas_call | solution.py:91
  57.6 1.1 slice_reduce_fusion.2
  58.7 1.3 %slice_reduce_fusion.1 = (f32[4,2,32]{2,1,0:T(2,128)S(1)}, f32[4,2,32]{2,1,0:T(2,128)S(1)}, f32[4,2,32]{2,1,0:T(2,128)S(1)}) fusion(f32[4,2,32,66]{3,2,1,0:T(8,128)} %shard_map.168, f32[2,32]{1,0:T(2,128)S(1)} %slice_reduce_fusion.2), kind=kLoop, calls=%fused_computation.18 | loop fusion | flops 256 | bytes 5376 | tf_op jit(solution)/shard_map/slice | solution.py:194
  60.0 1.0 multiply_reduce_fusion
  61.8 9.5 %shard_map.169 = bf16[32,2,64]{2,1,0:T(2,128)(2,1)} custom-call(bf16[32,2,64]{2,1,0:T(2,128)(2,1)} %fusion.34.x_ref), custom_call_target="tpu_custom_call" | custom-call | tf_op jit(solution)/shard_map/pallas_call | solution.py:91
  71.3 1.2 %convolution_convert_fusion.1 = bf16[64,2048]{1,0:T(8,128)(2,1)S(1)} fusion(bf16[64,64]{1,0:T(8,128)(2,1)} %bitcast.133, bf16[64,2048]{1,0:T(8,128)(2,1)} %param.18), kind=kOutput, calls=%fused_computation.1 | convolution fusion | flops 16908288 | bytes 532480 | tf_op jit(solution)/shard_map/dot_general | solution.py:204
  72.5 0.9 reshape.400.x_ref
  73.3 10.2 %shard_map.170 = bf16[32,2,2048]{2,1,0:T(2,128)(2,1)} custom-call(bf16[32,2,2048]{2,1,0:T(2,128)(2,1)} %reshape.400.x_ref), custom_call_target="tpu_custom_call" | custom-call | tf_op jit(solution)/shard_map/pallas_call | solution.py:91
  83.5 1.2 %convert_reduce_fusion.1 = f32[2,2048]{1,0:T(2,128)S(1)} fusion(bf16[32,2,2048]{2,1,0:T(2,128)(2,1)} %shard_map.170), kind=kLoop, calls=%fused_computation.5 | loop fusion | flops 258048 | bytes 278528 | tf_op jit(solution)/shard_map/reduce_sum | solution.py:206
  85.6 10.4 %shard_map.171 = bf16[32,2,2048]{2,1,0:T(2,128)(2,1)} custom-call(bf16[2,2048]{1,0:T(2,128)(2,1)} %fusion.44.x_ref), custom_call_target="tpu_custom_call" | custom-call | tf_op jit(solution)/shard_map/pallas_call | solution.py:91
  95.9 1.0 reshape.401
  98.2 0.9 reshape.403.x_ref
  99.1 10.2 %shard_map.172 = bf16[32,2,2048]{2,1,0:T(2,128)(2,1)} custom-call(bf16[32,2,2048]{2,1,0:T(2,128)(2,1)} %reshape.403.x_ref), custom_call_target="tpu_custom_call" | custom-call | tf_op jit(solution)/shard_map/pallas_call | solution.py:91
  109.4 1.2 %convert_reduce_fusion = f32[2,2048]{1,0:T(2,128)S(1)} fusion(bf16[32,2,2048]{2,1,0:T(2,128)(2,1)} %shard_map.172), kind=kLoop, calls=%fused_computation.4 | loop fusion | flops 258048 | bytes 278528 | tf_op jit(solution)/shard_map/reduce_sum | solution.py:214
  (63 shorter events, 13.8 us)
Async XLA Ops:
  0.6 97.3 %copy-start = (bf16[256,2048]{1,0:T(8,128)(2,1)S(1)}, bf16[256,2048]{1,0:T(8,128)(2,1)}, u32[]{:S(2)}) copy-start(bf16[256,2048]{1,0:T(8,128)(2,1)} %param.21) | copy-start | bytes 3145732
  44.2 40.6 %copy-start.2 = (bf16[2,2048]{1,0:T(2,128)(2,1)S(1)}, bf16[2,2048]{1,0:T(2,128)(2,1)}, u32[]{:S(2)}) copy-start(bf16[2,2048]{1,0:T(2,128)(2,1)} %param.15) | copy-start | bytes 24580
  44.2 52.8 %copy-start.1 = (bf16[2048,2,256]{2,1,0:T(2,128)(2,1)S(1)}, bf16[2048,2,256]{2,1,0:T(2,128)(2,1)}, u32[]{:S(2)}) copy-start(bf16[2048,2,256]{2,1,0:T(2,128)(2,1)} %param.20) | copy-start | bytes 6291460

commit v2 on v1

--- a/solution.py
+++ b/solution.py
@@ -100,6 +100,129 @@
         ],
         compiler_params=pltpu.CompilerParams(collective_id=cid, has_side_effects=True),
     )(x)
+
+
+def _tail_kernel(
+    n,
+    att_ref,
+    w_out_ref,
+    states_ref,
+    gain_ref,
+    gate_ref,
+    down_ref,
+    out_ref,
+    abuf,
+    pbuf,
+    rbuf,
+    sbuf,
+    nbuf,
+    gbuf,
+    qbuf,
+    rbuf2,
+    send_sem,
+    recv_sem,
+    local_sem,
+):
+    axis = "tensor"
+    me = lax.axis_index(axis)
+    rows = states_ref.shape[0]
+    units = down_ref.shape[0]
+    barrier = pltpu.get_barrier_semaphore()
+
+    def greet(d, carry):
+        pl.semaphore_signal(
+            barrier, 1, device_id={axis: lax.rem(me + d, n)}, device_id_type=MESH_ID
+        )
+        return carry
+
+    lax.fori_loop(1, n, greet, 0)
+    pl.semaphore_wait(barrier, n - 1)
+
+    def phase(p, src_of, dst_of):
+        def outgoing(d):
+            j = lax.rem(me + d, n)
+            return pltpu.make_async_remote_copy(
+                src_ref=src_of(j),
+                dst_ref=dst_of(me),
+                send_sem=send_sem.at[p, j],
+                recv_sem=recv_sem.at[p, me],
+                device_id={axis: j},
+                device_id_type=MESH_ID,
+            )
+
+        def incoming(d):
+            k = lax.rem(me + n - d, n)
+            return pltpu.make_async_remote_copy(
+                src_ref=src_of(k),
+                dst_ref=dst_of(k),
+                send_sem=send_sem.at[p, k],
+                recv_sem=recv_sem.at[p, k],
+                device_id={axis: k},
+                device_id_type=MESH_ID,
+            )
+
+        local = pltpu.make_async_copy(src_of(me), dst_of(me), local_sem)
+        local.start()
+
+        def start(d, carry):
+            outgoing(d).start()
+            return carry
+
+        lax.fori_loop(1, n, start, 0)
+
+        def finish(d, carry):
+            outgoing(d).wait_send()
+            incoming(d).wait_recv()
+            return carry
+
+        lax.fori_loop(1, n, finish, 0)
+        local.wait()
+
+    def row_block(ref):
+        return lambda i: ref.at[pl.ds(i * rows, rows)]
+
+    phase(0, lambda j: att_ref.at[j], row_block(abuf))
+    partial = jnp.dot(abuf[...], w_out_ref[...], preferred_element_type=jnp.float32)
+    pbuf[...] = partial.astype(jnp.bfloat16)
+    phase(1, row_block(pbuf), lambda k: rbuf.at[k])
+    summed = jnp.sum(rbuf[...].astype(jnp.float32), axis=0)
+    resid = (states_ref[...].astype(jnp.float32) + summed).astype(jnp.bfloat16)
+    sbuf[...] = resid
+    nbuf[...] = rms_norm(resid.astype(jnp.float32), gain_ref[...])
+    phase(2, lambda j: nbuf, row_block(gbuf))
+    gate_up = jnp.dot(gbuf[...], gate_ref[...], preferred_element_type=jnp.float32)
+    hidden = (jax.nn.silu(gate_up[:, :units]) * gate_up[:, units:]).astype(jnp.bfloat16)
+    down = jnp.dot(hidden, down_ref[...], preferred_element_type=jnp.float32)
+    qbuf[...] = down.astype(jnp.bfloat16)
+    phase(3, row_block(qbuf), lambda k: rbuf2.at[k])
+    summed2 = jnp.sum(rbuf2[...].astype(jnp.float32), axis=0)
+    out_ref[...] = (sbuf[...].astype(jnp.float32) + summed2).astype(out_ref.dtype)
+
+
+def tail(att, w_out, states, gain, gate_matrix, w_down, n, cid):
+    rows, width = states.shape
+    lanes = att.shape[2]
+    vmem = pl.BlockSpec(memory_space=pltpu.VMEM)
+    return pl.pallas_call(
+        functools.partial(_tail_kernel, n),
+        out_shape=jax.ShapeDtypeStruct((rows, width), states.dtype),
+        in_specs=[vmem] * 6,
+        out_specs=vmem,
+        scratch_shapes=[
+            pltpu.VMEM((n * rows, lanes), jnp.bfloat16),
+            pltpu.VMEM((n * rows, width), jnp.bfloat16),
+            pltpu.VMEM((n, rows, width), jnp.bfloat16),
+            pltpu.VMEM((rows, width), jnp.bfloat16),
+            pltpu.VMEM((rows, width), jnp.bfloat16),
+            pltpu.VMEM((n * rows, width), jnp.bfloat16),
+            pltpu.VMEM((n * rows, width), jnp.bfloat16),
+            pltpu.VMEM((n, rows, width), jnp.bfloat16),
+            pltpu.SemaphoreType.DMA((4, n)),
+            pltpu.SemaphoreType.DMA((4, n)),
+            pltpu.SemaphoreType.DMA(()),
+        ],
+        compiler_params=pltpu.CompilerParams(collective_id=cid, has_side_effects=True),
+    )(att, w_out, states, gain.reshape(1, width), gate_matrix, w_down)
 
 
 def per_device(
@@ -198,21 +321,9 @@
     mixture = jnp.sum(parts[..., :HEAD_SIZE] * scale[..., None], axis=0)
     attended_own = (mixture / total[..., None]).astype(jnp.bfloat16)
     to_send = jnp.transpose(attended_own.reshape(rows, tn, lanes), (1, 0, 2))
-    attended = exchange(to_send, "tensor", tn, 3).reshape(batch, lanes)
     units = w_gate_up.shape[2]
     gate_matrix = w_gate_up.reshape(width, 2 * units)
-    partial_out = jnp.dot(attended, w_out, preferred_element_type=jnp.float32).astype(jnp.bfloat16)
-    pieces = exchange(partial_out.reshape(tn, rows, width), "tensor", tn, 4)
-    projected_out = jnp.sum(pieces.astype(jnp.float32), axis=0)
-    resid_part = (floats + projected_out).astype(jnp.bfloat16)
-    normed2 = rms_norm(resid_part.astype(jnp.float32), mlp_gain)
-    normed2_all = exchange(normed2, "tensor", tn, 5, gather=True).reshape(tn * rows, width)
-    gate_up = jnp.dot(normed2_all, gate_matrix, preferred_element_type=jnp.float32)
-    hidden = (jax.nn.silu(gate_up[:, :units]) * gate_up[:, units:]).astype(jnp.bfloat16)
-    partial_down = jnp.dot(hidden, w_down, preferred_element_type=jnp.float32).astype(jnp.bfloat16)
-    pieces = exchange(partial_down.reshape(tn, rows, width), "tensor", tn, 6)
-    mlp_out = jnp.sum(pieces.astype(jnp.float32), axis=0)
-    out_states = (resid_part.astype(jnp.float32) + mlp_out).astype(jnp.bfloat16)
+    out_states = tail(to_send, w_out, states, mlp_gain, gate_matrix, w_down, tn, 3)
     return (out_states, keys_all.reshape(batch, lanes), values_all.reshape(batch, lanes))
 
 

time: 112 us -> 99 us (0.88)
  Pallas kernels: 69.7 us -> 63.5 us
  other arithmetic: 15.3 us -> 10.9 us
  matrix products: 14.3 us -> 11.2 us
    pallas_call x7 -> x3, Pallas kernels: 69.7 us -> 29.5 us  [exchange(): pl.pallas_call(functools.partial(_exchange_kernel, n, axis, gather), out_...]
    pallas_call x0 -> x1, Pallas kernels: none -> 34 us  [tail(): pl.pallas_call(functools.partial(_tail_kernel, n), out_shape=jax.ShapeDty...]
    unnamed x9 -> x8, local copies, waits for them, and re-layouts: 1.86 us -> 4.52 us
    reduce_sum x2 -> x0, other arithmetic: 2.36 us -> none  [the longest x1 1.18 us: per_device(): projected_out = jnp.sum(pieces.astype(jnp.float32), axis=0)]
    dot_general x3 -> x0, matrix products: 1.93 us -> none  [the longest x1 1.17 us: per_device(): jnp.dot(attended, w_out, preferred_element_type=jnp.float32)]
    reshape x3 -> x1, local copies, waits for them, and re-layouts: 2.8 us -> 1.28 us  [tail(): gain.reshape(1, width)]
    dot_general x1, matrix products: 1.49 us -> 0.35 us  [per_device(): jnp.dot(normed_all, qkv_matrix, preferred_element_type=jnp.float32)]
where the time goes in v2:
time: 99 us; the launch traced here: 98.4 us
  Pallas kernels  63.5 us (64%)
  local copies, waits for them, and re-layouts  12 us (12%)
  matrix products  11.2 us (11%)
  other arithmetic  10.9 us (11%)
    pallas_call x1, Pallas kernels, tail(): pl.pallas_call(functools.partial(_tail_kernel, n), out_shape=jax.ShapeDty...  34 us
    pallas_call x3, Pallas kernels, exchange(): pl.pallas_call(functools.partial(_exchange_kernel, n, axis, gather), out_...  29.5 us
    dot_general x1, matrix products, per_device(): jnp.einsum('bhs,bhds->bhd', weight_win.astype(jnp.bfloat16), vwin, prefer...  5.85 us
    dot_general x1, matrix products, per_device(): jnp.einsum('bhd,bhds->bhs', queries, kwin, preferred_element_type=jnp.flo...  4.58 us
    unnamed x8, local copies, waits for them, and re-layouts  4.52 us

profile of v2, /device:TPU:1, one launch (start us, length us, event | category | flops | bytes accessed | tf_op | source)
XLA Modules:
  0.0 98.4 jit_solution(13488262095671204714)
XLA Ops:
  0.7 0.8 dynamic_slice.6
  1.5 0.7 dynamic_slice.7
  2.8 0.8 fusion.35
  3.7 0.8 compare_and_fusion
  5.2 1.4 %fusion.37.x_ref = bf16[2,2048]{1,0:T(2,128)(2,1)} fusion(bf16[2,2048]{1,0:T(2,128)(2,1)} %states_ref.1, f32[2]{0:T(128)S(1)} %add_rsqrt_fusion, f32[2048]{0:T(1024)S(1)} %convert_element_type.69), kind=kLoop, calls=%fused_computation.58 | loop fusion | flops 16384 | bytes 24584 | tf_op jit(solution)/shard_map/convert_element_type | solution.py:20
  6.6 1.3 %reshape.381.gain_ref = bf16[1,2048]{1,0:T(2,128)(2,1)} reshape(bf16[2048]{0:T(1024)(128)(2,1)} %param.19) | data formatting | bytes 8192 | tf_op jit(solution)/shard_map/reshape | solution.py:225
  7.9 0.9 reshape.378
  8.8 0.9 reshape.380
  9.7 14.7 %shard_map.166 = bf16[32,2,2048]{2,1,0:T(2,128)(2,1)} custom-call(bf16[2,2048]{1,0:T(2,128)(2,1)} %fusion.37.x_ref), custom_call_target="tpu_custom_call" | custom-call | tf_op jit(solution)/shard_map/pallas_call | solution.py:91
  24.4 1.0 %reshape.385 = bf16[64,2048,1]{1,0,2:T(8,128)(2,1)S(1)} reshape(bf16[32,2,2048]{2,1,0:T(2,128)(2,1)} %shard_map.166) | data formatting | bytes 524288 | tf_op jit(solution)/shard_map/reshape | solution.py:255
  27.0 0.7 copy.93
  27.8 0.8 pad_maximum_fusion.x_ref
  28.6 9.1 %shard_map.167 = bf16[32,2,3,1,64]{4,3,2,1,0:T(2,128)(2,1)} custom-call(bf16[32,2,3,1,64]{4,3,2,1,0:T(2,128)(2,1)} %pad_maximum_fusion.x_ref), custom_call_target="tpu_custom_call" | custom-call | tf_op jit(solution)/shard_map/pallas_call | solution.py:91
  37.7 0.9 copy.128
  39.0 4.6 %fusion.33 = f32[2,32,1,1024]{3,2,1,0:T(1,128)S(1)} fusion(bf16[2,32,64,1024]{3,2,1,0:T(8,128)(2,1)} %bitcast.111, bf16[2,32,64,1]{2,1,0,3:T(8,128)(2,1)S(1)} %slice_bitcast_fusion.7), kind=kOutput, calls=%fused_computation.52 | convolution fusion | flops 8388608 | bytes 8658944 | tf_op jit(solution)/shard_map/bhd,bhds->bhs/dot_general | solution.py:291
  44.0 5.9 %fusion.3 = f32[2,32,1,64]{3,2,1,0:T(1,128)S(1)} fusion(bf16[2,32,64,1024]{3,2,1,0:T(8,128)(2,1)} %bitcast.130, bf16[2,32,1024,1]{2,1,0,3:T(8,128)(2,1)S(1)} %get-tuple-element.25), kind=kOutput, calls=%fused_computation.4 | convolution fusion | flops 8388608 | bytes 8536064 | tf_op jit(solution)/shard_map/bhs,bhds->bhd/dot_general | solution.py:308
  51.3 5.7 %shard_map.168 = f32[4,2,32,66]{3,2,1,0:T(8,128)} custom-call(f32[2,32,66]{2,1,0:T(8,128)} %pad_maximum_fusion.2.x_ref), custom_call_target="tpu_custom_call" | custom-call | tf_op jit(solution)/shard_map/pallas_call | solution.py:91
  57.0 1.1 %slice_reduce_fusion.2 = f32[2,32]{1,0:T(2,128)S(1)} fusion(f32[4,2,32,66]{3,2,1,0:T(8,128)} %shard_map.168), kind=kLoop, calls=%fused_computation.15 | loop fusion | flops 192 | bytes 1280 | tf_op jit(solution)/shard_map/reduce_max | solution.py:318
  58.1 1.3 %slice_reduce_fusion.1 = (f32[4,2,32]{2,1,0:T(2,128)S(1)}, f32[4,2,32]{2,1,0:T(2,128)S(1)}, f32[4,2,32]{2,1,0:T(2,128)S(1)}) fusion(f32[4,2,32,66]{3,2,1,0:T(8,128)} %shard_map.168, f32[2,32]{1,0:T(2,128)S(1)} %slice_reduce_fusion.2), kind=kLoop, calls=%fused_computation.14 | loop fusion | flops 256 | bytes 5376 | tf_op jit(solution)/shard_map/slice | solution.py:317
  59.4 1.0 %multiply_reduce_fusion = f32[2,32,64]{2,1,0:T(8,128)S(1)} fusion(f32[4,2,32,66]{3,2,1,0:T(8,128)} %shard_map.168, f32[4,2,32]{2,1,0:T(2,128)S(1)} %get-tuple-element.19), kind=kLoop, calls=%fused_computation.12 | loop fusion | flops 28672 | bytes 82944 | tf_op jit(solution)/shard_map/reduce_sum | solution.py:321
  60.5 0.7 fusion.31.att_ref
  61.2 1.8 %copy.104 = bf16[256,8,2,256]{3,1,2,0:T(8,128)(2,1)} copy(bf16[256,8,2,256]{3,2,1,0:T(2,128)(2,1)S(1)} %bitcast.113) | data formatting | bytes 4194304
  63.0 34.0 %shard_map.169 = bf16[2,2048]{1,0:T(2,128)(2,1)} custom-call(bf16[32,2,64]{2,1,0:T(2,128)(2,1)} %fusion.31.att_ref, bf16[64,2048]{1,0:T(8,128)(2,1)} %w_out_ref.1, bf16[2,2048]{1,0:T(2,128)(2,1)} %states_ref.1, bf16[1,2048]{1,0:T(2,128)(2,1)} %reshape.381.gain_ref, bf16[2048,512]{1,0:T(8,128)(2,1)} %bitcast.112, bf16[256,2048]{1,0:T(8,128)(2,1)} %down_ref.1), custom_call_target="tpu_custom_call" | custom-call | tf_op jit(solution)/shard_map/pallas_call | solution.py:206
  97.1 1.3 %copy.130 = bf16[2,2048]{1,0:T(2,128)(2,1)} copy(bf16[2,2048]{1,0:T(2,128)(2,1)} %shard_map.169) | data formatting | bytes 16384
  (47 shorter events, 5.4 us)
Async XLA Ops:
  0.6 24.8 %copy-start = (bf16[2048,3,64]{0,2,1:T(8,128)(2,1)S(1)}, bf16[2048,3,64]{0,2,1:T(8,128)(2,1)}, u32[]{:S(2)}) copy-start(bf16[2048,3,64]{0,2,1:T(8,128)(2,1)} %param.17) | copy-start | bytes 2359300
  43.6 17.6 %copy-start.1 = (bf16[2048,2,256]{2,1,0:T(2,128)(2,1)S(1)}, bf16[2048,2,256]{2,1,0:T(2,128)(2,1)}, u32[]{:S(2)}) copy-start(bf16[2048,2,256]{2,1,0:T(2,128)(2,1)} %param.20) | copy-start | bytes 6291460

commit v3 on v2

--- a/solution.py
+++ b/solution.py
@@ -104,13 +104,18 @@
 
 def _tail_kernel(
     n,
-    att_ref,
+    sn,
+    part_ref,
     w_out_ref,
     states_ref,
     gain_ref,
     gate_ref,
     down_ref,
     out_ref,
+    seq_buf,
+    att_buf,
+    seq_send,
+    seq_recv,
     abuf,
     pbuf,
     rbuf,
@@ -125,8 +130,8 @@
 ):
     axis = "tensor"
     me = lax.axis_index(axis)
+    seq_me = lax.axis_index("seq")
     rows = states_ref.shape[0]
-    units = down_ref.shape[0]
     barrier = pltpu.get_barrier_semaphore()
 
     def greet(d, carry):
@@ -136,7 +141,63 @@
         return carry
 
     lax.fori_loop(1, n, greet, 0)
-    pl.semaphore_wait(barrier, n - 1)
+
+    def greet_seq(d, carry):
+        pl.semaphore_signal(
+            barrier, 1, device_id={"seq": lax.rem(seq_me + d, sn)}, device_id_type=MESH_ID
+        )
+        return carry
+
+    lax.fori_loop(1, sn, greet_seq, 0)
+    pl.semaphore_wait(barrier, n - 1 + sn - 1)
+
+    def seq_out(d):
+        j = lax.rem(seq_me + d, sn)
+        return pltpu.make_async_remote_copy(
+            src_ref=part_ref,
+            dst_ref=seq_buf.at[seq_me],
+            send_sem=seq_send.at[j],
+            recv_sem=seq_recv.at[seq_me],
+            device_id={"seq": j},
+            device_id_type=MESH_ID,
+        )
+
+    def seq_in(d):
+        k = lax.rem(seq_me + sn - d, sn)
+        return pltpu.make_async_remote_copy(
+            src_ref=part_ref,
+            dst_ref=seq_buf.at[k],
+            send_sem=seq_send.at[k],
+            recv_sem=seq_recv.at[k],
+            device_id={"seq": k},
+            device_id_type=MESH_ID,
+        )
+
+    seq_local = pltpu.make_async_copy(part_ref, seq_buf.at[seq_me], local_sem)
+    seq_local.start()
+
+    def seq_start(d, carry):
+        seq_out(d).start()
+        return carry
+
+    lax.fori_loop(1, sn, seq_start, 0)
+
+    def seq_finish(d, carry):
+        seq_out(d).wait_send()
+        seq_in(d).wait_recv()
+        return carry
+
+    lax.fori_loop(1, sn, seq_finish, 0)
+    seq_local.wait()
+    parts = seq_buf[...]
+    lanes = att_buf.shape[2]
+    part_top = parts[..., lanes + 1 : lanes + 2]
+    top = jnp.max(part_top, axis=0)
+    scale = jnp.exp(part_top - top[None])
+    total = jnp.sum(parts[..., lanes : lanes + 1] * scale, axis=0)
+    mixture = jnp.sum(parts[..., :lanes] * scale, axis=0)
+    att_buf[...] = (mixture / total).astype(att_buf.dtype)
+    units = down_ref.shape[0]
 
     def phase(p, src_of, dst_of):
         def outgoing(d):
@@ -181,7 +242,7 @@
     def row_block(ref):
         return lambda i: ref.at[pl.ds(i * rows, rows)]
 
-    phase(0, lambda j: att_ref.at[j], row_block(abuf))
+    phase(0, lambda j: att_buf.at[j], row_block(abuf))
     partial = jnp.dot(abuf[...], w_out_ref[...], preferred_element_type=jnp.float32)
     pbuf[...] = partial.astype(jnp.bfloat16)
     phase(1, row_block(pbuf), lambda k: rbuf.at[k])
@@ -199,16 +260,21 @@
     out_ref[...] = (sbuf[...].astype(jnp.float32) + summed2).astype(out_ref.dtype)
 
 
-def tail(att, w_out, states, gain, gate_matrix, w_down, n, cid):
+def tail(part, w_out, states, gain, w_gate_up, w_down, n, sn, cid):
     rows, width = states.shape
-    lanes = att.shape[2]
+    lanes = part.shape[2] - 2
+    units = w_gate_up.shape[2]
     vmem = pl.BlockSpec(memory_space=pltpu.VMEM)
     return pl.pallas_call(
-        functools.partial(_tail_kernel, n),
+        functools.partial(_tail_kernel, n, sn),
         out_shape=jax.ShapeDtypeStruct((rows, width), states.dtype),
         in_specs=[vmem] * 6,
         out_specs=vmem,
         scratch_shapes=[
+            pltpu.VMEM((sn,) + part.shape, jnp.float32),
+            pltpu.VMEM((n, rows, lanes), jnp.bfloat16),
+            pltpu.SemaphoreType.DMA((sn,)),
+            pltpu.SemaphoreType.DMA((sn,)),
             pltpu.VMEM((n * rows, lanes), jnp.bfloat16),
             pltpu.VMEM((n * rows, width), jnp.bfloat16),
             pltpu.VMEM((n, rows, width), jnp.bfloat16),
@@ -222,7 +288,7 @@
             pltpu.SemaphoreType.DMA(()),
         ],
         compiler_params=pltpu.CompilerParams(collective_id=cid, has_side_effects=True),
-    )(att, w_out, states, gain.reshape(1, width), gate_matrix, w_down)
+    )(part, w_out, states, gain.reshape(1, width), w_gate_up.reshape(width, 2 * units), w_down)
 
 
 def per_device(
@@ -313,17 +379,8 @@
     )
     mixture = mixture + undo_round(weight_new)[..., None] * values_new.astype(jnp.float32)
     packed = jnp.concatenate([mixture, total[..., None], local_top[..., None]], axis=-1)
-    parts = exchange(packed, "seq", sn, 2, gather=True)
-    part_top = parts[..., HEAD_SIZE + 1]
-    top = jnp.max(part_top, axis=0)
-    scale = jnp.exp(part_top - top[None])
-    total = jnp.sum(parts[..., HEAD_SIZE] * scale, axis=0)
-    mixture = jnp.sum(parts[..., :HEAD_SIZE] * scale[..., None], axis=0)
-    attended_own = (mixture / total[..., None]).astype(jnp.bfloat16)
-    to_send = jnp.transpose(attended_own.reshape(rows, tn, lanes), (1, 0, 2))
-    units = w_gate_up.shape[2]
-    gate_matrix = w_gate_up.reshape(width, 2 * units)
-    out_states = tail(to_send, w_out, states, mlp_gain, gate_matrix, w_down, tn, 3)
+    packed = jnp.transpose(packed, (1, 0, 2))
+    out_states = tail(packed, w_out, states, mlp_gain, w_gate_up, w_down, tn, sn, 3)
     return (out_states, keys_all.reshape(batch, lanes), values_all.reshape(batch, lanes))
 
 

time: 99 us -> 94.4 us (0.954)
  other arithmetic: 10.9 us -> 6.87 us
    pallas_call x3 -> x2, Pallas kernels: 29.5 us -> 23.8 us  [exchange(): pl.pallas_call(functools.partial(_exchange_kernel, n, axis, gather), out_...]
    pallas_call x1, Pallas kernels: 34 us -> 39 us  [tail(): pl.pallas_call(functools.partial(_tail_kernel, n, sn), out_shape=jax.Shap...]
    slice x1 -> x0, other arithmetic: 1.3 us -> none  [per_device(): part_top = parts[..., HEAD_SIZE + 1]]
    reduce_max x1 -> x0, other arithmetic: 1.08 us -> none  [per_device(): top = jnp.max(part_top, axis=0)]
    reduce_sum x2 -> x0, other arithmetic: 1.03 us -> none  [the longest x1 1.01 us: per_device(): mixture = jnp.sum(parts[..., :HEAD_SIZE] * scale[..., None], axis=0)]
where the time goes in v3:
time: 94.4 us; the launch traced here: 93.8 us
  Pallas kernels  62.7 us (66%)
  local copies, waits for them, and re-layouts  12.2 us (13%)
  matrix products  11.2 us (12%)
  other arithmetic  6.87 us (7%)
    pallas_call x1, Pallas kernels, tail(): pl.pallas_call(functools.partial(_tail_kernel, n, sn), out_shape=jax.Shap...  39 us
    pallas_call x2, Pallas kernels, exchange(): pl.pallas_call(functools.partial(_exchange_kernel, n, axis, gather), out_...  23.8 us
    dot_general x1, matrix products, per_device(): jnp.einsum('bhs,bhds->bhd', weight_win.astype(jnp.bfloat16), vwin, prefer...  5.85 us
    dot_general x1, matrix products, per_device(): jnp.einsum('bhd,bhds->bhs', queries, kwin, preferred_element_type=jnp.flo...  4.58 us
    unnamed x8, local copies, waits for them, and re-layouts  4.57 us

profile of v3, /device:TPU:1, one launch (start us, length us, event | category | flops | bytes accessed | tf_op | source)
XLA Modules:
  0.0 93.8 jit_solution(11400014005440375225)
XLA Ops:
  0.7 0.8 dynamic_slice.6
  1.5 0.7 dynamic_slice.7
  2.2 0.7 convert_element_type.67
  2.8 0.8 fusion.34
  3.7 0.8 compare_and_fusion
  4.5 0.7 convert_element_type.65
  5.2 1.4 %fusion.36.x_ref = bf16[2,2048]{1,0:T(2,128)(2,1)} fusion(bf16[2,2048]{1,0:T(2,128)(2,1)} %states_ref.1, f32[2]{0:T(128)S(1)} %add_rsqrt_fusion, f32[2048]{0:T(1024)S(1)} %convert_element_type.65), kind=kLoop, calls=%fused_computation.52 | loop fusion | flops 16384 | bytes 24584 | tf_op jit(solution)/shard_map/convert_element_type | solution.py:20
  6.6 1.3 %reshape.379.gain_ref = bf16[1,2048]{1,0:T(2,128)(2,1)} reshape(bf16[2048]{0:T(1024)(128)(2,1)} %param.19) | data formatting | bytes 8192 | tf_op jit(solution)/shard_map/reshape | solution.py:291
  7.9 0.9 reshape.376
  8.8 0.9 reshape.378
  9.7 14.7 %shard_map.166 = bf16[32,2,2048]{2,1,0:T(2,128)(2,1)} custom-call(bf16[2,2048]{1,0:T(2,128)(2,1)} %fusion.36.x_ref), custom_call_target="tpu_custom_call" | custom-call | tf_op jit(solution)/shard_map/pallas_call | solution.py:91
  24.4 1.0 %reshape.383 = bf16[64,2048,1]{1,0,2:T(8,128)(2,1)S(1)} reshape(bf16[32,2,2048]{2,1,0:T(2,128)(2,1)} %shard_map.166) | data formatting | bytes 524288 | tf_op jit(solution)/shard_map/reshape | solution.py:321
  25.4 0.3 fusion
  25.8 0.7 copy.82
  27.0 0.7 copy.81
  27.8 0.8 pad_maximum_fusion.x_ref
  28.6 9.1 %shard_map.167 = bf16[32,2,3,1,64]{4,3,2,1,0:T(2,128)(2,1)} custom-call(bf16[32,2,3,1,64]{4,3,2,1,0:T(2,128)(2,1)} %pad_maximum_fusion.x_ref), custom_call_target="tpu_custom_call" | custom-call | tf_op jit(solution)/shard_map/pallas_call | solution.py:91
  37.7 0.9 %copy.115 = bf16[32,2,3,1,64]{4,1,0,2,3:T(2,128)(2,1)S(1)} copy(bf16[32,2,3,1,64]{4,3,2,1,0:T(2,128)(2,1)} %shard_map.167) | data formatting | bytes 49152 | tf_op jit(solution)/shard_map/pallas_call | solution.py:91
  39.2 4.6 %fusion.32 = f32[2,32,1,1024]{3,2,1,0:T(1,128)S(1)} fusion(bf16[2,32,64,1024]{3,2,1,0:T(8,128)(2,1)} %bitcast.110, bf16[2,32,64,1]{2,0,1,3:T(2,128)(2,1)S(1)} %slice_bitcast_fusion.7), kind=kOutput, calls=%fused_computation.46 | convolution fusion | flops 8388608 | bytes 8658944 | tf_op jit(solution)/shard_map/bhd,bhds->bhs/dot_general | solution.py:357
  44.2 5.9 %fusion.3 = f32[2,32,1,64]{3,2,1,0:T(1,128)S(1)} fusion(bf16[2,32,64,1024]{3,2,1,0:T(8,128)(2,1)} %bitcast.126, bf16[2,32,1024,1]{2,1,0,3:T(8,128)(2,1)S(1)} %get-tuple-element.19), kind=kOutput, calls=%fused_computation.4 | convolution fusion | flops 8388608 | bytes 8536064 | tf_op jit(solution)/shard_map/bhs,bhds->bhd/dot_general | solution.py:374
  51.0 0.7 maximum_bitcast_fusion.part_ref
  51.7 1.9 %copy.92 = bf16[256,8,2,256]{3,1,2,0:T(8,128)(2,1)} copy(bf16[256,8,2,256]{3,2,1,0:T(2,128)(2,1)S(1)} %bitcast.112) | data formatting | bytes 4194304
  53.5 39.0 %shard_map.168 = bf16[2,2048]{1,0:T(2,128)(2,1)} custom-call(f32[32,2,66]{2,1,0:T(2,128)} %maximum_bitcast_fusion.part_ref, bf16[64,2048]{1,0:T(8,128)(2,1)} %w_out_ref.1, bf16[2,2048]{1,0:T(2,128)(2,1)} %states_ref.1, bf16[1,2048]{1,0:T(2,128)(2,1)} %reshape.379.gain_ref, bf16[2048,512]{1,0:T(8,128)(2,1)} %bitcast.111, bf16[256,2048]{1,0:T(8,128)(2,1)} %down_ref.1), custom_call_target="tpu_custom_call" | custom-call | tf_op jit(solution)/shard_map/pallas_call | solution.py:268
  92.5 1.3 %copy.117 = bf16[2,2048]{1,0:T(2,128)(2,1)} copy(bf16[2,2048]{1,0:T(2,128)(2,1)} %shard_map.168) | data formatting | bytes 16384
  (41 shorter events, 2.5 us)
Async XLA Ops:
  0.6 24.8 %copy-start = (bf16[2048,3,64]{0,2,1:T(8,128)(2,1)S(1)}, bf16[2048,3,64]{0,2,1:T(8,128)(2,1)}, u32[]{:S(2)}) copy-start(bf16[2048,3,64]{0,2,1:T(8,128)(2,1)} %param.17) | copy-start | bytes 2359300
  43.8 7.9 %copy-start.1 = (bf16[2048,2,256]{2,1,0:T(2,128)(2,1)S(1)}, bf16[2048,2,256]{2,1,0:T(2,128)(2,1)}, u32[]{:S(2)}) copy-start(bf16[2048,2,256]{2,1,0:T(2,128)(2,1)} %param.20) | copy-start | bytes 6291460

commit v4 on v3

--- a/solution.py
+++ b/solution.py
@@ -291,6 +291,93 @@
     )(part, w_out, states, gain.reshape(1, width), w_gate_up.reshape(width, 2 * units), w_down)
 
 
+def _head_kernel(n, x_ref, w_ref, trig_ref, qkv_ref, recv_ref, gbuf, send_sem, recv_sem, local_sem):
+    axis = "tensor"
+    me = lax.axis_index(axis)
+    rows = x_ref.shape[0]
+    block = qkv_ref.shape[1] // 2
+    barrier = pltpu.get_barrier_semaphore()
+
+    def greet(d, carry):
+        pl.semaphore_signal(
+            barrier, 1, device_id={axis: lax.rem(me + d, n)}, device_id_type=MESH_ID
+        )
+        return carry
+
+    lax.fori_loop(1, n, greet, 0)
+    pl.semaphore_wait(barrier, n - 1)
+
+    def phase(p, src_of, dst_of):
+        def outgoing(d):
+            j = lax.rem(me + d, n)
+            return pltpu.make_async_remote_copy(
+                src_ref=src_of(j),
+                dst_ref=dst_of(me),
+                send_sem=send_sem.at[p, j],
+                recv_sem=recv_sem.at[p, me],
+                device_id={axis: j},
+                device_id_type=MESH_ID,
+            )
+
+        def incoming(d):
+            k = lax.rem(me + n - d, n)
+            return pltpu.make_async_remote_copy(
+                src_ref=src_of(k),
+                dst_ref=dst_of(k),
+                send_sem=send_sem.at[p, k],
+                recv_sem=recv_sem.at[p, k],
+                device_id={axis: k},
+                device_id_type=MESH_ID,
+            )
+
+        local = pltpu.make_async_copy(src_of(me), dst_of(me), local_sem)
+        local.start()
+
+        def start(d, carry):
+            outgoing(d).start()
+            return carry
+
+        lax.fori_loop(1, n, start, 0)
+
+        def finish(d, carry):
+            outgoing(d).wait_send()
+            incoming(d).wait_recv()
+            return carry
+
+        lax.fori_loop(1, n, finish, 0)
+        local.wait()
+
+    phase(0, lambda j: x_ref, lambda k: gbuf.at[pl.ds(k * rows, rows)])
+    proj = jnp.dot(gbuf[...], w_ref[...], preferred_element_type=jnp.float32)
+    trig = trig_ref[...]
+    turned = proj[:, :block] * trig[:, :block] + proj[:, block : 2 * block] * trig[:, block:]
+    qkv_ref[:, :block] = turned.astype(qkv_ref.dtype)
+    qkv_ref[:, block:] = proj[:, 2 * block :].astype(qkv_ref.dtype)
+    phase(1, lambda j: qkv_ref.at[pl.ds(j * rows, rows)], lambda k: recv_ref.at[k])
+
+
+def head(normed, w_ext, trig, n, cid):
+    rows, width = normed.shape
+    cols = w_ext.shape[1] // 3 * 2
+    vmem = pl.BlockSpec(memory_space=pltpu.VMEM)
+    return pl.pallas_call(
+        functools.partial(_head_kernel, n),
+        out_shape=(
+            jax.ShapeDtypeStruct((n * rows, cols), jnp.bfloat16),
+            jax.ShapeDtypeStruct((n, rows, cols), jnp.bfloat16),
+        ),
+        in_specs=[vmem] * 3,
+        out_specs=(vmem, vmem),
+        scratch_shapes=[
+            pltpu.VMEM((n * rows, width), jnp.bfloat16),
+            pltpu.SemaphoreType.DMA((2, n)),
+            pltpu.SemaphoreType.DMA((2, n)),
+            pltpu.SemaphoreType.DMA(()),
+        ],
+        compiler_params=pltpu.CompilerParams(collective_id=cid, has_side_effects=True),
+    )(normed, w_ext, trig)
+
+
 def per_device(
     states,
     attn_gain,
@@ -318,24 +405,30 @@
     lanes = w_qkv.shape[2]
     heads_here = lanes // HEAD_SIZE
     qkv_matrix = w_qkv.reshape(width, 3 * lanes)
-    normed_all = exchange(normed, "tensor", tn, 0, gather=True).reshape(tn * rows, width)
-    projected = jnp.dot(normed_all, qkv_matrix, preferred_element_type=jnp.float32)
-    batch = projected.shape[0]
-    projected = projected.reshape(batch, 3, heads_here, HEAD_SIZE)
     half = HEAD_SIZE // 2
     inverse = jnp.exp(
         -jnp.log(jnp.float32(130000.0)) * jnp.arange(half, dtype=jnp.float32) * (2.0 / HEAD_SIZE)
     )
     angle = new_pos.astype(jnp.float32)[:, None] * inverse[None, :]
-    angle = jnp.concatenate([angle, angle], axis=-1)[:, None, :]
-    cosine = jnp.cos(angle)
-    sine = jnp.sin(angle)
-    queries_all = rotary(projected[:, 0], cosine, sine).astype(jnp.bfloat16)
-    keys_all = rotary(projected[:, 1], cosine, sine).astype(jnp.bfloat16)
-    values_all = projected[:, 2].astype(jnp.bfloat16)
-    stacked = jnp.stack([queries_all, keys_all, values_all], axis=1)
-    mine = exchange(stacked.reshape(tn, rows, 3, heads_here, HEAD_SIZE), "tensor", tn, 1)
-    mine = jnp.transpose(mine, (1, 2, 0, 3, 4)).reshape(rows, 3, tn * heads_here, HEAD_SIZE)
+    angle = jnp.concatenate([angle] * (4 * heads_here), axis=-1)
+    trig = jnp.concatenate([jnp.cos(angle), jnp.sin(angle)], axis=-1)
+    w_heads = w_qkv.reshape(width, 3, heads_here, HEAD_SIZE)
+    w_turned = jnp.concatenate([-w_heads[..., half:], w_heads[..., :half]], axis=-1)
+    w_ext = jnp.concatenate(
+        [
+            w_heads[:, 0:2].reshape(width, 2 * lanes),
+            w_turned[:, 0:2].reshape(width, 2 * lanes),
+            w_heads[:, 2].reshape(width, lanes),
+            jnp.zeros((width, lanes), w_qkv.dtype),
+        ],
+        axis=-1,
+    )
+    qkv_all, mine = head(normed, w_ext, trig, tn, 0)
+    batch = qkv_all.shape[0]
+    keys_all = qkv_all[:, lanes : 2 * lanes]
+    values_all = qkv_all[:, 2 * lanes : 3 * lanes]
+    mine = mine.reshape(tn, rows, 4, heads_here, HEAD_SIZE)
+    mine = jnp.transpose(mine, (1, 2, 0, 3, 4)).reshape(rows, 4, tn * heads_here, HEAD_SIZE)
     queries = mine[:, 0]
     keys_new = mine[:, 1]
     values_new = mine[:, 2]
@@ -381,7 +474,7 @@
     packed = jnp.concatenate([mixture, total[..., None], local_top[..., None]], axis=-1)
     packed = jnp.transpose(packed, (1, 0, 2))
     out_states = tail(packed, w_out, states, mlp_gain, w_gate_up, w_down, tn, sn, 3)
-    return (out_states, keys_all.reshape(batch, lanes), values_all.reshape(batch, lanes))
+    return (out_states, keys_all, values_all)
 
 
 def solution(mesh):

time: 94.4 us -> 92.1 us (0.976)
  Pallas kernels: 62.7 us -> 60.9 us
    concatenate x2 -> x3, other arithmetic: 0.01 us -> 2.73 us  [the longest x1 1.53 us: per_device(): jnp.concatenate([w_heads[:, 0:2].reshape(width, 2 * lanes), w_turned[:, 0...]
    slice x1 -> x4, local copies, waits for them, and re-layouts: 0.01 us -> 1.45 us  [the longest x1 0.68 us: per_device(): values_all = qkv_all[:, 2 * lanes:3 * lanes]]
    reshape x1 -> x4, local copies, waits for them, and re-layouts: 1.05 us -> 2.21 us  [the longest x1 1 us: per_device(): w_turned[:, 0:2].reshape(width, 2 * lanes)]
    unnamed x8 -> x21, local copies, waits for them, and re-layouts: 4.57 us -> 5.59 us
    pallas_call x2 -> x1, Pallas kernels: 23.8 us -> 22.7 us  [head(): pl.pallas_call(functools.partial(_head_kernel, n), out_shape=(jax.ShapeDt...]
    pallas_call x1 -> x0, local copies, waits for them, and re-layouts: 0.94 us -> none  [exchange(): pl.pallas_call(functools.partial(_exchange_kernel, n, axis, gather), out_...]
where the time goes in v4:
time: 92.1 us; the launch traced here: 91.7 us
  Pallas kernels  60.9 us (66%)
  local copies, waits for them, and re-layouts  12.4 us (13%)
  matrix products  10.8 us (12%)
  other arithmetic  6.76 us (7%)
    pallas_call x1, Pallas kernels, tail(): pl.pallas_call(functools.partial(_tail_kernel, n, sn), out_shape=jax.Shap...  38.2 us
    pallas_call x1, Pallas kernels, head(): pl.pallas_call(functools.partial(_head_kernel, n), out_shape=(jax.ShapeDt...  22.7 us
    dot_general x1, matrix products, per_device(): jnp.einsum('bhs,bhds->bhd', weight_win.astype(jnp.bfloat16), vwin, prefer...  5.8 us
    unnamed x21, local copies, waits for them, and re-layouts  5.59 us
    dot_general x1, matrix products, per_device(): jnp.einsum('bhd,bhds->bhs', queries, kwin, preferred_element_type=jnp.flo...  4.59 us

profile of v4, /device:TPU:1, one launch (start us, length us, event | category | flops | bytes accessed | tf_op | source)
XLA Modules:
  0.0 91.7 jit_solution(9178619343796052359)
XLA Ops:
  0.6 0.7 dynamic_slice.6
  1.4 0.7 dynamic_slice.7
  2.1 0.8 compare_and_fusion
  2.9 1.8 %copy.51 = bf16[2048,3,64]{2,0,1:T(8,128)(2,1)S(1)} copy(bf16[2048,3,64]{0,2,1:T(8,128)(2,1)} %param.17) | data formatting | bytes 1572864 | tf_op args[2]
  4.7 0.7 slice_negate_fusion
  5.4 0.6 pad_maximum_fusion
  6.0 0.3 copy.53
  6.3 1.0 %copy.55 = bf16[2048,128]{1,0:T(8,128)(2,1)} copy(bf16[2048,128]{0,1:T(8,128)(2,1)S(1)} %bitcast.82) | data formatting | bytes 1048576 | tf_op jit(solution)/shard_map/reshape | solution.py:420
  7.4 0.3 copy.52
  7.8 0.3 copy.54
  8.2 0.6 copy-done.1
  8.8 1.5 %maximum_maximum_fusion.w_ref = bf16[2048,384]{1,0:T(8,128)(2,1)} fusion(bf16[2048,64]{1,0:T(8,128)(2,1)S(1)} %slice_bitcast_fusion, bf16[2048,128]{1,0:T(8,128)(2,1)S(1)} %copy-done.1, bf16[2048,128]{1,0:T(8,128)(2,1)S(1)} %copy.54, bf16[384]{0:T(512)(128)(2,1)S(1)} %pad.12.clone), kind=kLoop, calls=%fused_computation.1 | loop fusion | flops 6291456 | bytes 2884352 | tf_op jit(solution)/shard_map/concatenate | solution.py:417
  10.6 0.6 pad_maximum_fusion.1.trig_ref
  11.4 0.7 fusion.20.x_ref
  12.1 22.7 %shard_map.166 = (bf16[64,256]{1,0:T(8,128)(2,1)}, bf16[32,2,256]{2,1,0:T(2,128)(2,1)}) custom-call(bf16[2,2048]{1,0:T(2,128)(2,1)} %fusion.20.x_ref, bf16[2048,384]{1,0:T(8,128)(2,1)} %maximum_maximum_fusion.w_ref, f32[64,256]{1,0:T(8,128)} %pad_maximum_fusion.1.trig_ref), custom_call_target="tpu_custom_call" | custom-call | tf_op jit(solution)/shard_map/pallas_call | solution.py:363
  34.8 0.9 reshape.152
  35.8 4.6 %fusion.14 = f32[2,32,1,1024]{3,2,1,0:T(1,128)S(1)} fusion(bf16[2,32,64,1024]{3,2,1,0:T(8,128)(2,1)} %bitcast.77, bf16[2,32,64,1]{2,0,1,3:T(2,128)(2,1)S(1)} %slice_bitcast_fusion.3), kind=kOutput, calls=%fused_computation.28 | convolution fusion | flops 8388608 | bytes 8658944 | tf_op jit(solution)/shard_map/bhd,bhds->bhs/dot_general | solution.py:450
  41.4 5.8 %fusion.1 = f32[2,32,1,64]{3,2,1,0:T(1,128)S(1)} fusion(bf16[2,32,64,1024]{3,2,1,0:T(8,128)(2,1)} %bitcast.88, bf16[2,32,1024,1]{2,1,0,3:T(8,128)(2,1)S(1)} %get-tuple-element.13), kind=kOutput, calls=%fused_computation.6 | convolution fusion | flops 8388608 | bytes 8536064 | tf_op jit(solution)/shard_map/bhs,bhds->bhd/dot_general | solution.py:467
  48.3 0.7 maximum_bitcast_fusion.part_ref
  49.1 1.9 %copy.75 = bf16[256,8,2,256]{3,1,2,0:T(8,128)(2,1)} copy(bf16[256,8,2,256]{3,2,1,0:T(2,128)(2,1)S(1)} %bitcast.84) | data formatting | bytes 4194304
  50.9 0.6 reshape.141.gain_ref
  51.5 38.2 %shard_map.167 = bf16[2,2048]{1,0:T(2,128)(2,1)} custom-call(f32[32,2,66]{2,1,0:T(2,128)} %maximum_bitcast_fusion.part_ref, bf16[64,2048]{1,0:T(8,128)(2,1)} %w_out_ref.1, bf16[2,2048]{1,0:T(2,128)(2,1)} %states_ref.1, bf16[1,2048]{1,0:T(2,128)(2,1)} %reshape.141.gain_ref, bf16[2048,512]{1,0:T(8,128)(2,1)} %bitcast.81, bf16[256,2048]{1,0:T(8,128)(2,1)} %down_ref.1), custom_call_target="tpu_custom_call" | custom-call | tf_op jit(solution)/shard_map/pallas_call | solution.py:268
  89.7 0.7 fusion.25
  90.4 1.3 %copy.100 = bf16[2,2048]{1,0:T(2,128)(2,1)} copy(bf16[2,2048]{1,0:T(2,128)(2,1)} %shard_map.167) | data formatting | bytes 16384
  (51 shorter events, 2.8 us)
Async XLA Ops:
  7.8 1.0 %copy-start.1 = (bf16[2048,128]{1,0:T(8,128)(2,1)S(1)}, bf16[2048,128]{1,0:T(8,128)(2,1)}, u32[]{:S(2)}) copy-start(bf16[2048,128]{1,0:T(8,128)(2,1)} %copy.55) | copy-start | bytes 1572868
  8.1 2.3 %copy-start.8 = (s32[64]{0:T(128)S(1)}, s32[64]{0:T(128)}, u32[]{:S(2)}) copy-start(s32[64]{0:T(128)} %param.29) | copy-start | bytes 772
  8.1 3.2 %copy-start.6 = (bf16[2048]{0:T(1024)(128)(2,1)S(1)}, bf16[2048]{0:T(1024)(128)(2,1)}, u32[]{:S(2)}) copy-start(bf16[2048]{0:T(1024)(128)(2,1)} %param.16) | copy-start | bytes 12292
  8.1 3.2 %copy-start.2 = (bf16[2,2048]{1,0:T(2,128)(2,1)S(1)}, bf16[2,2048]{1,0:T(2,128)(2,1)}, u32[]{:S(2)}) copy-start(bf16[2,2048]{1,0:T(2,128)(2,1)} %states_ref.1) | copy-start | bytes 24580
  35.8 4.7 %copy-start.3 = (bf16[2,2048,4]{1,2,0:T(4,128)(2,1)S(1)}, bf16[2,2048,4]{1,2,0:T(4,128)(2,1)}, u32[]{:S(2)}) copy-start(bf16[2,2048,4]{1,2,0:T(4,128)(2,1)} %param.24) | copy-start | bytes 98308
  41.4 6.0 %copy-start.4 = (bf16[2,2048,4]{1,2,0:T(4,128)(2,1)S(1)}, bf16[2,2048,4]{1,2,0:T(4,128)(2,1)}, u32[]{:S(2)}) copy-start(bf16[2,2048,4]{1,2,0:T(4,128)(2,1)} %param.25) | copy-start | bytes 98308
  41.4 7.6 %copy-start = (bf16[2048,2,256]{2,1,0:T(2,128)(2,1)S(1)}, bf16[2048,2,256]{2,1,0:T(2,128)(2,1)}, u32[]{:S(2)}) copy-start(bf16[2048,2,256]{2,1,0:T(2,128)(2,1)} %param.20) | copy-start | bytes 6291460
  49.1 1.9 %copy-start.7 = (bf16[2048]{0:T(1024)(128)(2,1)S(1)}, bf16[2048]{0:T(1024)(128)(2,1)}, u32[]{:S(2)}) copy-start(bf16[2048]{0:T(1024)(128)(2,1)} %param.19) | copy-start | bytes 12292
  50.9 38.8 %copy-start.5 = (bf16[64,256]{1,0:T(8,128)(2,1)S(1)}, bf16[64,256]{1,0:T(8,128)(2,1)}, u32[]{:S(2)}) copy-start(bf16[64,256]{1,0:T(8,128)(2,1)} %get-tuple-element.6) | copy-start | bytes 98308

commit v5 on v4

--- a/solution.py
+++ b/solution.py
@@ -350,15 +350,24 @@
     phase(0, lambda j: x_ref, lambda k: gbuf.at[pl.ds(k * rows, rows)])
     proj = jnp.dot(gbuf[...], w_ref[...], preferred_element_type=jnp.float32)
     trig = trig_ref[...]
-    turned = proj[:, :block] * trig[:, :block] + proj[:, block : 2 * block] * trig[:, block:]
-    qkv_ref[:, :block] = turned.astype(qkv_ref.dtype)
-    qkv_ref[:, block:] = proj[:, 2 * block :].astype(qkv_ref.dtype)
+    pair = proj[:, :block]
+    half = HEAD_SIZE // 2
+    lane = lax.broadcasted_iota(jnp.int32, pair.shape, 1)
+    turned = jnp.where(
+        lane % HEAD_SIZE < half,
+        -pltpu.roll(pair, block - half, 1),
+        pltpu.roll(pair, half, 1),
+    )
+    rotated = pair * trig[:, :block] + turned * trig[:, block:]
+    qkv_ref[:, :block] = rotated.astype(qkv_ref.dtype)
+    qkv_ref[:, block : block + block // 2] = proj[:, block:].astype(qkv_ref.dtype)
+    qkv_ref[:, block + block // 2 :] = jnp.zeros((pair.shape[0], block // 2), qkv_ref.dtype)
     phase(1, lambda j: qkv_ref.at[pl.ds(j * rows, rows)], lambda k: recv_ref.at[k])
 
 
 def head(normed, w_ext, trig, n, cid):
     rows, width = normed.shape
-    cols = w_ext.shape[1] // 3 * 2
+    cols = w_ext.shape[1] // 3 * 4
     vmem = pl.BlockSpec(memory_space=pltpu.VMEM)
     return pl.pallas_call(
         functools.partial(_head_kernel, n),
@@ -412,18 +421,7 @@
     angle = new_pos.astype(jnp.float32)[:, None] * inverse[None, :]
     angle = jnp.concatenate([angle] * (4 * heads_here), axis=-1)
     trig = jnp.concatenate([jnp.cos(angle), jnp.sin(angle)], axis=-1)
-    w_heads = w_qkv.reshape(width, 3, heads_here, HEAD_SIZE)
-    w_turned = jnp.concatenate([-w_heads[..., half:], w_heads[..., :half]], axis=-1)
-    w_ext = jnp.concatenate(
-        [
-            w_heads[:, 0:2].reshape(width, 2 * lanes),
-            w_turned[:, 0:2].reshape(width, 2 * lanes),
-            w_heads[:, 2].reshape(width, lanes),
-            jnp.zeros((width, lanes), w_qkv.dtype),
-        ],
-        axis=-1,
-    )
-    qkv_all, mine = head(normed, w_ext, trig, tn, 0)
+    qkv_all, mine = head(normed, qkv_matrix, trig, tn, 0)
     batch = qkv_all.shape[0]
     keys_all = qkv_all[:, lanes : 2 * lanes]
     values_all = qkv_all[:, 2 * lanes : 3 * lanes]

time: 92.1 us -> 92.6 us (level)
    unnamed x21 -> x4, local copies, waits for them, and re-layouts: 5.59 us -> 3.16 us
    concatenate x2 -> x0, other arithmetic: 2.1 us -> none  [the longest x1 1.53 us: per_device(): jnp.concatenate([w_heads[:, 0:2].reshape(width, 2 * lanes), w_turned[:, 0...]
    reshape x2 -> x1, local copies, waits for them, and re-layouts: 1.28 us -> 2.24 us  [per_device(): qkv_matrix = w_qkv.reshape(width, 3 * lanes)]
where the time goes in v5:
time: 92.6 us; the launch traced here: 91.9 us
  Pallas kernels  60.7 us (66%)
  local copies, waits for them, and re-layouts  12.9 us (14%)
  matrix products  10.8 us (12%)
  other arithmetic  6.71 us (7%)
    pallas_call x1, Pallas kernels, tail(): pl.pallas_call(functools.partial(_tail_kernel, n, sn), out_shape=jax.Shap...  38.1 us
    pallas_call x1, Pallas kernels, head(): pl.pallas_call(functools.partial(_head_kernel, n), out_shape=(jax.ShapeDt...  22.5 us
    dot_general x1, matrix products, per_device(): jnp.einsum('bhs,bhds->bhd', weight_win.astype(jnp.bfloat16), vwin, prefer...  5.86 us
    dot_general x1, matrix products, per_device(): jnp.einsum('bhd,bhds->bhs', queries, kwin, preferred_element_type=jnp.flo...  4.58 us
    unnamed x4, local copies, waits for them, and re-layouts  3.16 us
    reshape x1, local copies, waits for them, and re-layouts, per_device(): qkv_matrix = w_qkv.reshape(width, 3 * lanes)  2.24 us

profile of v5, /device:TPU:1, one launch (start us, length us, event | category | flops | bytes accessed | tf_op | source)
XLA Modules:
  0.0 91.9 jit_solution(13215581550321350779)
XLA Ops:
  0.6 0.7 dynamic_slice.6
  1.4 0.7 dynamic_slice.7
  2.1 0.7 convert_element_type.42
  2.8 0.8 fusion.18
  3.6 0.8 compare_and_fusion
  4.4 0.7 convert_element_type.40
  5.1 1.4 %fusion.20.x_ref = bf16[2,2048]{1,0:T(2,128)(2,1)} fusion(bf16[2,2048]{1,0:T(2,128)(2,1)} %states_ref.1, f32[2]{0:T(128)S(1)} %add_rsqrt_fusion, f32[2048]{0:T(1024)S(1)} %convert_element_type.40), kind=kLoop, calls=%fused_computation.32 | loop fusion | flops 16384 | bytes 24584 | tf_op jit(solution)/shard_map/convert_element_type | solution.py:20
  6.5 1.3 %reshape.133.gain_ref = bf16[1,2048]{1,0:T(2,128)(2,1)} reshape(bf16[2048]{0:T(1024)(128)(2,1)} %param.19) | data formatting | bytes 8192 | tf_op jit(solution)/shard_map/reshape | solution.py:291
  7.8 0.2 fusion.17
  8.1 0.6 pad_maximum_fusion.trig_ref
  8.7 0.9 reshape.130
  9.6 0.9 reshape.132
  10.4 2.2 %copy.43.w_ref = bf16[2048,192]{1,0:T(8,128)(2,1)} copy(bf16[2048,192]{0,1:T(8,128)(2,1)} %bitcast.76) | data formatting | bytes 1572864 | tf_op jit(solution)/shard_map/reshape | solution.py:416
  12.7 22.5 %shard_map.166 = (bf16[64,256]{1,0:T(8,128)(2,1)}, bf16[32,2,256]{2,1,0:T(2,128)(2,1)}) custom-call(bf16[2,2048]{1,0:T(2,128)(2,1)} %fusion.20.x_ref, bf16[2048,192]{1,0:T(8,128)(2,1)} %copy.43.w_ref, f32[64,256]{1,0:T(8,128)} %pad_maximum_fusion.trig_ref), custom_call_target="tpu_custom_call" | custom-call | tf_op jit(solution)/shard_map/pallas_call | solution.py:372
  35.2 0.9 reshape.144
  36.7 1.4 %fusion.25 = (bf16[64,64]{1,0:T(8,128)(2,1)}, bf16[64,64]{1,0:T(8,128)(2,1)}) fusion(bf16[64,256]{1,0:T(8,128)(2,1)} %get-tuple-element.6), kind=kLoop, calls=%fused_computation.53 | loop fusion | bytes 32768 | tf_op jit(solution)/shard_map/slice | solution.py:427
  38.1 4.6 %fusion.14 = f32[2,32,1,1024]{3,2,1,0:T(1,128)S(1)} fusion(bf16[2,32,64,1024]{3,2,1,0:T(8,128)(2,1)} %bitcast.73, bf16[2,32,64,1]{2,0,1,3:T(2,128)(2,1)S(1)} %slice_bitcast_fusion.2), kind=kOutput, calls=%fused_computation.24 | convolution fusion | flops 8388608 | bytes 8658944 | tf_op jit(solution)/shard_map/bhd,bhds->bhs/dot_general | solution.py:448
  42.9 0.2 fusion.6
  43.1 5.9 %fusion.1 = f32[2,32,1,64]{3,2,1,0:T(1,128)S(1)} fusion(bf16[2,32,64,1024]{3,2,1,0:T(8,128)(2,1)} %bitcast.80, bf16[2,32,1024,1]{2,1,0,3:T(8,128)(2,1)S(1)} %get-tuple-element.11), kind=kOutput, calls=%fused_computation.2 | convolution fusion | flops 8388608 | bytes 8536064 | tf_op jit(solution)/shard_map/bhs,bhds->bhd/dot_general | solution.py:465
  49.2 0.2 fusion.7
  49.9 0.7 maximum_bitcast_fusion.part_ref
  50.6 1.9 %copy.63 = bf16[256,8,2,256]{3,1,2,0:T(8,128)(2,1)} copy(bf16[256,8,2,256]{3,2,1,0:T(2,128)(2,1)S(1)} %bitcast.75) | data formatting | bytes 4194304
  52.5 38.1 %shard_map.167 = bf16[2,2048]{1,0:T(2,128)(2,1)} custom-call(f32[32,2,66]{2,1,0:T(2,128)} %maximum_bitcast_fusion.part_ref, bf16[64,2048]{1,0:T(8,128)(2,1)} %w_out_ref.1, bf16[2,2048]{1,0:T(2,128)(2,1)} %states_ref.1, bf16[1,2048]{1,0:T(2,128)(2,1)} %reshape.133.gain_ref, bf16[2048,512]{1,0:T(8,128)(2,1)} %bitcast.74, bf16[256,2048]{1,0:T(8,128)(2,1)} %down_ref.1), custom_call_target="tpu_custom_call" | custom-call | tf_op jit(solution)/shard_map/pallas_call | solution.py:268
  90.6 1.3 %copy.88 = bf16[2,2048]{1,0:T(2,128)(2,1)} copy(bf16[2,2048]{1,0:T(2,128)(2,1)} %shard_map.167) | data formatting | bytes 16384
  (24 shorter events, 1.5 us)
Async XLA Ops:
  42.7 7.9 %copy-start = (bf16[2048,2,256]{2,1,0:T(2,128)(2,1)S(1)}, bf16[2048,2,256]{2,1,0:T(2,128)(2,1)}, u32[]{:S(2)}) copy-start(bf16[2048,2,256]{2,1,0:T(2,128)(2,1)} %param.20) | copy-start | bytes 6291460

commit v6 on v5

--- a/solution.py
+++ b/solution.py
@@ -249,7 +249,7 @@
     summed = jnp.sum(rbuf[...].astype(jnp.float32), axis=0)
     resid = (states_ref[...].astype(jnp.float32) + summed).astype(jnp.bfloat16)
     sbuf[...] = resid
-    nbuf[...] = rms_norm(resid.astype(jnp.float32), gain_ref[...])
+    nbuf[...] = rms_norm(resid.astype(jnp.float32), gain_ref[1:2, :])
     phase(2, lambda j: nbuf, row_block(gbuf))
     gate_up = jnp.dot(gbuf[...], gate_ref[...], preferred_element_type=jnp.float32)
     hidden = (jax.nn.silu(gate_up[:, :units]) * gate_up[:, units:]).astype(jnp.bfloat16)
@@ -288,14 +288,17 @@
             pltpu.SemaphoreType.DMA(()),
         ],
         compiler_params=pltpu.CompilerParams(collective_id=cid, has_side_effects=True),
-    )(part, w_out, states, gain.reshape(1, width), w_gate_up.reshape(width, 2 * units), w_down)
-
-
-def _head_kernel(n, x_ref, w_ref, trig_ref, qkv_ref, recv_ref, gbuf, send_sem, recv_sem, local_sem):
+    )(part, w_out, states, gain, w_gate_up.reshape(width, 2 * units), w_down)
+
+
+def _head_kernel(
+    n, states_ref, gains_ref, w_ref, trig_ref, qkv_ref, recv_ref, x_ref, gbuf, send_sem, recv_sem, local_sem
+):
     axis = "tensor"
     me = lax.axis_index(axis)
     rows = x_ref.shape[0]
     block = qkv_ref.shape[1] // 2
+    x_ref[...] = rms_norm(states_ref[...].astype(jnp.float32), gains_ref[0:1, :])
     barrier = pltpu.get_barrier_semaphore()
 
     def greet(d, carry):
@@ -365,8 +368,8 @@
     phase(1, lambda j: qkv_ref.at[pl.ds(j * rows, rows)], lambda k: recv_ref.at[k])
 
 
-def head(normed, w_ext, trig, n, cid):
-    rows, width = normed.shape
+def head(states, gains, w_ext, trig, n, cid):
+    rows, width = states.shape
     cols = w_ext.shape[1] // 3 * 4
     vmem = pl.BlockSpec(memory_space=pltpu.VMEM)
     return pl.pallas_call(
@@ -375,16 +378,17 @@
             jax.ShapeDtypeStruct((n * rows, cols), jnp.bfloat16),
             jax.ShapeDtypeStruct((n, rows, cols), jnp.bfloat16),
         ),
-        in_specs=[vmem] * 3,
+        in_specs=[vmem] * 4,
         out_specs=(vmem, vmem),
         scratch_shapes=[
+            pltpu.VMEM((rows, width), jnp.bfloat16),
             pltpu.VMEM((n * rows, width), jnp.bfloat16),
             pltpu.SemaphoreType.DMA((2, n)),
             pltpu.SemaphoreType.DMA((2, n)),
             pltpu.SemaphoreType.DMA(()),
         ],
         compiler_params=pltpu.CompilerParams(collective_id=cid, has_side_effects=True),
-    )(normed, w_ext, trig)
+    )(states, gains, w_ext, trig)
 
 
 def per_device(
@@ -410,7 +414,6 @@
     width = states.shape[1]
     row_start = lax.axis_index("tensor") * rows
     floats = states.astype(jnp.float32)
-    normed = rms_norm(floats, attn_gain)
     lanes = w_qkv.shape[2]
     heads_here = lanes // HEAD_SIZE
     qkv_matrix = w_qkv.reshape(width, 3 * lanes)
@@ -421,7 +424,8 @@
     angle = new_pos.astype(jnp.float32)[:, None] * inverse[None, :]
     angle = jnp.concatenate([angle] * (4 * heads_here), axis=-1)
     trig = jnp.concatenate([jnp.cos(angle), jnp.sin(angle)], axis=-1)
-    qkv_all, mine = head(normed, qkv_matrix, trig, tn, 0)
+    gains = jnp.stack([attn_gain, mlp_gain])
+    qkv_all, mine = head(states, gains, qkv_matrix, trig, tn, 0)
     batch = qkv_all.shape[0]
     keys_all = qkv_all[:, lanes : 2 * lanes]
     values_all = qkv_all[:, 2 * lanes : 3 * lanes]
@@ -471,7 +475,7 @@
     mixture = mixture + undo_round(weight_new)[..., None] * values_new.astype(jnp.float32)
     packed = jnp.concatenate([mixture, total[..., None], local_top[..., None]], axis=-1)
     packed = jnp.transpose(packed, (1, 0, 2))
-    out_states = tail(packed, w_out, states, mlp_gain, w_gate_up, w_down, tn, sn, 3)
+    out_states = tail(packed, w_out, states, gains, w_gate_up, w_down, tn, sn, 3)
     return (out_states, keys_all, values_all)
 
 

time: 92.6 us -> 90.8 us (0.981)
  other arithmetic: 6.71 us -> 4.44 us
    convert_element_type x2 -> x0, other arithmetic: 2.06 us -> none  [the longest x1 1.37 us: rms_norm(): (values * lax.rsqrt(meansq + 1e-05) * gain.astype(jnp.float32)).astype(jn...]
    another operation x0 -> x2, local copies, waits for them, and re-layouts: none -> 1.39 us  [per_device(): gains = jnp.stack([attn_gain, mlp_gain])]
    reshape x1 -> x0, local copies, waits for them, and re-layouts: 1.28 us -> none  [tail(): gain.reshape(1, width)]
where the time goes in v6:
time: 90.8 us; the launch traced here: 90.1 us
  Pallas kernels  61.1 us (67%)
  local copies, waits for them, and re-layouts  13 us (14%)
  matrix products  10.8 us (12%)
  other arithmetic  4.44 us (5%)
    pallas_call x1, Pallas kernels, tail(): pl.pallas_call(functools.partial(_tail_kernel, n, sn), out_shape=jax.Shap...  38.2 us
    pallas_call x1, Pallas kernels, head(): pl.pallas_call(functools.partial(_head_kernel, n), out_shape=(jax.ShapeDt...  22.9 us
    dot_general x1, matrix products, per_device(): jnp.einsum('bhs,bhds->bhd', weight_win.astype(jnp.bfloat16), vwin, prefer...  5.86 us
    dot_general x1, matrix products, per_device(): jnp.einsum('bhd,bhds->bhs', queries, kwin, preferred_element_type=jnp.flo...  4.58 us
    unnamed x4, local copies, waits for them, and re-layouts  3.16 us
    reshape x1, local copies, waits for them, and re-layouts, per_device(): qkv_matrix = w_qkv.reshape(width, 3 * lanes)  2.24 us

profile of v6, /device:TPU:1, one launch (start us, length us, event | category | flops | bytes accessed | tf_op | source)
XLA Modules:
  0.0 90.1 jit_solution(14425701662596376080)
XLA Ops:
  0.6 0.7 dynamic_slice.6
  1.4 0.7 dynamic_slice.7
  2.1 0.7 convert_element_type.30
  2.8 0.8 compare_and_fusion
  3.6 0.7 stack.9
  4.3 0.7 stack.10
  5.0 0.6 pad_maximum_fusion.2.gains_ref.gain_ref
  5.7 0.2 fusion.17
  5.9 0.6 pad_maximum_fusion.trig_ref
  6.5 0.9 reshape.118
  7.4 0.9 reshape.120
  8.3 2.2 %copy.43.w_ref = bf16[2048,192]{1,0:T(8,128)(2,1)} copy(bf16[2048,192]{0,1:T(8,128)(2,1)} %bitcast.76) | data formatting | bytes 1572864 | tf_op jit(solution)/shard_map/reshape | solution.py:419
  10.5 22.9 %shard_map.166 = (bf16[64,256]{1,0:T(8,128)(2,1)}, bf16[32,2,256]{2,1,0:T(2,128)(2,1)}) custom-call(bf16[2,2048]{1,0:T(2,128)(2,1)} %states_ref.3, bf16[2,2048]{1,0:T(2,128)(2,1)} %pad_maximum_fusion.2.gains_ref.gain_ref, bf16[2048,192]{1,0:T(8,128)(2,1)} %copy.43.w_ref, f32[64,256]{1,0:T(8,128)} %pad_maximum_fusion.trig_ref), custom_call_target="tpu_custom_call" | custom-call | tf_op jit(solution)/shard_map/pallas_call | solution.py:375
  33.4 0.9 reshape.131
  34.4 0.2 fusion.9
  34.9 1.4 %fusion.22 = (bf16[64,64]{1,0:T(8,128)(2,1)}, bf16[64,64]{1,0:T(8,128)(2,1)}) fusion(bf16[64,256]{1,0:T(8,128)(2,1)} %get-tuple-element.6), kind=kLoop, calls=%fused_computation.48 | loop fusion | bytes 32768 | tf_op jit(solution)/shard_map/slice | solution.py:431
  36.3 4.6 %fusion.14 = f32[2,32,1,1024]{3,2,1,0:T(1,128)S(1)} fusion(bf16[2,32,64,1024]{3,2,1,0:T(8,128)(2,1)} %bitcast.73, bf16[2,32,64,1]{2,0,1,3:T(2,128)(2,1)S(1)} %slice_bitcast_fusion.2), kind=kOutput, calls=%fused_computation.24 | convolution fusion | flops 8388608 | bytes 8658944 | tf_op jit(solution)/shard_map/bhd,bhds->bhs/dot_general | solution.py:452
  41.1 0.2 fusion.6
  41.3 5.9 %fusion.1 = f32[2,32,1,64]{3,2,1,0:T(1,128)S(1)} fusion(bf16[2,32,64,1024]{3,2,1,0:T(8,128)(2,1)} %bitcast.80, bf16[2,32,1024,1]{2,1,0,3:T(8,128)(2,1)S(1)} %get-tuple-element.11), kind=kOutput, calls=%fused_computation.2 | convolution fusion | flops 8388608 | bytes 8536064 | tf_op jit(solution)/shard_map/bhs,bhds->bhd/dot_general | solution.py:469
  47.4 0.2 fusion.7
  48.1 0.7 maximum_bitcast_fusion.part_ref
  48.8 1.9 %copy.63 = bf16[256,8,2,256]{3,1,2,0:T(8,128)(2,1)} copy(bf16[256,8,2,256]{3,2,1,0:T(2,128)(2,1)S(1)} %bitcast.75) | data formatting | bytes 4194304
  50.7 38.2 %shard_map.167 = bf16[2,2048]{1,0:T(2,128)(2,1)} custom-call(f32[32,2,66]{2,1,0:T(2,128)} %maximum_bitcast_fusion.part_ref, bf16[64,2048]{1,0:T(8,128)(2,1)} %w_out_ref.1, bf16[2,2048]{1,0:T(2,128)(2,1)} %states_ref.3, bf16[2,2048]{1,0:T(2,128)(2,1)} %pad_maximum_fusion.2.gains_ref.gain_ref, bf16[2048,512]{1,0:T(8,128)(2,1)} %bitcast.74, ...), custom_call_target="tpu_custom_call" | custom-call | tf_op jit(solution)/shard_map/pallas_call | solution.py:268
  88.8 1.3 %copy.88 = bf16[2,2048]{1,0:T(2,128)(2,1)} copy(bf16[2,2048]{1,0:T(2,128)(2,1)} %shard_map.167) | data formatting | bytes 16384
  (22 shorter events, 1.3 us)
Async XLA Ops:
  40.9 7.9 %copy-start = (bf16[2048,2,256]{2,1,0:T(2,128)(2,1)S(1)}, bf16[2048,2,256]{2,1,0:T(2,128)(2,1)}, u32[]{:S(2)}) copy-start(bf16[2048,2,256]{2,1,0:T(2,128)(2,1)} %param.20) | copy-start | bytes 6291460

commit v7 on v6

--- a/solution.py
+++ b/solution.py
@@ -453,7 +453,9 @@
     )
     score_win = jnp.where(live, score_win, NEG)
     score_sink = (
-        jnp.einsum("bhd,bhds->bhs", queries, sink_key_rows, preferred_element_type=jnp.float32)
+        jnp.sum(
+            queries.astype(jnp.float32)[..., None] * sink_key_rows.astype(jnp.float32), axis=2
+        )
         * 0.125
     )
     score_sink = jnp.where(first_shard, score_sink, NEG)
@@ -469,8 +471,8 @@
     mixture = jnp.einsum(
         "bhs,bhds->bhd", weight_win.astype(jnp.bfloat16), vwin, preferred_element_type=jnp.float32
     )
-    mixture = mixture + jnp.einsum(
-        "bhs,bhds->bhd", weight_sink.astype(jnp.bfloat16), vsink, preferred_element_type=jnp.float32
+    mixture = mixture + jnp.sum(
+        undo_round(weight_sink)[:, :, None, :] * vsink.astype(jnp.float32), axis=-1
     )
     mixture = mixture + undo_round(weight_new)[..., None] * values_new.astype(jnp.float32)
     packed = jnp.concatenate([mixture, total[..., None], local_top[..., None]], axis=-1)

time: 90.8 us -> 86.8 us (0.956)
  matrix products: 10.8 us -> 7 us
    dot_general x1, matrix products: 5.86 us -> 2.26 us  [per_device(): jnp.einsum('bhs,bhds->bhd', weight_win.astype(jnp.bfloat16), vwin, prefer...]
    reshape x2 -> x0, local copies, waits for them, and re-layouts: 1.75 us -> none  [the longest x1 0.88 us: per_device(): sink_values.reshape(rows, all_heads, HEAD_SIZE, sink_values.shape[2])]
    unnamed x4 -> x10, local copies, waits for them, and re-layouts: 3.16 us -> 3.74 us
where the time goes in v7:
time: 86.8 us; the launch traced here: 86.3 us
  Pallas kernels  61.1 us (70%)
  local copies, waits for them, and re-layouts  12.8 us (15%)
  matrix products  7 us (8%)
  other arithmetic  4.61 us (5%)
    pallas_call x1, Pallas kernels, tail(): pl.pallas_call(functools.partial(_tail_kernel, n, sn), out_shape=jax.Shap...  38.2 us
    pallas_call x1, Pallas kernels, head(): pl.pallas_call(functools.partial(_head_kernel, n), out_shape=(jax.ShapeDt...  22.9 us
    dot_general x1, matrix products, per_device(): jnp.einsum('bhd,bhds->bhs', queries, kwin, preferred_element_type=jnp.flo...  4.73 us
    unnamed x10, local copies, waits for them, and re-layouts  3.74 us
    dot_general x1, matrix products, per_device(): jnp.einsum('bhs,bhds->bhd', weight_win.astype(jnp.bfloat16), vwin, prefer...  2.26 us
    reshape x1, local copies, waits for them, and re-layouts, per_device(): qkv_matrix = w_qkv.reshape(width, 3 * lanes)  2.23 us

profile of v7, /device:TPU:1, one launch (start us, length us, event | category | flops | bytes accessed | tf_op | source)
XLA Modules:
  0.0 86.3 jit_solution(744485132346290950)
XLA Ops:
  0.6 0.7 dynamic_slice.6
  1.4 0.7 dynamic_slice.7
  2.1 0.7 convert_element_type.48
  2.8 0.8 compare_and_fusion
  3.6 0.7 stack.9
  4.3 0.7 stack.10
  5.0 0.6 pad_maximum_fusion.2.gains_ref.gain_ref
  5.7 0.2 fusion.12
  5.9 0.6 pad_maximum_fusion.trig_ref
  6.5 0.9 %reshape.126 = f32[2,32,64,4]{2,1,3,0:T(8,128)S(1)} reshape(bf16[2,2048,4]{1,2,0:T(4,128)(2,1)} %param.24) | data formatting | bytes 98304 | tf_op jit(solution)/shard_map/convert_element_type | solution.py:457
  7.4 2.2 %copy.59.w_ref = bf16[2048,192]{1,0:T(8,128)(2,1)} copy(bf16[2048,192]{0,1:T(8,128)(2,1)} %bitcast.63) | data formatting | bytes 1572864 | tf_op jit(solution)/shard_map/reshape | solution.py:419
  9.6 22.9 %shard_map.166 = (bf16[64,256]{1,0:T(8,128)(2,1)}, bf16[32,2,256]{2,1,0:T(2,128)(2,1)}) custom-call(bf16[2,2048]{1,0:T(2,128)(2,1)} %states_ref.3, bf16[2,2048]{1,0:T(2,128)(2,1)} %pad_maximum_fusion.2.gains_ref.gain_ref, bf16[2048,192]{1,0:T(8,128)(2,1)} %copy.59.w_ref, f32[64,256]{1,0:T(8,128)} %pad_maximum_fusion.trig_ref), custom_call_target="tpu_custom_call" | custom-call | tf_op jit(solution)/shard_map/pallas_call | solution.py:375
  32.5 0.9 %reshape.133 = bf16[32,2,4,1,64]{4,2,1,0,3:T(4,128)(2,1)S(1)} reshape(bf16[32,2,256]{2,1,0:T(2,128)(2,1)} %get-tuple-element.5) | data formatting | bytes 65536 | tf_op jit(solution)/shard_map/reshape | solution.py:432
  33.7 1.4 %fusion.17 = (bf16[64,64]{1,0:T(8,128)(2,1)}, bf16[64,64]{1,0:T(8,128)(2,1)}) fusion(bf16[64,256]{1,0:T(8,128)(2,1)} %get-tuple-element.6), kind=kLoop, calls=%fused_computation.45 | loop fusion | bytes 32768 | tf_op jit(solution)/shard_map/slice | solution.py:431
  35.1 0.1 multiply_reduce_fusion
  35.3 4.7 %fusion.9 = f32[2,32,1,1024]{3,2,1,0:T(1,128)S(1)} fusion(bf16[2,32,64,1024]{3,2,1,0:T(8,128)(2,1)} %bitcast.60, bf16[2,32,64,1]{2,0,1,3:T(2,128)(2,1)S(1)} %get-tuple-element.14), kind=kOutput, calls=%fused_computation.20 | convolution fusion | flops 8388608 | bytes 8658944 | tf_op jit(solution)/shard_map/bhd,bhds->bhs/dot_general | solution.py:452
  40.0 0.1 fusion.5
  40.2 0.2 fusion.6
  40.4 0.6 slice-done.1
  41.0 2.3 %fusion.1 = f32[2,32,1,64]{3,2,1,0:T(1,128)S(1)} fusion(bf16[2,32,64,1024]{3,2,1,0:T(8,128)(2,1)S(1)} %bitcast.69, bf16[2,32,1024,1]{2,1,0,3:T(8,128)(2,1)S(1)} %get-tuple-element.11), kind=kOutput, calls=%fused_computation.2 | convolution fusion | flops 8388608 | bytes 8536064 | tf_op jit(solution)/shard_map/bhs,bhds->bhd/dot_general | solution.py:471
  44.2 0.7 maximum_bitcast_fusion.part_ref
  45.0 1.9 %copy.76 = bf16[256,8,2,256]{3,1,2,0:T(8,128)(2,1)} copy(bf16[256,8,2,256]{3,2,1,0:T(2,128)(2,1)S(1)} %bitcast.62) | data formatting | bytes 4194304
  46.8 38.2 %shard_map.167 = bf16[2,2048]{1,0:T(2,128)(2,1)} custom-call(f32[32,2,66]{2,1,0:T(2,128)} %maximum_bitcast_fusion.part_ref, bf16[64,2048]{1,0:T(8,128)(2,1)} %w_out_ref.1, bf16[2,2048]{1,0:T(2,128)(2,1)} %states_ref.3, bf16[2,2048]{1,0:T(2,128)(2,1)} %pad_maximum_fusion.2.gains_ref.gain_ref, bf16[2048,512]{1,0:T(8,128)(2,1)} %bitcast.61, ...), custom_call_target="tpu_custom_call" | custom-call | tf_op jit(solution)/shard_map/pallas_call | solution.py:268
  85.0 1.3 %copy.95 = bf16[2,2048]{1,0:T(2,128)(2,1)} copy(bf16[2,2048]{1,0:T(2,128)(2,1)} %shard_map.167) | data formatting | bytes 16384
  (30 shorter events, 1.3 us)
Async XLA Ops:
  35.1 5.3 %slice-start = ((s8[8388608]{0:T(1024)(128)(4,1)}), s8[4194304]{0:T(1024)(128)(4,1)S(1)}, s32[]{:S(2)}) async-start(s8[8388608]{0:T(1024)(128)(4,1)} %bitcast.67), calls=%async_computation | async-start | bytes 8388608
  35.3 5.7 %slice-start.1 = ((s8[8388608]{0:T(1024)(128)(4,1)}), s8[4194304]{0:T(1024)(128)(4,1)S(1)}, s32[]{:S(2)}) async-start(s8[8388608]{0:T(1024)(128)(4,1)} %bitcast.67), calls=%async_computation.1 | async-start | bytes 8388608
  40.0 3.9 %copy-start.1 = (bf16[2,2048,4]{1,2,0:T(4,128)(2,1)S(1)}, bf16[2,2048,4]{1,2,0:T(4,128)(2,1)}, u32[]{:S(2)}) copy-start(bf16[2,2048,4]{1,2,0:T(4,128)(2,1)} %param.25) | copy-start | bytes 98308
  40.0 4.9 %copy-start = (bf16[2048,2,256]{2,1,0:T(2,128)(2,1)S(1)}, bf16[2048,2,256]{2,1,0:T(2,128)(2,1)}, u32[]{:S(2)}) copy-start(bf16[2048,2,256]{2,1,0:T(2,128)(2,1)} %param.20) | copy-start | bytes 6291460

commit v8 on v7

--- a/solution.py
+++ b/solution.py
@@ -449,7 +449,8 @@
     sink_key_rows = sink_keys.reshape(rows, all_heads, HEAD_SIZE, sink_keys.shape[2])
     vsink = sink_values.reshape(rows, all_heads, HEAD_SIZE, sink_values.shape[2])
     score_win = (
-        jnp.einsum("bhd,bhds->bhs", queries, kwin, preferred_element_type=jnp.float32) * 0.125
+        jnp.sum(queries.astype(jnp.float32)[..., None] * kwin.astype(jnp.float32), axis=2)
+        * 0.125
     )
     score_win = jnp.where(live, score_win, NEG)
     score_sink = (

time: 86.8 us -> 89.1 us (1.026)
  other arithmetic: 4.61 us -> 12.1 us
  matrix products: 7 us -> 2.27 us
    reduce_sum x0 -> x1, other arithmetic: none -> 7.57 us  [per_device(): jnp.sum(queries.astype(jnp.float32)[..., None] * kwin.astype(jnp.float32)...]
    dot_general x1 -> x0, matrix products: 4.73 us -> none  [per_device(): jnp.einsum('bhd,bhds->bhs', queries, kwin, preferred_element_type=jnp.flo...]
    unnamed x10 -> x8, local copies, waits for them, and re-layouts: 3.74 us -> 3.17 us
where the time goes in v8:
time: 89.1 us; the launch traced here: 88.6 us
  Pallas kernels  61.1 us (69%)
  local copies, waits for them, and re-layouts  12.4 us (14%)
  other arithmetic  12.1 us (14%)
  matrix products  2.27 us (3%)
    pallas_call x1, Pallas kernels, tail(): pl.pallas_call(functools.partial(_tail_kernel, n, sn), out_shape=jax.Shap...  38.2 us
    pallas_call x1, Pallas kernels, head(): pl.pallas_call(functools.partial(_head_kernel, n), out_shape=(jax.ShapeDt...  22.9 us
    reduce_sum x1, other arithmetic, per_device(): jnp.sum(queries.astype(jnp.float32)[..., None] * kwin.astype(jnp.float32)...  7.57 us
    unnamed x8, local copies, waits for them, and re-layouts  3.17 us
    dot_general x1, matrix products, per_device(): jnp.einsum('bhs,bhds->bhd', weight_win.astype(jnp.bfloat16), vwin, prefer...  2.27 us
    reshape x1, local copies, waits for them, and re-layouts, per_device(): qkv_matrix = w_qkv.reshape(width, 3 * lanes)  2.23 us

profile of v8, /device:TPU:1, one launch (start us, length us, event | category | flops | bytes accessed | tf_op | source)
XLA Modules:
  0.0 88.6 jit_solution(14487810515337732434)
XLA Ops:
  0.6 0.7 dynamic_slice.6
  1.4 0.7 dynamic_slice.7
  2.1 0.7 convert_element_type.58
  2.8 0.8 compare_and_fusion
  3.6 0.7 stack.9
  4.3 0.7 stack.10
  5.0 0.6 pad_maximum_fusion.2.gains_ref.gain_ref
  5.7 0.2 fusion.10
  5.9 0.6 pad_maximum_fusion.trig_ref
  6.5 0.9 reshape.129
  7.4 2.2 %copy.63.w_ref = bf16[2048,192]{1,0:T(8,128)(2,1)} copy(bf16[2048,192]{0,1:T(8,128)(2,1)} %bitcast.52) | data formatting | bytes 1572864 | tf_op jit(solution)/shard_map/reshape | solution.py:419
  9.6 22.9 %shard_map.166 = (bf16[64,256]{1,0:T(8,128)(2,1)}, bf16[32,2,256]{2,1,0:T(2,128)(2,1)}) custom-call(bf16[2,2048]{1,0:T(2,128)(2,1)} %states_ref.3, bf16[2,2048]{1,0:T(2,128)(2,1)} %pad_maximum_fusion.2.gains_ref.gain_ref, bf16[2048,192]{1,0:T(8,128)(2,1)} %copy.63.w_ref, f32[64,256]{1,0:T(8,128)} %pad_maximum_fusion.trig_ref), custom_call_target="tpu_custom_call" | custom-call | tf_op jit(solution)/shard_map/pallas_call | solution.py:375
  32.5 0.9 reshape.134
  33.5 0.1 fusion.8
  33.7 0.1 multiply_reduce_fusion
  33.8 1.6 %fusion.16 = (bf16[64,64]{1,0:T(8,128)(2,1)}, bf16[64,64]{1,0:T(8,128)(2,1)}) fusion(bf16[64,256]{1,0:T(8,128)(2,1)} %get-tuple-element.6), kind=kLoop, calls=%fused_computation.44 | loop fusion | bytes 32768 | tf_op jit(solution)/shard_map/slice | solution.py:431
  35.4 7.6 %fusion = f32[2,32,1024]{2,1,0:T(8,128)S(1)} fusion(f32[2,32,64]{2,1,0:T(8,128)S(1)} %copy.66, bf16[2,2048,1024]{2,1,0:T(8,128)(2,1)} %param.22), kind=kLoop, calls=%fused_computation.1 | loop fusion | flops 12517376 | bytes 8667136 | tf_op jit(solution)/shard_map/reduce_sum | solution.py:452
  43.0 0.1 fusion.3
  43.1 0.2 fusion.6
  43.4 2.3 %fusion.1 = f32[2,32,1,64]{3,2,1,0:T(1,128)S(1)} fusion(bf16[2,32,64,1024]{3,2,1,0:T(8,128)(2,1)S(1)} %bitcast.56, bf16[2,32,1024,1]{2,1,0,3:T(8,128)(2,1)S(1)} %get-tuple-element.11), kind=kOutput, calls=%fused_computation.2 | convolution fusion | flops 8388608 | bytes 8536064 | tf_op jit(solution)/shard_map/bhs,bhds->bhd/dot_general | solution.py:472
  46.6 0.7 maximum_bitcast_fusion.part_ref
  47.3 1.9 %copy.79 = bf16[256,8,2,256]{3,1,2,0:T(8,128)(2,1)} copy(bf16[256,8,2,256]{3,2,1,0:T(2,128)(2,1)S(1)} %bitcast.51) | data formatting | bytes 4194304
  49.2 38.2 %shard_map.167 = bf16[2,2048]{1,0:T(2,128)(2,1)} custom-call(f32[32,2,66]{2,1,0:T(2,128)} %maximum_bitcast_fusion.part_ref, bf16[64,2048]{1,0:T(8,128)(2,1)} %w_out_ref.1, bf16[2,2048]{1,0:T(2,128)(2,1)} %states_ref.3, bf16[2,2048]{1,0:T(2,128)(2,1)} %pad_maximum_fusion.2.gains_ref.gain_ref, bf16[2048,512]{1,0:T(8,128)(2,1)} %bitcast.50, ...), custom_call_target="tpu_custom_call" | custom-call | tf_op jit(solution)/shard_map/pallas_call | solution.py:268
  87.3 1.3 %copy.87 = bf16[2,2048]{1,0:T(2,128)(2,1)} copy(bf16[2,2048]{1,0:T(2,128)(2,1)} %shard_map.167) | data formatting | bytes 16384
  (27 shorter events, 1.2 us)
Async XLA Ops:
  33.7 9.7 %copy-start.2 = (bf16[2,2048,1024]{2,1,0:T(8,128)(2,1)S(1)}, bf16[2,2048,1024]{2,1,0:T(8,128)(2,1)}, u32[]{:S(2)}) copy-start(bf16[2,2048,1024]{2,1,0:T(8,128)(2,1)} %param.23) | copy-start | bytes 25165828
  35.4 10.9 %copy-start.1 = (bf16[2,2048,4]{1,2,0:T(4,128)(2,1)S(1)}, bf16[2,2048,4]{1,2,0:T(4,128)(2,1)}, u32[]{:S(2)}) copy-start(bf16[2,2048,4]{1,2,0:T(4,128)(2,1)} %param.25) | copy-start | bytes 98308
  35.4 11.9 %copy-start = (bf16[2048,2,256]{2,1,0:T(2,128)(2,1)S(1)}, bf16[2048,2,256]{2,1,0:T(2,128)(2,1)}, u32[]{:S(2)}) copy-start(bf16[2048,2,256]{2,1,0:T(2,128)(2,1)} %param.20) | copy-start | bytes 6291460

commit v9 on v7

--- a/solution.py
+++ b/solution.py
@@ -249,7 +249,7 @@
     summed = jnp.sum(rbuf[...].astype(jnp.float32), axis=0)
     resid = (states_ref[...].astype(jnp.float32) + summed).astype(jnp.bfloat16)
     sbuf[...] = resid
-    nbuf[...] = rms_norm(resid.astype(jnp.float32), gain_ref[1:2, :])
+    nbuf[...] = rms_norm(resid.astype(jnp.float32), gain_ref[...].reshape(1, -1))
     phase(2, lambda j: nbuf, row_block(gbuf))
     gate_up = jnp.dot(gbuf[...], gate_ref[...], preferred_element_type=jnp.float32)
     hidden = (jax.nn.silu(gate_up[:, :units]) * gate_up[:, units:]).astype(jnp.bfloat16)
@@ -298,7 +298,7 @@
     me = lax.axis_index(axis)
     rows = x_ref.shape[0]
     block = qkv_ref.shape[1] // 2
-    x_ref[...] = rms_norm(states_ref[...].astype(jnp.float32), gains_ref[0:1, :])
+    x_ref[...] = rms_norm(states_ref[...].astype(jnp.float32), gains_ref[...].reshape(1, -1))
     barrier = pltpu.get_barrier_semaphore()
 
     def greet(d, carry):
@@ -424,8 +424,7 @@
     angle = new_pos.astype(jnp.float32)[:, None] * inverse[None, :]
     angle = jnp.concatenate([angle] * (4 * heads_here), axis=-1)
     trig = jnp.concatenate([jnp.cos(angle), jnp.sin(angle)], axis=-1)
-    gains = jnp.stack([attn_gain, mlp_gain])
-    qkv_all, mine = head(states, gains, qkv_matrix, trig, tn, 0)
+    qkv_all, mine = head(states, attn_gain, qkv_matrix, trig, tn, 0)
     batch = qkv_all.shape[0]
     keys_all = qkv_all[:, lanes : 2 * lanes]
     values_all = qkv_all[:, 2 * lanes : 3 * lanes]
@@ -477,7 +476,7 @@
     mixture = mixture + undo_round(weight_new)[..., None] * values_new.astype(jnp.float32)
     packed = jnp.concatenate([mixture, total[..., None], local_top[..., None]], axis=-1)
     packed = jnp.transpose(packed, (1, 0, 2))
-    out_states = tail(packed, w_out, states, gains, w_gate_up, w_down, tn, sn, 3)
+    out_states = tail(packed, w_out, states, mlp_gain, w_gate_up, w_down, tn, sn, 3)
     return (out_states, keys_all, values_all)
 
 

time: 86.8 us -> 84.7 us (0.976)
  local copies, waits for them, and re-layouts: 12.8 us -> 11.4 us
    another operation x2 -> x0, local copies, waits for them, and re-layouts: 1.39 us -> none  [per_device(): gains = jnp.stack([attn_gain, mlp_gain])]
where the time goes in v9:
time: 84.7 us; the launch traced here: 84.3 us
  Pallas kernels  61.1 us (72%)
  local copies, waits for them, and re-layouts  11.4 us (13%)
  matrix products  7 us (8%)
  other arithmetic  3.99 us (5%)
    pallas_call x1, Pallas kernels, tail(): pl.pallas_call(functools.partial(_tail_kernel, n, sn), out_shape=jax.Shap...  38.2 us
    pallas_call x1, Pallas kernels, head(): pl.pallas_call(functools.partial(_head_kernel, n), out_shape=(jax.ShapeDt...  22.9 us
    dot_general x1, matrix products, per_device(): jnp.einsum('bhd,bhds->bhs', queries, kwin, preferred_element_type=jnp.flo...  4.73 us
    unnamed x10, local copies, waits for them, and re-layouts  3.74 us
    dot_general x1, matrix products, per_device(): jnp.einsum('bhs,bhds->bhd', weight_win.astype(jnp.bfloat16), vwin, prefer...  2.26 us
    reshape x1, local copies, waits for them, and re-layouts, per_device(): qkv_matrix = w_qkv.reshape(width, 3 * lanes)  2.23 us

profile of v9, /device:TPU:1, one launch (start us, length us, event | category | flops | bytes accessed | tf_op | source)
XLA Modules:
  0.0 84.3 jit_solution(7087516236685007877)
XLA Ops:
  0.6 0.7 dynamic_slice.6
  1.4 0.7 dynamic_slice.7
  2.1 0.7 convert_element_type.48
  2.8 0.8 compare_and_fusion
  3.6 0.2 fusion.12
  3.9 0.6 pad_maximum_fusion.trig_ref
  4.5 0.9 %reshape.126 = f32[2,32,64,4]{2,1,3,0:T(8,128)S(1)} reshape(bf16[2,2048,4]{1,2,0:T(4,128)(2,1)} %param.24) | data formatting | bytes 98304 | tf_op jit(solution)/shard_map/convert_element_type | solution.py:456
  5.4 2.2 %copy.59.w_ref = bf16[2048,192]{1,0:T(8,128)(2,1)} copy(bf16[2048,192]{0,1:T(8,128)(2,1)} %bitcast.63) | data formatting | bytes 1572864 | tf_op jit(solution)/shard_map/reshape | solution.py:419
  7.6 22.9 %shard_map.166 = (bf16[64,256]{1,0:T(8,128)(2,1)}, bf16[32,2,256]{2,1,0:T(2,128)(2,1)}) custom-call(bf16[2,2048]{1,0:T(2,128)(2,1)} %states_ref.3, bf16[2048]{0:T(1024)(128)(2,1)} %gains_ref.1, bf16[2048,192]{1,0:T(8,128)(2,1)} %copy.59.w_ref, f32[64,256]{1,0:T(8,128)} %pad_maximum_fusion.trig_ref), custom_call_target="tpu_custom_call" | custom-call | tf_op jit(solution)/shard_map/pallas_call | solution.py:375
  30.5 0.9 %reshape.133 = bf16[32,2,4,1,64]{4,2,1,0,3:T(4,128)(2,1)S(1)} reshape(bf16[32,2,256]{2,1,0:T(2,128)(2,1)} %get-tuple-element.5) | data formatting | bytes 65536 | tf_op jit(solution)/shard_map/reshape | solution.py:431
  31.5 0.1 fusion.8
  31.6 1.4 %fusion.17 = (bf16[64,64]{1,0:T(8,128)(2,1)}, bf16[64,64]{1,0:T(8,128)(2,1)}) fusion(bf16[64,256]{1,0:T(8,128)(2,1)} %get-tuple-element.6), kind=kLoop, calls=%fused_computation.44 | loop fusion | bytes 32768 | tf_op jit(solution)/shard_map/slice | solution.py:430
  33.1 0.1 multiply_reduce_fusion
  33.3 4.7 %fusion.9 = f32[2,32,1,1024]{3,2,1,0:T(1,128)S(1)} fusion(bf16[2,32,64,1024]{3,2,1,0:T(8,128)(2,1)} %bitcast.60, bf16[2,32,64,1]{2,0,1,3:T(2,128)(2,1)S(1)} %get-tuple-element.14), kind=kOutput, calls=%fused_computation.20 | convolution fusion | flops 8388608 | bytes 8658944 | tf_op jit(solution)/shard_map/bhd,bhds->bhs/dot_general | solution.py:451
  38.0 0.1 fusion.5
  38.2 0.2 fusion.6
  38.4 0.6 slice-done.1
  39.0 2.3 %fusion.1 = f32[2,32,1,64]{3,2,1,0:T(1,128)S(1)} fusion(bf16[2,32,64,1024]{3,2,1,0:T(8,128)(2,1)S(1)} %bitcast.69, bf16[2,32,1024,1]{2,1,0,3:T(8,128)(2,1)S(1)} %get-tuple-element.11), kind=kOutput, calls=%fused_computation.2 | convolution fusion | flops 8388608 | bytes 8536064 | tf_op jit(solution)/shard_map/bhs,bhds->bhd/dot_general | solution.py:470
  41.4 0.1 copy.69
  41.8 0.1 mul.109
  42.2 0.7 maximum_bitcast_fusion.part_ref
  42.9 1.9 %copy.76 = bf16[256,8,2,256]{3,1,2,0:T(8,128)(2,1)} copy(bf16[256,8,2,256]{3,2,1,0:T(2,128)(2,1)S(1)} %bitcast.62) | data formatting | bytes 4194304
  44.8 38.2 %shard_map.167 = bf16[2,2048]{1,0:T(2,128)(2,1)} custom-call(f32[32,2,66]{2,1,0:T(2,128)} %maximum_bitcast_fusion.part_ref, bf16[64,2048]{1,0:T(8,128)(2,1)} %w_out_ref.1, bf16[2,2048]{1,0:T(2,128)(2,1)} %states_ref.3, bf16[2048]{0:T(1024)(128)(2,1)} %gain_ref.1, bf16[2048,512]{1,0:T(8,128)(2,1)} %bitcast.61, bf16[256,2048]{1,0:T(8,128)(2,1)} %down_ref.1), custom_call_target="tpu_custom_call" | custom-call | tf_op jit(solution)/shard_map/pallas_call | solution.py:268
  83.0 1.3 %copy.95 = bf16[2,2048]{1,0:T(2,128)(2,1)} copy(bf16[2,2048]{1,0:T(2,128)(2,1)} %shard_map.167) | data formatting | bytes 16384
  (27 shorter events, 1.0 us)
Async XLA Ops:
  33.1 5.3 %slice-start = ((s8[8388608]{0:T(1024)(128)(4,1)}), s8[4194304]{0:T(1024)(128)(4,1)S(1)}, s32[]{:S(2)}) async-start(s8[8388608]{0:T(1024)(128)(4,1)} %bitcast.67), calls=%async_computation | async-start | bytes 8388608
  33.3 5.7 %slice-start.1 = ((s8[8388608]{0:T(1024)(128)(4,1)}), s8[4194304]{0:T(1024)(128)(4,1)S(1)}, s32[]{:S(2)}) async-start(s8[8388608]{0:T(1024)(128)(4,1)} %bitcast.67), calls=%async_computation.1 | async-start | bytes 8388608
  38.0 3.9 %copy-start.1 = (bf16[2,2048,4]{1,2,0:T(4,128)(2,1)S(1)}, bf16[2,2048,4]{1,2,0:T(4,128)(2,1)}, u32[]{:S(2)}) copy-start(bf16[2,2048,4]{1,2,0:T(4,128)(2,1)} %param.25) | copy-start | bytes 98308
  38.0 4.9 %copy-start = (bf16[2048,2,256]{2,1,0:T(2,128)(2,1)S(1)}, bf16[2048,2,256]{2,1,0:T(2,128)(2,1)}, u32[]{:S(2)}) copy-start(bf16[2048,2,256]{2,1,0:T(2,128)(2,1)} %param.20) | copy-start | bytes 6291460

commit v10 on v9

--- a/solution.py
+++ b/solution.py
@@ -351,9 +351,19 @@
         local.wait()
 
     phase(0, lambda j: x_ref, lambda k: gbuf.at[pl.ds(k * rows, rows)])
-    proj = jnp.dot(gbuf[...], w_ref[...], preferred_element_type=jnp.float32)
+    lanes = w_ref.shape[1]
+    gathered = gbuf[...]
+    contract_last = (((1,), (1,)), ((), ()))
+    pair = lax.dot_general(
+        gathered,
+        w_ref[0:2].reshape(2 * lanes, w_ref.shape[2]),
+        contract_last,
+        preferred_element_type=jnp.float32,
+    )
+    value_proj = lax.dot_general(
+        gathered, w_ref[2], contract_last, preferred_element_type=jnp.float32
+    )
     trig = trig_ref[...]
-    pair = proj[:, :block]
     half = HEAD_SIZE // 2
     lane = lax.broadcasted_iota(jnp.int32, pair.shape, 1)
     turned = jnp.where(
@@ -363,14 +373,14 @@
     )
     rotated = pair * trig[:, :block] + turned * trig[:, block:]
     qkv_ref[:, :block] = rotated.astype(qkv_ref.dtype)
-    qkv_ref[:, block : block + block // 2] = proj[:, block:].astype(qkv_ref.dtype)
+    qkv_ref[:, block : block + block // 2] = value_proj.astype(qkv_ref.dtype)
     qkv_ref[:, block + block // 2 :] = jnp.zeros((pair.shape[0], block // 2), qkv_ref.dtype)
     phase(1, lambda j: qkv_ref.at[pl.ds(j * rows, rows)], lambda k: recv_ref.at[k])
 
 
 def head(states, gains, w_ext, trig, n, cid):
     rows, width = states.shape
-    cols = w_ext.shape[1] // 3 * 4
+    cols = w_ext.shape[1] * 4
     vmem = pl.BlockSpec(memory_space=pltpu.VMEM)
     return pl.pallas_call(
         functools.partial(_head_kernel, n),
@@ -416,7 +426,6 @@
     floats = states.astype(jnp.float32)
     lanes = w_qkv.shape[2]
     heads_here = lanes // HEAD_SIZE
-    qkv_matrix = w_qkv.reshape(width, 3 * lanes)
     half = HEAD_SIZE // 2
     inverse = jnp.exp(
         -jnp.log(jnp.float32(130000.0)) * jnp.arange(half, dtype=jnp.float32) * (2.0 / HEAD_SIZE)
@@ -424,7 +433,7 @@
     angle = new_pos.astype(jnp.float32)[:, None] * inverse[None, :]
     angle = jnp.concatenate([angle] * (4 * heads_here), axis=-1)
     trig = jnp.concatenate([jnp.cos(angle), jnp.sin(angle)], axis=-1)
-    qkv_all, mine = head(states, attn_gain, qkv_matrix, trig, tn, 0)
+    qkv_all, mine = head(states, attn_gain, jnp.transpose(w_qkv, (1, 2, 0)), trig, tn, 0)
     batch = qkv_all.shape[0]
     keys_all = qkv_all[:, lanes : 2 * lanes]
     values_all = qkv_all[:, 2 * lanes : 3 * lanes]

time: 84.7 us -> 85.4 us (level)
  matrix products: 7 us -> 10.5 us
  local copies, waits for them, and re-layouts: 11.4 us -> 8.61 us
    dot_general x1, matrix products: 2.26 us -> 5.87 us  [per_device(): jnp.einsum('bhs,bhds->bhd', weight_win.astype(jnp.bfloat16), vwin, prefer...]
    reshape x1 -> x0, local copies, waits for them, and re-layouts: 2.23 us -> none  [per_device(): qkv_matrix = w_qkv.reshape(width, 3 * lanes)]
    unnamed x10 -> x6, local copies, waits for them, and re-layouts: 3.74 us -> 3.16 us
where the time goes in v10:
time: 85.4 us; the launch traced here: 84.9 us
  Pallas kernels  61.1 us (72%)
  matrix products  10.5 us (12%)
  local copies, waits for them, and re-layouts  8.61 us (10%)
  other arithmetic  3.99 us (5%)
    pallas_call x1, Pallas kernels, tail(): pl.pallas_call(functools.partial(_tail_kernel, n, sn), out_shape=jax.Shap...  38.2 us
    pallas_call x1, Pallas kernels, head(): pl.pallas_call(functools.partial(_head_kernel, n), out_shape=(jax.ShapeDt...  22.9 us
    dot_general x1, matrix products, per_device(): jnp.einsum('bhs,bhds->bhd', weight_win.astype(jnp.bfloat16), vwin, prefer...  5.87 us
    dot_general x1, matrix products, per_device(): jnp.einsum('bhd,bhds->bhs', queries, kwin, preferred_element_type=jnp.flo...  4.58 us
    unnamed x6, local copies, waits for them, and re-layouts  3.16 us

profile of v10, /device:TPU:1, one launch (start us, length us, event | category | flops | bytes accessed | tf_op | source)
XLA Modules:
  0.0 84.9 jit_solution(4985507947510541216)
XLA Ops:
  0.6 0.7 dynamic_slice.6
  1.4 0.7 dynamic_slice.7
  2.1 0.7 convert_element_type.48
  2.8 0.8 compare_and_fusion
  3.6 0.2 fusion.12
  3.9 0.6 pad_maximum_fusion.trig_ref
  4.5 22.9 %shard_map.166 = (bf16[64,256]{1,0:T(8,128)(2,1)}, bf16[32,2,256]{2,1,0:T(2,128)(2,1)}) custom-call(bf16[2,2048]{1,0:T(2,128)(2,1)} %states_ref.3, bf16[2048]{0:T(1024)(128)(2,1)} %gains_ref.1, bf16[3,64,2048]{2,1,0:T(8,128)(2,1)} %bitcast.63, f32[64,256]{1,0:T(8,128)} %pad_maximum_fusion.trig_ref), custom_call_target="tpu_custom_call" | custom-call | tf_op jit(solution)/shard_map/pallas_call | solution.py:385
  27.4 0.9 %reshape.129 = bf16[32,2,4,1,64]{4,2,1,0,3:T(4,128)(2,1)S(1)} reshape(bf16[32,2,256]{2,1,0:T(2,128)(2,1)} %get-tuple-element.5) | data formatting | bytes 65536 | tf_op jit(solution)/shard_map/reshape | solution.py:440
  28.3 0.1 fusion.8
  28.5 1.4 %fusion.17 = (bf16[64,64]{1,0:T(8,128)(2,1)}, bf16[64,64]{1,0:T(8,128)(2,1)}) fusion(bf16[64,256]{1,0:T(8,128)(2,1)} %get-tuple-element.6), kind=kLoop, calls=%fused_computation.44 | loop fusion | bytes 32768 | tf_op jit(solution)/shard_map/slice | solution.py:439
  30.0 0.9 %reshape.122 = f32[2,32,64,4]{2,1,3,0:T(8,128)S(1)} reshape(bf16[2,2048,4]{1,2,0:T(4,128)(2,1)} %param.24) | data formatting | bytes 98304 | tf_op jit(solution)/shard_map/convert_element_type | solution.py:465
  30.9 0.1 multiply_reduce_fusion
  31.0 4.6 %fusion.9 = f32[2,32,1,1024]{3,2,1,0:T(1,128)S(1)} fusion(bf16[2,32,64,1024]{3,2,1,0:T(8,128)(2,1)} %bitcast.60, bf16[2,32,64,1]{2,0,1,3:T(2,128)(2,1)S(1)} %get-tuple-element.14), kind=kOutput, calls=%fused_computation.20 | convolution fusion | flops 8388608 | bytes 8658944 | tf_op jit(solution)/shard_map/bhd,bhds->bhs/dot_general | solution.py:460
  35.6 0.1 fusion.5
  35.7 0.2 fusion.6
  36.0 5.9 %fusion.1 = f32[2,32,1,64]{3,2,1,0:T(1,128)S(1)} fusion(bf16[2,32,64,1024]{3,2,1,0:T(8,128)(2,1)} %bitcast.67, bf16[2,32,1024,1]{2,1,0,3:T(8,128)(2,1)S(1)} %get-tuple-element.11), kind=kOutput, calls=%fused_computation.2 | convolution fusion | flops 8388608 | bytes 8536064 | tf_op jit(solution)/shard_map/bhs,bhds->bhd/dot_general | solution.py:479
  42.0 0.1 copy.64
  42.1 0.1 copy.61
  42.4 0.1 mul.109
  42.7 0.1 fusion.7
  42.8 0.7 maximum_bitcast_fusion.part_ref
  43.5 1.9 %copy.71 = bf16[256,8,2,256]{3,1,2,0:T(8,128)(2,1)} copy(bf16[256,8,2,256]{3,2,1,0:T(2,128)(2,1)S(1)} %bitcast.62) | data formatting | bytes 4194304
  45.4 38.2 %shard_map.167 = bf16[2,2048]{1,0:T(2,128)(2,1)} custom-call(f32[32,2,66]{2,1,0:T(2,128)} %maximum_bitcast_fusion.part_ref, bf16[64,2048]{1,0:T(8,128)(2,1)} %w_out_ref.1, bf16[2,2048]{1,0:T(2,128)(2,1)} %states_ref.3, bf16[2048]{0:T(1024)(128)(2,1)} %gain_ref.1, bf16[2048,512]{1,0:T(8,128)(2,1)} %bitcast.61, bf16[256,2048]{1,0:T(8,128)(2,1)} %down_ref.1), custom_call_target="tpu_custom_call" | custom-call | tf_op jit(solution)/shard_map/pallas_call | solution.py:268
  83.6 1.3 %copy.90 = bf16[2,2048]{1,0:T(2,128)(2,1)} copy(bf16[2,2048]{1,0:T(2,128)(2,1)} %shard_map.167) | data formatting | bytes 16384
  (21 shorter events, 0.8 us)
Async XLA Ops:
  35.6 7.0 %copy-start.1 = (bf16[2,2048,4]{1,2,0:T(4,128)(2,1)S(1)}, bf16[2,2048,4]{1,2,0:T(4,128)(2,1)}, u32[]{:S(2)}) copy-start(bf16[2,2048,4]{1,2,0:T(4,128)(2,1)} %param.25) | copy-start | bytes 98308
  35.6 8.0 %copy-start = (bf16[2048,2,256]{2,1,0:T(2,128)(2,1)S(1)}, bf16[2048,2,256]{2,1,0:T(2,128)(2,1)}, u32[]{:S(2)}) copy-start(bf16[2048,2,256]{2,1,0:T(2,128)(2,1)} %param.20) | copy-start | bytes 6291460

commit v11 on v10

--- a/solution.py
+++ b/solution.py
@@ -433,6 +433,10 @@
     angle = new_pos.astype(jnp.float32)[:, None] * inverse[None, :]
     angle = jnp.concatenate([angle] * (4 * heads_here), axis=-1)
     trig = jnp.concatenate([jnp.cos(angle), jnp.sin(angle)], axis=-1)
+    sink_rows = sink_keys.astype(jnp.float32).reshape(
+        rows, lanes * tn // HEAD_SIZE, HEAD_SIZE, sink_keys.shape[2]
+    )
+    states, sink_rows = lax.optimization_barrier((states, sink_rows))
     qkv_all, mine = head(states, attn_gain, jnp.transpose(w_qkv, (1, 2, 0)), trig, tn, 0)
     batch = qkv_all.shape[0]
     keys_all = qkv_all[:, lanes : 2 * lanes]
@@ -462,7 +466,7 @@
     score_win = jnp.where(live, score_win, NEG)
     score_sink = (
         jnp.sum(
-            queries.astype(jnp.float32)[..., None] * sink_key_rows.astype(jnp.float32), axis=2
+            queries.astype(jnp.float32)[..., None] * sink_rows, axis=2
         )
         * 0.125
     )

time: 85.4 us -> 82.5 us (0.966)
  matrix products: 10.5 us -> 7 us
    dot_general x1, matrix products: 5.87 us -> 2.26 us  [per_device(): jnp.einsum('bhs,bhds->bhd', weight_win.astype(jnp.bfloat16), vwin, prefer...]
    convert_element_type x2 -> x1, local copies, waits for them, and re-layouts: 0.87 us -> 0.01 us  [per_device(): queries.astype(jnp.float32)[..., None] * sink_rows]
    reshape x0 -> x1, local copies, waits for them, and re-layouts: none -> 0.87 us  [per_device(): sink_keys.astype(jnp.float32)]
    unnamed x6 -> x10, local copies, waits for them, and re-layouts: 3.16 us -> 3.74 us
where the time goes in v11:
time: 82.5 us; the launch traced here: 82.1 us
  Pallas kernels  61.1 us (74%)
  local copies, waits for them, and re-layouts  9.19 us (11%)
  matrix products  7 us (8%)
  other arithmetic  4 us (5%)
    pallas_call x1, Pallas kernels, tail(): pl.pallas_call(functools.partial(_tail_kernel, n, sn), out_shape=jax.Shap...  38.2 us
    pallas_call x1, Pallas kernels, head(): pl.pallas_call(functools.partial(_head_kernel, n), out_shape=(jax.ShapeDt...  22.9 us
    dot_general x1, matrix products, per_device(): jnp.einsum('bhd,bhds->bhs', queries, kwin, preferred_element_type=jnp.flo...  4.73 us
    unnamed x10, local copies, waits for them, and re-layouts  3.74 us
    dot_general x1, matrix products, per_device(): jnp.einsum('bhs,bhds->bhd', weight_win.astype(jnp.bfloat16), vwin, prefer...  2.26 us

profile of v11, /device:TPU:1, one launch (start us, length us, event | category | flops | bytes accessed | tf_op | source)
XLA Modules:
  0.0 82.1 jit_solution(12449955076573233131)
XLA Ops:
  0.6 0.7 dynamic_slice.6
  1.4 0.7 dynamic_slice.7
  2.1 0.7 convert_element_type.43
  2.8 0.8 compare_and_fusion
  3.6 0.2 fusion.12
  3.9 0.6 pad_maximum_fusion.trig_ref
  4.5 0.9 %reshape.128 = f32[2,32,64,4]{2,1,3,0:T(8,128)S(1)} reshape(bf16[2,2048,4]{1,2,0:T(4,128)(2,1)} %param.24) | data formatting | bytes 98304 | tf_op jit(solution)/shard_map/reshape | solution.py:436
  5.4 22.9 %shard_map.166 = (bf16[64,256]{1,0:T(8,128)(2,1)}, bf16[32,2,256]{2,1,0:T(2,128)(2,1)}) custom-call(bf16[2,2048]{1,0:T(2,128)(2,1)} %states_ref.1, bf16[2048]{0:T(1024)(128)(2,1)} %gains_ref.1, bf16[3,64,2048]{2,1,0:T(8,128)(2,1)} %bitcast.63, f32[64,256]{1,0:T(8,128)} %pad_maximum_fusion.trig_ref), custom_call_target="tpu_custom_call" | custom-call | tf_op jit(solution)/shard_map/pallas_call | solution.py:385
  28.3 0.9 %reshape.135 = bf16[32,2,4,1,64]{4,2,1,0,3:T(4,128)(2,1)S(1)} reshape(bf16[32,2,256]{2,1,0:T(2,128)(2,1)} %get-tuple-element.8) | data formatting | bytes 65536 | tf_op jit(solution)/shard_map/reshape | solution.py:444
  29.3 0.1 fusion.8
  29.5 1.4 %fusion.17 = (bf16[64,64]{1,0:T(8,128)(2,1)}, bf16[64,64]{1,0:T(8,128)(2,1)}) fusion(bf16[64,256]{1,0:T(8,128)(2,1)} %get-tuple-element.10), kind=kLoop, calls=%fused_computation.44 | loop fusion | bytes 32768 | tf_op jit(solution)/shard_map/slice | solution.py:443
  30.9 0.1 multiply_reduce_fusion
  31.1 4.7 %fusion.9 = f32[2,32,1,1024]{3,2,1,0:T(1,128)S(1)} fusion(bf16[2,32,64,1024]{3,2,1,0:T(8,128)(2,1)} %bitcast.60, bf16[2,32,64,1]{2,0,1,3:T(2,128)(2,1)S(1)} %get-tuple-element.18), kind=kOutput, calls=%fused_computation.20 | convolution fusion | flops 8388608 | bytes 8658944 | tf_op jit(solution)/shard_map/bhd,bhds->bhs/dot_general | solution.py:464
  35.8 0.1 fusion.5
  36.0 0.2 fusion.6
  36.2 0.6 slice-done.1
  36.8 2.3 %fusion.1 = f32[2,32,1,64]{3,2,1,0:T(1,128)S(1)} fusion(bf16[2,32,64,1024]{3,2,1,0:T(8,128)(2,1)S(1)} %bitcast.69, bf16[2,32,1024,1]{2,1,0,3:T(8,128)(2,1)S(1)} %get-tuple-element.15), kind=kOutput, calls=%fused_computation.2 | convolution fusion | flops 8388608 | bytes 8536064 | tf_op jit(solution)/shard_map/bhs,bhds->bhd/dot_general | solution.py:483
  39.2 0.1 copy.64
  39.6 0.1 mul.109
  39.9 0.1 fusion.7
  40.0 0.7 maximum_bitcast_fusion.part_ref
  40.8 1.9 %copy.71 = bf16[256,8,2,256]{3,1,2,0:T(8,128)(2,1)} copy(bf16[256,8,2,256]{3,2,1,0:T(2,128)(2,1)S(1)} %bitcast.62) | data formatting | bytes 4194304
  42.6 38.2 %shard_map.167 = bf16[2,2048]{1,0:T(2,128)(2,1)} custom-call(f32[32,2,66]{2,1,0:T(2,128)} %maximum_bitcast_fusion.part_ref, bf16[64,2048]{1,0:T(8,128)(2,1)} %w_out_ref.1, bf16[2,2048]{1,0:T(2,128)(2,1)} %states_ref.1, bf16[2048]{0:T(1024)(128)(2,1)} %gain_ref.1, bf16[2048,512]{1,0:T(8,128)(2,1)} %bitcast.61, bf16[256,2048]{1,0:T(8,128)(2,1)} %down_ref.1), custom_call_target="tpu_custom_call" | custom-call | tf_op jit(solution)/shard_map/pallas_call | solution.py:268
  80.8 1.3 %copy.90 = bf16[2,2048]{1,0:T(2,128)(2,1)} copy(bf16[2,2048]{1,0:T(2,128)(2,1)} %shard_map.167) | data formatting | bytes 16384
  (26 shorter events, 0.9 us)
Async XLA Ops:
  30.9 5.3 %slice-start = ((s8[8388608]{0:T(1024)(128)(4,1)}), s8[4194304]{0:T(1024)(128)(4,1)S(1)}, s32[]{:S(2)}) async-start(s8[8388608]{0:T(1024)(128)(4,1)} %bitcast.67), calls=%async_computation | async-start | bytes 8388608
  31.1 5.7 %slice-start.1 = ((s8[8388608]{0:T(1024)(128)(4,1)}), s8[4194304]{0:T(1024)(128)(4,1)S(1)}, s32[]{:S(2)}) async-start(s8[8388608]{0:T(1024)(128)(4,1)} %bitcast.67), calls=%async_computation.1 | async-start | bytes 8388608
  35.8 3.9 %copy-start.1 = (bf16[2,2048,4]{1,2,0:T(4,128)(2,1)S(1)}, bf16[2,2048,4]{1,2,0:T(4,128)(2,1)}, u32[]{:S(2)}) copy-start(bf16[2,2048,4]{1,2,0:T(4,128)(2,1)} %param.25) | copy-start | bytes 98308
  35.8 4.9 %copy-start = (bf16[2048,2,256]{2,1,0:T(2,128)(2,1)S(1)}, bf16[2048,2,256]{2,1,0:T(2,128)(2,1)}, u32[]{:S(2)}) copy-start(bf16[2048,2,256]{2,1,0:T(2,128)(2,1)} %param.20) | copy-start | bytes 6291460

commit v12 on v11

--- a/solution.py
+++ b/solution.py
@@ -397,7 +397,9 @@
             pltpu.SemaphoreType.DMA((2, n)),
             pltpu.SemaphoreType.DMA(()),
         ],
-        compiler_params=pltpu.CompilerParams(collective_id=cid, has_side_effects=True),
+        compiler_params=pltpu.CompilerParams(
+            collective_id=cid, has_side_effects=True, vmem_limit_bytes=8 * 1024 * 1024
+        ),
     )(states, gains, w_ext, trig)
 
 

time: 82.5 us -> 81.1 us (0.983)
  Pallas kernels: 61.1 us -> 59.3 us
  local copies, waits for them, and re-layouts: 9.19 us -> 10.2 us
    unnamed x10 -> x16, local copies, waits for them, and re-layouts: 3.74 us -> 6.26 us
    pallas_call x1, Pallas kernels: 22.9 us -> 21.1 us  [head(): pl.pallas_call(functools.partial(_head_kernel, n), out_shape=(jax.ShapeDt...]
where the time goes in v12:
time: 81.1 us; the launch traced here: 80.7 us
  Pallas kernels  59.3 us (73%)
  local copies, waits for them, and re-layouts  10.2 us (13%)
  matrix products  7 us (9%)
  other arithmetic  3.38 us (4%)
    pallas_call x1, Pallas kernels, tail(): pl.pallas_call(functools.partial(_tail_kernel, n, sn), out_shape=jax.Shap...  38.2 us
    pallas_call x1, Pallas kernels, head(): pl.pallas_call(functools.partial(_head_kernel, n), out_shape=(jax.ShapeDt...  21.1 us
    unnamed x16, local copies, waits for them, and re-layouts  6.26 us
    dot_general x1, matrix products, per_device(): jnp.einsum('bhd,bhds->bhs', queries, kwin, preferred_element_type=jnp.flo...  4.73 us
    dot_general x1, matrix products, per_device(): jnp.einsum('bhs,bhds->bhd', weight_win.astype(jnp.bfloat16), vwin, prefer...  2.26 us

profile of v12, /device:TPU:1, one launch (start us, length us, event | category | flops | bytes accessed | tf_op | source)
XLA Modules:
  0.0 80.7 jit_solution(13373254432446098711)
XLA Ops:
  0.6 0.7 dynamic_slice.6
  1.4 0.7 dynamic_slice.7
  2.1 0.7 convert_element_type.43
  2.8 0.8 compare_and_fusion
  3.6 0.2 fusion.12
  3.9 0.9 %reshape.128 = f32[2,32,64,4]{2,1,3,0:T(8,128)S(1)} reshape(bf16[2,2048,4]{1,2,0:T(4,128)(2,1)} %param.24) | data formatting | bytes 98304 | tf_op jit(solution)/shard_map/reshape | solution.py:438
  4.8 1.1 %copy-done = bf16[2048,3,64]{0,2,1:T(8,128)(2,1)S(1)} copy-done((bf16[2048,3,64]{0,2,1:T(8,128)(2,1)S(1)}, bf16[2048,3,64]{0,2,1:T(8,128)(2,1)}, u32[]{:S(2)}) %copy-start) | copy-done | bytes 786456
  5.9 0.7 copy-done.1
  6.6 0.7 copy-done.2
  7.3 21.1 %shard_map.166 = (bf16[64,256]{1,0:T(8,128)(2,1)S(1)}, bf16[32,2,256]{2,1,0:T(2,128)(2,1)S(1)}) custom-call(bf16[2,2048]{1,0:T(2,128)(2,1)S(1)} %copy-done.1, bf16[2048]{0:T(1024)(128)(2,1)S(1)} %copy-done.2, bf16[3,64,2048]{2,1,0:T(8,128)(2,1)S(1)} %bitcast.60, f32[64,256]{1,0:T(8,128)S(1)} %pad_maximum_fusion.trig_ref), custom_call_target="tpu_custom_call" | custom-call | tf_op jit(solution)/shard_map/pallas_call | solution.py:385
  28.4 0.1 reshape.135
  28.6 0.1 fusion.8
  28.8 0.7 fusion.17
  29.5 0.1 multiply_reduce_fusion
  29.6 4.7 %fusion.9 = f32[2,32,1,1024]{3,2,1,0:T(1,128)S(1)} fusion(bf16[2,32,64,1024]{3,2,1,0:T(8,128)(2,1)} %bitcast.61, bf16[2,32,64,1]{2,0,1,3:T(2,128)(2,1)S(1)} %get-tuple-element.18), kind=kOutput, calls=%fused_computation.20 | convolution fusion | flops 8388608 | bytes 8658944 | tf_op jit(solution)/shard_map/bhd,bhds->bhs/dot_general | solution.py:466
  34.4 0.1 fusion.5
  34.5 0.2 fusion.6
  34.8 0.6 slice-done.1
  35.4 2.3 %fusion.1 = f32[2,32,1,64]{3,2,1,0:T(1,128)S(1)} fusion(bf16[2,32,64,1024]{3,2,1,0:T(8,128)(2,1)S(1)} %bitcast.69, bf16[2,32,1024,1]{2,1,0,3:T(8,128)(2,1)S(1)} %get-tuple-element.15), kind=kOutput, calls=%fused_computation.2 | convolution fusion | flops 8388608 | bytes 8536064 | tf_op jit(solution)/shard_map/bhs,bhds->bhd/dot_general | solution.py:485
  38.2 0.1 mul.109
  38.6 0.7 maximum_bitcast_fusion.part_ref
  39.3 1.9 %copy.71 = bf16[256,8,2,256]{3,1,2,0:T(8,128)(2,1)} copy(bf16[256,8,2,256]{3,2,1,0:T(2,128)(2,1)S(1)} %bitcast.63) | data formatting | bytes 4194304
  41.2 38.2 %shard_map.167 = bf16[2,2048]{1,0:T(2,128)(2,1)} custom-call(f32[32,2,66]{2,1,0:T(2,128)} %maximum_bitcast_fusion.part_ref, bf16[64,2048]{1,0:T(8,128)(2,1)} %w_out_ref.1, bf16[2,2048]{1,0:T(2,128)(2,1)} %states_ref.1, bf16[2048]{0:T(1024)(128)(2,1)} %gain_ref.1, bf16[2048,512]{1,0:T(8,128)(2,1)} %bitcast.62, bf16[256,2048]{1,0:T(8,128)(2,1)} %down_ref.1), custom_call_target="tpu_custom_call" | custom-call | tf_op jit(solution)/shard_map/pallas_call | solution.py:268
  79.4 1.3 %copy.90 = bf16[2,2048]{1,0:T(2,128)(2,1)} copy(bf16[2,2048]{1,0:T(2,128)(2,1)} %shard_map.167) | data formatting | bytes 16384
  (32 shorter events, 1.1 us)
Async XLA Ops:
  4.8 1.1 %copy-start = (bf16[2048,3,64]{0,2,1:T(8,128)(2,1)S(1)}, bf16[2048,3,64]{0,2,1:T(8,128)(2,1)}, u32[]{:S(2)}) copy-start(bf16[2048,3,64]{0,2,1:T(8,128)(2,1)} %param.17) | copy-start | bytes 2359300
  5.9 0.7 copy-start.1
  6.6 0.7 copy-start.2
  29.5 5.3 %slice-start = ((s8[8388608]{0:T(1024)(128)(4,1)}), s8[4194304]{0:T(1024)(128)(4,1)S(1)}, s32[]{:S(2)}) async-start(s8[8388608]{0:T(1024)(128)(4,1)} %bitcast.67), calls=%async_computation | async-start | bytes 8388608
  29.6 5.7 %slice-start.1 = ((s8[8388608]{0:T(1024)(128)(4,1)}), s8[4194304]{0:T(1024)(128)(4,1)S(1)}, s32[]{:S(2)}) async-start(s8[8388608]{0:T(1024)(128)(4,1)} %bitcast.67), calls=%async_computation.1 | async-start | bytes 8388608
  34.4 3.9 %copy-start.4 = (bf16[2,2048,4]{1,2,0:T(4,128)(2,1)S(1)}, bf16[2,2048,4]{1,2,0:T(4,128)(2,1)}, u32[]{:S(2)}) copy-start(bf16[2,2048,4]{1,2,0:T(4,128)(2,1)} %param.25) | copy-start | bytes 98308
  34.4 4.9 %copy-start.3 = (bf16[2048,2,256]{2,1,0:T(2,128)(2,1)S(1)}, bf16[2048,2,256]{2,1,0:T(2,128)(2,1)}, u32[]{:S(2)}) copy-start(bf16[2048,2,256]{2,1,0:T(2,128)(2,1)} %param.20) | copy-start | bytes 6291460

commit v13 on v12

--- a/solution.py
+++ b/solution.py
@@ -112,6 +112,7 @@
     gate_ref,
     down_ref,
     out_ref,
+    resid_ref,
     seq_buf,
     att_buf,
     seq_send,
@@ -256,8 +257,8 @@
     down = jnp.dot(hidden, down_ref[...], preferred_element_type=jnp.float32)
     qbuf[...] = down.astype(jnp.bfloat16)
     phase(3, row_block(qbuf), lambda k: rbuf2.at[k])
-    summed2 = jnp.sum(rbuf2[...].astype(jnp.float32), axis=0)
-    out_ref[...] = (sbuf[...].astype(jnp.float32) + summed2).astype(out_ref.dtype)
+    out_ref[...] = jnp.sum(rbuf2[...].astype(jnp.float32), axis=0)
+    resid_ref[...] = sbuf[...]
 
 
 def tail(part, w_out, states, gain, w_gate_up, w_down, n, sn, cid):
@@ -267,9 +268,12 @@
     vmem = pl.BlockSpec(memory_space=pltpu.VMEM)
     return pl.pallas_call(
         functools.partial(_tail_kernel, n, sn),
-        out_shape=jax.ShapeDtypeStruct((rows, width), states.dtype),
+        out_shape=(
+            jax.ShapeDtypeStruct((rows, width), jnp.float32),
+            jax.ShapeDtypeStruct((rows, width), states.dtype),
+        ),
         in_specs=[vmem] * 6,
-        out_specs=vmem,
+        out_specs=(vmem, vmem),
         scratch_shapes=[
             pltpu.VMEM((sn,) + part.shape, jnp.float32),
             pltpu.VMEM((n, rows, lanes), jnp.bfloat16),
@@ -298,7 +302,6 @@
     me = lax.axis_index(axis)
     rows = x_ref.shape[0]
     block = qkv_ref.shape[1] // 2
-    x_ref[...] = rms_norm(states_ref[...].astype(jnp.float32), gains_ref[...].reshape(1, -1))
     barrier = pltpu.get_barrier_semaphore()
 
     def greet(d, carry):
@@ -308,6 +311,7 @@
         return carry
 
     lax.fori_loop(1, n, greet, 0)
+    x_ref[...] = rms_norm(states_ref[...].astype(jnp.float32), gains_ref[...].reshape(1, -1))
     pl.semaphore_wait(barrier, n - 1)
 
     def phase(p, src_of, dst_of):
@@ -491,7 +495,8 @@
     mixture = mixture + undo_round(weight_new)[..., None] * values_new.astype(jnp.float32)
     packed = jnp.concatenate([mixture, total[..., None], local_top[..., None]], axis=-1)
     packed = jnp.transpose(packed, (1, 0, 2))
-    out_states = tail(packed, w_out, states, mlp_gain, w_gate_up, w_down, tn, sn, 3)
+    mlp_out, resid_part = tail(packed, w_out, states, mlp_gain, w_gate_up, w_down, tn, sn, 3)
+    out_states = (resid_part.astype(jnp.float32) + mlp_out).astype(jnp.bfloat16)
     return (out_states, keys_all, values_all)
 
 

time: 81.1 us -> 80.7 us (level)
  local copies, waits for them, and re-layouts: 10.2 us -> 8.86 us
  other arithmetic: 3.38 us -> 4.7 us
    unnamed x16 -> x15, local copies, waits for them, and re-layouts: 6.26 us -> 4.91 us
    convert_element_type x0 -> x1, other arithmetic: none -> 1.33 us  [per_device(): out_states = (resid_part.astype(jnp.float32) + mlp_out).astype(jnp.bfloat16)]
where the time goes in v13:
time: 80.7 us; the launch traced here: 80.3 us
  Pallas kernels  58.9 us (73%)
  local copies, waits for them, and re-layouts  8.86 us (11%)
  matrix products  7 us (9%)
  other arithmetic  4.7 us (6%)
    pallas_call x1, Pallas kernels, tail(): pl.pallas_call(functools.partial(_tail_kernel, n, sn), out_shape=(jax.Sha...  38.1 us
    pallas_call x1, Pallas kernels, head(): pl.pallas_call(functools.partial(_head_kernel, n), out_shape=(jax.ShapeDt...  20.8 us
    unnamed x15, local copies, waits for them, and re-layouts  4.91 us
    dot_general x1, matrix products, per_device(): jnp.einsum('bhd,bhds->bhs', queries, kwin, preferred_element_type=jnp.flo...  4.73 us
    dot_general x1, matrix products, per_device(): jnp.einsum('bhs,bhds->bhd', weight_win.astype(jnp.bfloat16), vwin, prefer...  2.27 us

profile of v13, /device:TPU:1, one launch (start us, length us, event | category | flops | bytes accessed | tf_op | source)
XLA Modules:
  0.0 80.3 jit_solution(11719738968770250547)
XLA Ops:
  0.6 0.7 dynamic_slice.6
  1.4 0.7 dynamic_slice.7
  2.1 0.7 convert_element_type.49
  2.8 0.8 compare_and_fusion
  3.6 0.2 fusion.12
  3.9 0.9 %reshape.128 = f32[2,32,64,4]{2,1,3,0:T(8,128)S(1)} reshape(bf16[2,2048,4]{1,2,0:T(4,128)(2,1)} %param.24) | data formatting | bytes 98304 | tf_op jit(solution)/shard_map/reshape | solution.py:442
  4.8 1.1 %copy-done = bf16[2048,3,64]{0,2,1:T(8,128)(2,1)S(1)} copy-done((bf16[2048,3,64]{0,2,1:T(8,128)(2,1)S(1)}, bf16[2048,3,64]{0,2,1:T(8,128)(2,1)}, u32[]{:S(2)}) %copy-start) | copy-done | bytes 786456
  5.9 0.7 copy-done.1
  6.6 0.7 copy-done.2
  7.3 20.8 %shard_map.166 = (bf16[64,256]{1,0:T(8,128)(2,1)S(1)}, bf16[32,2,256]{2,1,0:T(2,128)(2,1)S(1)}) custom-call(bf16[2,2048]{1,0:T(2,128)(2,1)S(1)} %copy-done.1, bf16[2048]{0:T(1024)(128)(2,1)S(1)} %copy-done.2, bf16[3,64,2048]{2,1,0:T(8,128)(2,1)S(1)} %bitcast.60, f32[64,256]{1,0:T(8,128)S(1)} %pad_maximum_fusion.trig_ref), custom_call_target="tpu_custom_call" | custom-call | tf_op jit(solution)/shard_map/pallas_call | solution.py:389
  28.1 0.1 reshape.135
  28.2 0.1 fusion.8
  28.4 0.7 fusion.17
  29.2 0.1 multiply_reduce_fusion
  29.3 4.7 %fusion.9 = f32[2,32,1,1024]{3,2,1,0:T(1,128)S(1)} fusion(bf16[2,32,64,1024]{3,2,1,0:T(8,128)(2,1)} %bitcast.61, bf16[2,32,64,1]{2,0,1,3:T(2,128)(2,1)S(1)} %get-tuple-element.22), kind=kOutput, calls=%fused_computation.20 | convolution fusion | flops 8388608 | bytes 8658944 | tf_op jit(solution)/shard_map/bhd,bhds->bhs/dot_general | solution.py:470
  34.0 0.1 fusion.5
  34.2 0.2 fusion.6
  34.5 0.6 slice-done.1
  35.0 2.3 %fusion.1 = f32[2,32,1,64]{3,2,1,0:T(1,128)S(1)} fusion(bf16[2,32,64,1024]{3,2,1,0:T(8,128)(2,1)S(1)} %bitcast.69, bf16[2,32,1024,1]{2,1,0,3:T(8,128)(2,1)S(1)} %get-tuple-element.19), kind=kOutput, calls=%fused_computation.2 | convolution fusion | flops 8388608 | bytes 8536064 | tf_op jit(solution)/shard_map/bhs,bhds->bhd/dot_general | solution.py:489
  37.9 0.1 mul.109
  38.3 0.7 maximum_bitcast_fusion.part_ref
  39.0 1.8 %copy.71 = bf16[256,8,2,256]{3,1,2,0:T(8,128)(2,1)} copy(bf16[256,8,2,256]{3,2,1,0:T(2,128)(2,1)S(1)} %bitcast.63) | data formatting | bytes 4194304
  40.8 38.1 %shard_map.167 = (f32[2,2048]{1,0:T(2,128)}, bf16[2,2048]{1,0:T(2,128)(2,1)}) custom-call(f32[32,2,66]{2,1,0:T(2,128)} %maximum_bitcast_fusion.part_ref, bf16[64,2048]{1,0:T(8,128)(2,1)} %w_out_ref.1, bf16[2,2048]{1,0:T(2,128)(2,1)} %states_ref.1, bf16[2048]{0:T(1024)(128)(2,1)} %gain_ref.1, bf16[2048,512]{1,0:T(8,128)(2,1)} %bitcast.62, ...), custom_call_target="tpu_custom_call" | custom-call | tf_op jit(solution)/shard_map/pallas_call | solution.py:269
  78.9 1.3 %add_convert_fusion = bf16[2,2048]{1,0:T(2,128)(2,1)} fusion(f32[2,2048]{1,0:T(2,128)} %get-tuple-element.13, bf16[2,2048]{1,0:T(2,128)(2,1)} %get-tuple-element.12), kind=kLoop, calls=%fused_computation.28 | loop fusion | flops 12288 | bytes 32768 | tf_op jit(solution)/shard_map/convert_element_type | solution.py:499
  (32 shorter events, 1.1 us)
Async XLA Ops:
  4.8 1.1 %copy-start = (bf16[2048,3,64]{0,2,1:T(8,128)(2,1)S(1)}, bf16[2048,3,64]{0,2,1:T(8,128)(2,1)}, u32[]{:S(2)}) copy-start(bf16[2048,3,64]{0,2,1:T(8,128)(2,1)} %param.17) | copy-start | bytes 2359300
  5.9 0.7 copy-start.1
  6.6 0.7 copy-start.2
  29.1 5.3 %slice-start = ((s8[8388608]{0:T(1024)(128)(4,1)}), s8[4194304]{0:T(1024)(128)(4,1)S(1)}, s32[]{:S(2)}) async-start(s8[8388608]{0:T(1024)(128)(4,1)} %bitcast.67), calls=%async_computation | async-start | bytes 8388608
  29.3 5.7 %slice-start.1 = ((s8[8388608]{0:T(1024)(128)(4,1)}), s8[4194304]{0:T(1024)(128)(4,1)S(1)}, s32[]{:S(2)}) async-start(s8[8388608]{0:T(1024)(128)(4,1)} %bitcast.67), calls=%async_computation.1 | async-start | bytes 8388608
  34.0 3.9 %copy-start.4 = (bf16[2,2048,4]{1,2,0:T(4,128)(2,1)S(1)}, bf16[2,2048,4]{1,2,0:T(4,128)(2,1)}, u32[]{:S(2)}) copy-start(bf16[2,2048,4]{1,2,0:T(4,128)(2,1)} %param.25) | copy-start | bytes 98308
  34.0 4.9 %copy-start.3 = (bf16[2048,2,256]{2,1,0:T(2,128)(2,1)S(1)}, bf16[2048,2,256]{2,1,0:T(2,128)(2,1)}, u32[]{:S(2)}) copy-start(bf16[2048,2,256]{2,1,0:T(2,128)(2,1)} %param.20) | copy-start | bytes 6291460

commit v14 on v12

--- a/solution.py
+++ b/solution.py
@@ -287,7 +287,9 @@
             pltpu.SemaphoreType.DMA((4, n)),
             pltpu.SemaphoreType.DMA(()),
         ],
-        compiler_params=pltpu.CompilerParams(collective_id=cid, has_side_effects=True),
+        compiler_params=pltpu.CompilerParams(
+            collective_id=cid, has_side_effects=True, vmem_limit_bytes=32 * 1024 * 1024
+        ),
     )(part, w_out, states, gain, w_gate_up.reshape(width, 2 * units), w_down)
 
 

time: 81.1 us -> 81.2 us (level)
  other arithmetic: 3.38 us -> 5.78 us
  Pallas kernels: 59.3 us -> 57 us
  local copies, waits for them, and re-layouts: 10.2 us -> 9.34 us
    pallas_call x1, Pallas kernels: 38.2 us -> 35.9 us  [tail(): pl.pallas_call(functools.partial(_tail_kernel, n, sn), out_shape=jax.Shap...]
    unnamed x16 -> x24, local copies, waits for them, and re-layouts: 6.26 us -> 4.17 us
    reduce_sum x1, other arithmetic: 0.06 us -> 0.9 us  [per_device(): jnp.sum(undo_round(weight_sink)[:, :, None, :] * vsink.astype(jnp.float32...]
where the time goes in v14:
time: 81.2 us; the launch traced here: 80.6 us
  Pallas kernels  57 us (70%)
  local copies, waits for them, and re-layouts  9.34 us (12%)
  matrix products  7.62 us (9%)
  other arithmetic  5.78 us (7%)
  between operations  0.87 us (1%)
    pallas_call x1, Pallas kernels, tail(): pl.pallas_call(functools.partial(_tail_kernel, n, sn), out_shape=jax.Shap...  35.9 us
    pallas_call x1, Pallas kernels, head(): pl.pallas_call(functools.partial(_head_kernel, n), out_shape=(jax.ShapeDt...  21.1 us
    dot_general x1, matrix products, per_device(): jnp.einsum('bhd,bhds->bhs', queries, kwin, preferred_element_type=jnp.flo...  4.73 us
    unnamed x24, local copies, waits for them, and re-layouts  4.17 us
    dot_general x1, matrix products, per_device(): jnp.einsum('bhs,bhds->bhd', weight_win.astype(jnp.bfloat16), vwin, prefer...  2.89 us

profile of v14, /device:TPU:1, one launch (start us, length us, event | category | flops | bytes accessed | tf_op | source)
XLA Modules:
  0.0 80.6 jit_solution(15764220695703476217)
XLA Ops:
  0.6 0.7 dynamic_slice.6
  1.4 0.7 dynamic_slice.7
  2.1 0.7 convert_element_type.43
  2.8 0.8 compare_and_fusion
  3.6 0.2 fusion.12
  3.9 0.9 %reshape.128 = f32[2,32,64,4]{2,1,3,0:T(8,128)S(1)} reshape(bf16[2,2048,4]{1,2,0:T(4,128)(2,1)} %param.24) | data formatting | bytes 98304 | tf_op jit(solution)/shard_map/reshape | solution.py:440
  4.8 1.1 %copy-done.1 = bf16[2048,3,64]{0,2,1:T(8,128)(2,1)S(1)} copy-done((bf16[2048,3,64]{0,2,1:T(8,128)(2,1)S(1)}, bf16[2048,3,64]{0,2,1:T(8,128)(2,1)}, u32[]{:S(2)}) %copy-start.1) | copy-done | bytes 786456
  5.9 0.7 copy-done.3
  6.6 0.7 copy-done.5
  7.3 21.1 %shard_map.166 = (bf16[64,256]{1,0:T(8,128)(2,1)S(1)}, bf16[32,2,256]{2,1,0:T(2,128)(2,1)S(1)}) custom-call(bf16[2,2048]{1,0:T(2,128)(2,1)S(1)} %copy-done.3, bf16[2048]{0:T(1024)(128)(2,1)S(1)} %copy-done.5, bf16[3,64,2048]{2,1,0:T(8,128)(2,1)S(1)} %bitcast.61, f32[64,256]{1,0:T(8,128)S(1)} %pad_maximum_fusion.trig_ref), custom_call_target="tpu_custom_call" | custom-call | tf_op jit(solution)/shard_map/pallas_call | solution.py:387
  28.8 0.7 fusion.17
  29.7 4.7 %fusion.9 = f32[2,32,1,1024]{3,2,1,0:T(1,128)S(1)} fusion(bf16[2,32,64,1024]{3,2,1,0:T(8,128)(2,1)} %bitcast.62, bf16[2,32,64,1]{2,0,1,3:T(2,128)(2,1)S(1)} %get-tuple-element.18), kind=kOutput, calls=%fused_computation.20 | convolution fusion | flops 8388608 | bytes 8658944 | tf_op jit(solution)/shard_map/bhd,bhds->bhs/dot_general | solution.py:468
  34.6 0.2 fusion.6
  34.9 0.5 slice-done.1
  35.4 2.9 %fusion.1 = f32[2,32,1,64]{3,2,1,0:T(1,128)} fusion(bf16[2,32,64,1024]{3,2,1,0:T(8,128)(2,1)S(1)} %bitcast.69, bf16[2,32,1024,1]{2,1,0,3:T(8,128)(2,1)S(1)} %get-tuple-element.15), kind=kOutput, calls=%fused_computation.2 | convolution fusion | flops 8388608 | bytes 8536064 | tf_op jit(solution)/shard_map/bhs,bhds->bhd/dot_general | solution.py:487
  38.3 0.7 copy.60
  39.3 0.7 select_add_fusion
  40.0 0.7 mul.109
  40.8 0.9 %multiply_reduce_fusion.1 = f32[2,2048]{1,0:T(2,128)S(1)} fusion(f32[2,2048,4]{1,2,0:T(4,128)} %mul.109, bf16[2,2048,4]{1,2,0:T(4,128)(2,1)} %param.25), kind=kLoop, calls=%fused_computation.12 | loop fusion | flops 45056 | bytes 114688 | tf_op jit(solution)/shard_map/reduce_sum | solution.py:490
  41.8 0.9 %fusion.7 = f32[2,32,64]{2,0,1:T(2,128)S(1)} fusion(f32[2,32,1,64]{3,2,1,0:T(1,128)} %fusion.1, f32[2,32,64]{2,1,0:T(8,128)S(1)} %reduce_sum.50, bf16[2,4,32,64]{3,0,2,1:T(2,128)(2,1)} %bitcast.66, f32[2,32]{0,1:T(8,128)} %copy.60), kind=kLoop, calls=%fused_computation.16 | loop fusion | flops 16384 | bytes 57600 | tf_op jit(solution)/shard_map/add | solution.py:493
  42.7 0.9 %maximum_bitcast_fusion.part_ref = f32[32,2,66]{2,1,0:T(2,128)S(1)} fusion(f32[2,32,1]{2,0,1:T(2,128)} %get-tuple-element.14, f32[2,32,1]{2,0,1:T(2,128)} %get-tuple-element.13, f32[2,32,64]{2,0,1:T(2,128)S(1)} %fusion.7), kind=kLoop, calls=%fused_computation.14 | loop fusion | flops 8448 | bytes 33792 | tf_op jit(solution)/shard_map/transpose | solution.py:495
  43.6 0.5 copy.71
  44.1 35.9 %shard_map.167 = bf16[2,2048]{1,0:T(2,128)(2,1)S(1)} custom-call(f32[32,2,66]{2,1,0:T(2,128)S(1)} %maximum_bitcast_fusion.part_ref, bf16[64,2048]{1,0:T(8,128)(2,1)S(1)} %copy-done.2, bf16[2,2048]{1,0:T(2,128)(2,1)S(1)} %copy-done.4, bf16[2048]{0:T(1024)(128)(2,1)S(1)} %copy-done.6, bf16[2048,512]{1,0:T(8,128)(2,1)S(1)} %bitcast.60, ...), custom_call_target="tpu_custom_call" | custom-call | tf_op jit(solution)/shard_map/pallas_call | solution.py:268
  80.0 0.6 copy.90
  (40 shorter events, 1.3 us)
Async XLA Ops:
  4.8 1.1 %copy-start.1 = (bf16[2048,3,64]{0,2,1:T(8,128)(2,1)S(1)}, bf16[2048,3,64]{0,2,1:T(8,128)(2,1)}, u32[]{:S(2)}) copy-start(bf16[2048,3,64]{0,2,1:T(8,128)(2,1)} %param.17) | copy-start | bytes 2359300
  5.9 0.7 copy-start.3
  6.6 0.7 copy-start.5
  28.6 1.1 %copy-start.8 = (bf16[32,2,4,1,64]{4,1,0,2,3:T(2,128)(2,1)}, bf16[32,2,4,1,64]{4,1,0,2,3:T(2,128)(2,1)S(1)}, u32[]{:S(2)}) copy-start(bf16[32,2,4,1,64]{4,1,0,2,3:T(2,128)(2,1)S(1)} %copy.88) | copy-start | bytes 98308
  29.5 5.4 %slice-start = ((s8[8388608]{0:T(1024)(128)(4,1)}), s8[4194304]{0:T(1024)(128)(4,1)S(1)}, s32[]{:S(2)}) async-start(s8[8388608]{0:T(1024)(128)(4,1)} %bitcast.67), calls=%async_computation | async-start | bytes 8388608
  29.7 5.7 %slice-start.1 = ((s8[8388608]{0:T(1024)(128)(4,1)}), s8[4194304]{0:T(1024)(128)(4,1)S(1)}, s32[]{:S(2)}) async-start(s8[8388608]{0:T(1024)(128)(4,1)} %bitcast.67), calls=%async_computation.1 | async-start | bytes 8388608
  34.4 9.2 %copy-start.7 = (bf16[2048,2,256]{2,1,0:T(2,128)(2,1)S(1)}, bf16[2048,2,256]{2,1,0:T(2,128)(2,1)}, u32[]{:S(2)}) copy-start(bf16[2048,2,256]{2,1,0:T(2,128)(2,1)} %param.20) | copy-start | bytes 6291460
  34.4 9.7 %copy-start = (bf16[256,2048]{1,0:T(8,128)(2,1)S(1)}, bf16[256,2048]{1,0:T(8,128)(2,1)}, u32[]{:S(2)}) copy-start(bf16[256,2048]{1,0:T(8,128)(2,1)} %down_ref.1) | copy-start | bytes 3145732
  34.4 9.7 %copy-start.2 = (bf16[64,2048]{1,0:T(8,128)(2,1)S(1)}, bf16[64,2048]{1,0:T(8,128)(2,1)}, u32[]{:S(2)}) copy-start(bf16[64,2048]{1,0:T(8,128)(2,1)} %w_out_ref.1) | copy-start | bytes 786436
  34.4 9.7 %copy-start.4 = (bf16[2,2048]{1,0:T(2,128)(2,1)S(1)}, bf16[2,2048]{1,0:T(2,128)(2,1)}, u32[]{:S(2)}) copy-start(bf16[2,2048]{1,0:T(2,128)(2,1)} %states_ref.1) | copy-start | bytes 24580
  34.4 9.7 %copy-start.6 = (bf16[2048]{0:T(1024)(128)(2,1)S(1)}, bf16[2048]{0:T(1024)(128)(2,1)}, u32[]{:S(2)}) copy-start(bf16[2048]{0:T(1024)(128)(2,1)} %gain_ref.1) | copy-start | bytes 12292

commit v15 on v12

--- a/solution.py
+++ b/solution.py
@@ -449,8 +449,11 @@
     keys_new = mine[:, 1]
     values_new = mine[:, 2]
     all_heads = queries.shape[1]
-    own_len = lax.dynamic_slice_in_dim(cache_len, row_start, rows, 0)
-    own_pos = lax.dynamic_slice_in_dim(new_pos, row_start, rows, 0)
+    pick = jnp.arange(cache_len.shape[0], dtype=jnp.int32)[None, :] == (
+        row_start + jnp.arange(rows, dtype=jnp.int32)
+    )[:, None]
+    own_len = jnp.sum(jnp.where(pick, cache_len[None, :], 0), axis=1)
+    own_pos = jnp.sum(jnp.where(pick, new_pos[None, :], 0), axis=1)
     window_here = key_cache.shape[2]
     seq_index = lax.axis_index("seq")
     slots = seq_index * window_here + jnp.arange(window_here, dtype=jnp.int32)

time: 81.1 us -> 80.5 us (level)
  local copies, waits for them, and re-layouts: 10.2 us -> 8.75 us
  other arithmetic: 3.38 us -> 4.27 us
    dynamic_slice x2 -> x0, local copies, waits for them, and re-layouts: 1.46 us -> none  [the longest x1 0.74 us: per_device(): own_len = lax.dynamic_slice_in_dim(cache_len, row_start, rows, 0)]
    reduce_sum x0 -> x1, other arithmetic: none -> 0.89 us  [per_device(): own_len = jnp.sum(jnp.where(pick, cache_len[None, :], 0), axis=1)]
where the time goes in v15:
time: 80.5 us; the launch traced here: 80.1 us
  Pallas kernels  59.3 us (74%)
  local copies, waits for them, and re-layouts  8.75 us (11%)
  matrix products  7 us (9%)
  other arithmetic  4.27 us (5%)
  between operations  0.81 us (1%)
    pallas_call x1, Pallas kernels, tail(): pl.pallas_call(functools.partial(_tail_kernel, n, sn), out_shape=jax.Shap...  38.2 us
    pallas_call x1, Pallas kernels, head(): pl.pallas_call(functools.partial(_head_kernel, n), out_shape=(jax.ShapeDt...  21.1 us
    unnamed x16, local copies, waits for them, and re-layouts  6.26 us
    dot_general x1, matrix products, per_device(): jnp.einsum('bhd,bhds->bhs', queries, kwin, preferred_element_type=jnp.flo...  4.73 us
    dot_general x1, matrix products, per_device(): jnp.einsum('bhs,bhds->bhd', weight_win.astype(jnp.bfloat16), vwin, prefer...  2.26 us

profile of v15, /device:TPU:1, one launch (start us, length us, event | category | flops | bytes accessed | tf_op | source)
XLA Modules:
  0.0 80.1 jit_solution(10269622099785927157)
XLA Ops:
  0.6 0.7 convert_element_type.43
  1.3 0.9 %select_reduce_fusion.1 = (s32[2]{0:T(128)S(1)}, s32[2]{0:T(128)S(1)}) fusion(s32[64]{0:T(128)} %param.26, s32[2]{0:T(128)S(1)} %iota_add_fusion.1, s32[64]{0:T(128)} %param.29), kind=kLoop, calls=%fused_computation.39 | loop fusion | flops 636 | bytes 536 | tf_op jit(solution)/shard_map/reduce_sum | solution.py:455
  2.2 0.8 compare_and_fusion
  3.1 0.2 fusion.12
  3.3 0.9 %reshape.134 = f32[2,32,64,4]{2,1,3,0:T(8,128)S(1)} reshape(bf16[2,2048,4]{1,2,0:T(4,128)(2,1)} %param.24) | data formatting | bytes 98304 | tf_op jit(solution)/shard_map/reshape | solution.py:438
  4.2 1.1 %copy-done = bf16[2048,3,64]{0,2,1:T(8,128)(2,1)S(1)} copy-done((bf16[2048,3,64]{0,2,1:T(8,128)(2,1)S(1)}, bf16[2048,3,64]{0,2,1:T(8,128)(2,1)}, u32[]{:S(2)}) %copy-start) | copy-done | bytes 786456
  5.3 0.7 copy-done.1
  6.0 0.7 copy-done.2
  6.7 21.1 %shard_map.166 = (bf16[64,256]{1,0:T(8,128)(2,1)S(1)}, bf16[32,2,256]{2,1,0:T(2,128)(2,1)S(1)}) custom-call(bf16[2,2048]{1,0:T(2,128)(2,1)S(1)} %copy-done.1, bf16[2048]{0:T(1024)(128)(2,1)S(1)} %copy-done.2, bf16[3,64,2048]{2,1,0:T(8,128)(2,1)S(1)} %bitcast.60, f32[64,256]{1,0:T(8,128)S(1)} %pad_maximum_fusion.trig_ref), custom_call_target="tpu_custom_call" | custom-call | tf_op jit(solution)/shard_map/pallas_call | solution.py:385
  27.8 0.1 reshape.141
  28.0 0.1 fusion.8
  28.2 0.7 fusion.17
  28.9 0.1 multiply_reduce_fusion
  29.1 4.7 %fusion.9 = f32[2,32,1,1024]{3,2,1,0:T(1,128)S(1)} fusion(bf16[2,32,64,1024]{3,2,1,0:T(8,128)(2,1)} %bitcast.61, bf16[2,32,64,1]{2,0,1,3:T(2,128)(2,1)S(1)} %get-tuple-element.20), kind=kOutput, calls=%fused_computation.20 | convolution fusion | flops 8388608 | bytes 8658944 | tf_op jit(solution)/shard_map/bhd,bhds->bhs/dot_general | solution.py:469
  33.8 0.1 fusion.5
  34.0 0.2 fusion.6
  34.2 0.6 slice-done.1
  34.8 2.3 %fusion.1 = f32[2,32,1,64]{3,2,1,0:T(1,128)S(1)} fusion(bf16[2,32,64,1024]{3,2,1,0:T(8,128)(2,1)S(1)} %bitcast.69, bf16[2,32,1024,1]{2,1,0,3:T(8,128)(2,1)S(1)} %get-tuple-element.17), kind=kOutput, calls=%fused_computation.2 | convolution fusion | flops 8388608 | bytes 8536064 | tf_op jit(solution)/shard_map/bhs,bhds->bhd/dot_general | solution.py:488
  37.2 0.1 copy.64
  37.6 0.1 mul.109
  38.0 0.7 maximum_bitcast_fusion.part_ref
  38.8 1.9 %copy.71 = bf16[256,8,2,256]{3,1,2,0:T(8,128)(2,1)} copy(bf16[256,8,2,256]{3,2,1,0:T(2,128)(2,1)S(1)} %bitcast.63) | data formatting | bytes 4194304
  40.6 38.2 %shard_map.167 = bf16[2,2048]{1,0:T(2,128)(2,1)} custom-call(f32[32,2,66]{2,1,0:T(2,128)} %maximum_bitcast_fusion.part_ref, bf16[64,2048]{1,0:T(8,128)(2,1)} %w_out_ref.1, bf16[2,2048]{1,0:T(2,128)(2,1)} %states_ref.1, bf16[2048]{0:T(1024)(128)(2,1)} %gain_ref.1, bf16[2048,512]{1,0:T(8,128)(2,1)} %bitcast.62, bf16[256,2048]{1,0:T(8,128)(2,1)} %down_ref.1), custom_call_target="tpu_custom_call" | custom-call | tf_op jit(solution)/shard_map/pallas_call | solution.py:268
  78.8 1.3 %copy.90 = bf16[2,2048]{1,0:T(2,128)(2,1)} copy(bf16[2,2048]{1,0:T(2,128)(2,1)} %shard_map.167) | data formatting | bytes 16384
  (32 shorter events, 1.0 us)
Async XLA Ops:
  4.2 1.1 %copy-start = (bf16[2048,3,64]{0,2,1:T(8,128)(2,1)S(1)}, bf16[2048,3,64]{0,2,1:T(8,128)(2,1)}, u32[]{:S(2)}) copy-start(bf16[2048,3,64]{0,2,1:T(8,128)(2,1)} %param.17) | copy-start | bytes 2359300
  5.3 0.7 copy-start.1
  6.0 0.7 copy-start.2
  28.9 5.3 %slice-start = ((s8[8388608]{0:T(1024)(128)(4,1)}), s8[4194304]{0:T(1024)(128)(4,1)S(1)}, s32[]{:S(2)}) async-start(s8[8388608]{0:T(1024)(128)(4,1)} %bitcast.67), calls=%async_computation | async-start | bytes 8388608
  29.1 5.7 %slice-start.1 = ((s8[8388608]{0:T(1024)(128)(4,1)}), s8[4194304]{0:T(1024)(128)(4,1)S(1)}, s32[]{:S(2)}) async-start(s8[8388608]{0:T(1024)(128)(4,1)} %bitcast.67), calls=%async_computation.1 | async-start | bytes 8388608
  33.8 3.9 %copy-start.4 = (bf16[2,2048,4]{1,2,0:T(4,128)(2,1)S(1)}, bf16[2,2048,4]{1,2,0:T(4,128)(2,1)}, u32[]{:S(2)}) copy-start(bf16[2,2048,4]{1,2,0:T(4,128)(2,1)} %param.25) | copy-start | bytes 98308
  33.8 4.9 %copy-start.3 = (bf16[2048,2,256]{2,1,0:T(2,128)(2,1)S(1)}, bf16[2048,2,256]{2,1,0:T(2,128)(2,1)}, u32[]{:S(2)}) copy-start(bf16[2048,2,256]{2,1,0:T(2,128)(2,1)} %param.20) | copy-start | bytes 6291460

commit v16 on v15

--- a/solution.py
+++ b/solution.py
@@ -251,8 +251,10 @@
     sbuf[...] = resid
     nbuf[...] = rms_norm(resid.astype(jnp.float32), gain_ref[...].reshape(1, -1))
     phase(2, lambda j: nbuf, row_block(gbuf))
-    gate_up = jnp.dot(gbuf[...], gate_ref[...], preferred_element_type=jnp.float32)
-    hidden = (jax.nn.silu(gate_up[:, :units]) * gate_up[:, units:]).astype(jnp.bfloat16)
+    gathered = gbuf[...]
+    gate = jnp.dot(gathered, gate_ref[:, 0, :], preferred_element_type=jnp.float32)
+    up = jnp.dot(gathered, gate_ref[:, 1, :], preferred_element_type=jnp.float32)
+    hidden = (jax.nn.silu(gate) * up).astype(jnp.bfloat16)
     down = jnp.dot(hidden, down_ref[...], preferred_element_type=jnp.float32)
     qbuf[...] = down.astype(jnp.bfloat16)
     phase(3, row_block(qbuf), lambda k: rbuf2.at[k])
@@ -288,7 +290,7 @@
             pltpu.SemaphoreType.DMA(()),
         ],
         compiler_params=pltpu.CompilerParams(collective_id=cid, has_side_effects=True),
-    )(part, w_out, states, gain, w_gate_up.reshape(width, 2 * units), w_down)
+    )(part, w_out, states, gain, w_gate_up, w_down)
 
 
 def _head_kernel(

time: 80.5 us -> 82.1 us (1.020)
  Pallas kernels: 59.3 us -> 62.7 us
  local copies, waits for them, and re-layouts: 8.75 us -> 6.89 us
    pallas_call x1, Pallas kernels: 38.2 us -> 41.6 us  [tail(): pl.pallas_call(functools.partial(_tail_kernel, n, sn), out_shape=jax.Shap...]
    unnamed x16 -> x13, local copies, waits for them, and re-layouts: 6.26 us -> 4.41 us
where the time goes in v16:
time: 82.1 us; the launch traced here: 81.7 us
  Pallas kernels  62.7 us (76%)
  matrix products  7 us (9%)
  local copies, waits for them, and re-layouts  6.89 us (8%)
  other arithmetic  4.27 us (5%)
    pallas_call x1, Pallas kernels, tail(): pl.pallas_call(functools.partial(_tail_kernel, n, sn), out_shape=jax.Shap...  41.6 us
    pallas_call x1, Pallas kernels, head(): pl.pallas_call(functools.partial(_head_kernel, n), out_shape=(jax.ShapeDt...  21.1 us
    dot_general x1, matrix products, per_device(): jnp.einsum('bhd,bhds->bhs', queries, kwin, preferred_element_type=jnp.flo...  4.73 us
    unnamed x13, local copies, waits for them, and re-layouts  4.41 us
    dot_general x1, matrix products, per_device(): jnp.einsum('bhs,bhds->bhd', weight_win.astype(jnp.bfloat16), vwin, prefer...  2.26 us

profile of v16, /device:TPU:1, one launch (start us, length us, event | category | flops | bytes accessed | tf_op | source)
XLA Modules:
  0.0 81.7 jit_solution(6593215365423317255)
XLA Ops:
  0.6 0.7 convert_element_type.43
  1.3 0.9 %select_reduce_fusion.1 = (s32[2]{0:T(128)S(1)}, s32[2]{0:T(128)S(1)}) fusion(s32[64]{0:T(128)} %param.26, s32[2]{0:T(128)S(1)} %iota_add_fusion.1, s32[64]{0:T(128)} %param.29), kind=kLoop, calls=%fused_computation.39 | loop fusion | flops 636 | bytes 536 | tf_op jit(solution)/shard_map/reduce_sum | solution.py:457
  2.2 0.8 compare_and_fusion
  3.1 0.2 fusion.12
  3.3 0.9 %reshape.130 = f32[2,32,64,4]{2,1,3,0:T(8,128)S(1)} reshape(bf16[2,2048,4]{1,2,0:T(4,128)(2,1)} %param.24) | data formatting | bytes 98304 | tf_op jit(solution)/shard_map/reshape | solution.py:440
  4.2 1.1 %copy-done = bf16[2048,3,64]{0,2,1:T(8,128)(2,1)S(1)} copy-done((bf16[2048,3,64]{0,2,1:T(8,128)(2,1)S(1)}, bf16[2048,3,64]{0,2,1:T(8,128)(2,1)}, u32[]{:S(2)}) %copy-start) | copy-done | bytes 786456
  5.3 0.7 copy-done.1
  6.0 0.7 copy-done.2
  6.7 21.1 %shard_map.166 = (bf16[64,256]{1,0:T(8,128)(2,1)S(1)}, bf16[32,2,256]{2,1,0:T(2,128)(2,1)S(1)}) custom-call(bf16[2,2048]{1,0:T(2,128)(2,1)S(1)} %copy-done.1, bf16[2048]{0:T(1024)(128)(2,1)S(1)} %copy-done.2, bf16[3,64,2048]{2,1,0:T(8,128)(2,1)S(1)} %bitcast.58, f32[64,256]{1,0:T(8,128)S(1)} %pad_maximum_fusion.trig_ref), custom_call_target="tpu_custom_call" | custom-call | tf_op jit(solution)/shard_map/pallas_call | solution.py:387
  27.8 0.1 reshape.137
  28.0 0.1 fusion.8
  28.2 0.7 fusion.17
  28.9 0.1 multiply_reduce_fusion
  29.1 4.7 %fusion.9 = f32[2,32,1,1024]{3,2,1,0:T(1,128)S(1)} fusion(bf16[2,32,64,1024]{3,2,1,0:T(8,128)(2,1)} %bitcast.59, bf16[2,32,64,1]{2,0,1,3:T(2,128)(2,1)S(1)} %get-tuple-element.20), kind=kOutput, calls=%fused_computation.20 | convolution fusion | flops 8388608 | bytes 8658944 | tf_op jit(solution)/shard_map/bhd,bhds->bhs/dot_general | solution.py:471
  33.8 0.1 fusion.5
  34.0 0.2 fusion.6
  34.2 0.6 slice-done.1
  34.8 2.3 %fusion.1 = f32[2,32,1,64]{3,2,1,0:T(1,128)S(1)} fusion(bf16[2,32,64,1024]{3,2,1,0:T(8,128)(2,1)S(1)} %bitcast.65, bf16[2,32,1024,1]{2,1,0,3:T(8,128)(2,1)S(1)} %get-tuple-element.17), kind=kOutput, calls=%fused_computation.2 | convolution fusion | flops 8388608 | bytes 8536064 | tf_op jit(solution)/shard_map/bhs,bhds->bhd/dot_general | solution.py:490
  37.2 0.1 copy.64
  37.6 0.1 mul.109
  37.9 0.1 fusion.7
  38.0 0.7 maximum_bitcast_fusion.part_ref
  38.8 41.6 %shard_map.167 = bf16[2,2048]{1,0:T(2,128)(2,1)} custom-call(f32[32,2,66]{2,1,0:T(2,128)} %maximum_bitcast_fusion.part_ref, bf16[64,2048]{1,0:T(8,128)(2,1)} %w_out_ref.1, bf16[2,2048]{1,0:T(2,128)(2,1)} %states_ref.1, bf16[2048]{0:T(1024)(128)(2,1)} %gain_ref.1, bf16[2048,2,256]{2,1,0:T(2,128)(2,1)} %gate_ref.1, bf16[256,2048]{1,0:T(8,128)(2,1)} %down_ref.1), custom_call_target="tpu_custom_call" | custom-call | tf_op jit(solution)/shard_map/pallas_call | solution.py:270
  80.4 1.3 %copy.89 = bf16[2,2048]{1,0:T(2,128)(2,1)} copy(bf16[2,2048]{1,0:T(2,128)(2,1)} %shard_map.167) | data formatting | bytes 16384
  (29 shorter events, 0.9 us)
Async XLA Ops:
  4.2 1.1 %copy-start = (bf16[2048,3,64]{0,2,1:T(8,128)(2,1)S(1)}, bf16[2048,3,64]{0,2,1:T(8,128)(2,1)}, u32[]{:S(2)}) copy-start(bf16[2048,3,64]{0,2,1:T(8,128)(2,1)} %param.17) | copy-start | bytes 2359300
  5.3 0.7 copy-start.1
  6.0 0.7 copy-start.2
  28.9 5.3 %slice-start = ((s8[8388608]{0:T(1024)(128)(4,1)}), s8[4194304]{0:T(1024)(128)(4,1)S(1)}, s32[]{:S(2)}) async-start(s8[8388608]{0:T(1024)(128)(4,1)} %bitcast.63), calls=%async_computation | async-start | bytes 8388608
  29.1 5.7 %slice-start.1 = ((s8[8388608]{0:T(1024)(128)(4,1)}), s8[4194304]{0:T(1024)(128)(4,1)S(1)}, s32[]{:S(2)}) async-start(s8[8388608]{0:T(1024)(128)(4,1)} %bitcast.63), calls=%async_computation.1 | async-start | bytes 8388608
  33.8 3.9 %copy-start.3 = (bf16[2,2048,4]{1,2,0:T(4,128)(2,1)S(1)}, bf16[2,2048,4]{1,2,0:T(4,128)(2,1)}, u32[]{:S(2)}) copy-start(bf16[2,2048,4]{1,2,0:T(4,128)(2,1)} %param.25) | copy-start | bytes 98308

commit v17 on v15

--- a/solution.py
+++ b/solution.py
@@ -298,7 +298,6 @@
     me = lax.axis_index(axis)
     rows = x_ref.shape[0]
     block = qkv_ref.shape[1] // 2
-    x_ref[...] = rms_norm(states_ref[...].astype(jnp.float32), gains_ref[...].reshape(1, -1))
     barrier = pltpu.get_barrier_semaphore()
 
     def greet(d, carry):
@@ -308,6 +307,7 @@
         return carry
 
     lax.fori_loop(1, n, greet, 0)
+    x_ref[...] = rms_norm(states_ref[...].astype(jnp.float32), gains_ref[...].reshape(1, -1))
     pl.semaphore_wait(barrier, n - 1)
 
     def phase(p, src_of, dst_of):

time: 80.5 us -> 80.2 us (level)
  no operation moved by 1% of the time
where the time goes in v17:
time: 80.2 us; the launch traced here: 79.7 us
  Pallas kernels  58.9 us (73%)
  local copies, waits for them, and re-layouts  8.75 us (11%)
  matrix products  7 us (9%)
  other arithmetic  4.27 us (5%)
  between operations  0.81 us (1%)
    pallas_call x1, Pallas kernels, tail(): pl.pallas_call(functools.partial(_tail_kernel, n, sn), out_shape=jax.Shap...  38.2 us
    pallas_call x1, Pallas kernels, head(): pl.pallas_call(functools.partial(_head_kernel, n), out_shape=(jax.ShapeDt...  20.8 us
    unnamed x16, local copies, waits for them, and re-layouts  6.26 us
    dot_general x1, matrix products, per_device(): jnp.einsum('bhd,bhds->bhs', queries, kwin, preferred_element_type=jnp.flo...  4.73 us
    dot_general x1, matrix products, per_device(): jnp.einsum('bhs,bhds->bhd', weight_win.astype(jnp.bfloat16), vwin, prefer...  2.26 us

profile of v17, /device:TPU:1, one launch (start us, length us, event | category | flops | bytes accessed | tf_op | source)
XLA Modules:
  0.0 79.7 jit_solution(17185847303740509373)
XLA Ops:
  0.6 0.7 convert_element_type.43
  1.3 0.9 %select_reduce_fusion.1 = (s32[2]{0:T(128)S(1)}, s32[2]{0:T(128)S(1)}) fusion(s32[64]{0:T(128)} %param.26, s32[2]{0:T(128)S(1)} %iota_add_fusion.1, s32[64]{0:T(128)} %param.29), kind=kLoop, calls=%fused_computation.39 | loop fusion | flops 636 | bytes 536 | tf_op jit(solution)/shard_map/reduce_sum | solution.py:455
  2.2 0.8 %compare_and_fusion = pred[2,1024]{1,0:T(4,128)(4,1)S(1)} fusion(s32[2,1024]{1,0:T(2,128)} %param.28, s32[2,1024]{1,0:T(2,128)} %param.27, s32[2]{0:T(128)S(1)} %get-tuple-element.12, s32[1024]{0:T(1024)S(1)} %iota_add_fusion, s32[2]{0:T(128)S(1)} %get-tuple-element.11), kind=kLoop, calls=%fused_computation.29 | loop fusion | flops 16384 | bytes 22544 | tf_op jit(solution)/shard_map/and | solution.py:461
  3.1 0.2 fusion.12
  3.3 0.9 %reshape.134 = f32[2,32,64,4]{2,1,3,0:T(8,128)S(1)} reshape(bf16[2,2048,4]{1,2,0:T(4,128)(2,1)} %param.24) | data formatting | bytes 98304 | tf_op jit(solution)/shard_map/reshape | solution.py:438
  4.2 1.1 %copy-done = bf16[2048,3,64]{0,2,1:T(8,128)(2,1)S(1)} copy-done((bf16[2048,3,64]{0,2,1:T(8,128)(2,1)S(1)}, bf16[2048,3,64]{0,2,1:T(8,128)(2,1)}, u32[]{:S(2)}) %copy-start) | copy-done | bytes 786456
  5.3 0.7 copy-done.1
  6.0 0.7 copy-done.2
  6.7 20.8 %shard_map.166 = (bf16[64,256]{1,0:T(8,128)(2,1)S(1)}, bf16[32,2,256]{2,1,0:T(2,128)(2,1)S(1)}) custom-call(bf16[2,2048]{1,0:T(2,128)(2,1)S(1)} %copy-done.1, bf16[2048]{0:T(1024)(128)(2,1)S(1)} %copy-done.2, bf16[3,64,2048]{2,1,0:T(8,128)(2,1)S(1)} %bitcast.60, f32[64,256]{1,0:T(8,128)S(1)} %pad_maximum_fusion.trig_ref), custom_call_target="tpu_custom_call" | custom-call | tf_op jit(solution)/shard_map/pallas_call | solution.py:385
  27.5 0.1 reshape.141
  27.7 0.1 fusion.8
  27.9 0.7 fusion.17
  28.6 0.1 multiply_reduce_fusion
  28.8 4.7 %fusion.9 = f32[2,32,1,1024]{3,2,1,0:T(1,128)S(1)} fusion(bf16[2,32,64,1024]{3,2,1,0:T(8,128)(2,1)} %bitcast.61, bf16[2,32,64,1]{2,0,1,3:T(2,128)(2,1)S(1)} %get-tuple-element.20), kind=kOutput, calls=%fused_computation.20 | convolution fusion | flops 8388608 | bytes 8658944 | tf_op jit(solution)/shard_map/bhd,bhds->bhs/dot_general | solution.py:469
  33.5 0.1 fusion.5
  33.6 0.2 fusion.6
  33.9 0.6 slice-done.1
  34.5 2.3 %fusion.1 = f32[2,32,1,64]{3,2,1,0:T(1,128)S(1)} fusion(bf16[2,32,64,1024]{3,2,1,0:T(8,128)(2,1)S(1)} %bitcast.69, bf16[2,32,1024,1]{2,1,0,3:T(8,128)(2,1)S(1)} %get-tuple-element.17), kind=kOutput, calls=%fused_computation.2 | convolution fusion | flops 8388608 | bytes 8536064 | tf_op jit(solution)/shard_map/bhs,bhds->bhd/dot_general | solution.py:488
  36.8 0.1 copy.64
  37.3 0.1 mul.109
  37.7 0.7 maximum_bitcast_fusion.part_ref
  38.4 1.9 %copy.71 = bf16[256,8,2,256]{3,1,2,0:T(8,128)(2,1)} copy(bf16[256,8,2,256]{3,2,1,0:T(2,128)(2,1)S(1)} %bitcast.63) | data formatting | bytes 4194304
  40.3 38.2 %shard_map.167 = bf16[2,2048]{1,0:T(2,128)(2,1)} custom-call(f32[32,2,66]{2,1,0:T(2,128)} %maximum_bitcast_fusion.part_ref, bf16[64,2048]{1,0:T(8,128)(2,1)} %w_out_ref.1, bf16[2,2048]{1,0:T(2,128)(2,1)} %states_ref.1, bf16[2048]{0:T(1024)(128)(2,1)} %gain_ref.1, bf16[2048,512]{1,0:T(8,128)(2,1)} %bitcast.62, bf16[256,2048]{1,0:T(8,128)(2,1)} %down_ref.1), custom_call_target="tpu_custom_call" | custom-call | tf_op jit(solution)/shard_map/pallas_call | solution.py:268
  78.4 1.3 %copy.90 = bf16[2,2048]{1,0:T(2,128)(2,1)} copy(bf16[2,2048]{1,0:T(2,128)(2,1)} %shard_map.167) | data formatting | bytes 16384
  (32 shorter events, 1.0 us)
Async XLA Ops:
  4.2 1.1 %copy-start = (bf16[2048,3,64]{0,2,1:T(8,128)(2,1)S(1)}, bf16[2048,3,64]{0,2,1:T(8,128)(2,1)}, u32[]{:S(2)}) copy-start(bf16[2048,3,64]{0,2,1:T(8,128)(2,1)} %param.17) | copy-start | bytes 2359300
  5.3 0.7 copy-start.1
  6.0 0.7 copy-start.2
  28.6 5.3 %slice-start = ((s8[8388608]{0:T(1024)(128)(4,1)}), s8[4194304]{0:T(1024)(128)(4,1)S(1)}, s32[]{:S(2)}) async-start(s8[8388608]{0:T(1024)(128)(4,1)} %bitcast.67), calls=%async_computation | async-start | bytes 8388608
  28.7 5.7 %slice-start.1 = ((s8[8388608]{0:T(1024)(128)(4,1)}), s8[4194304]{0:T(1024)(128)(4,1)S(1)}, s32[]{:S(2)}) async-start(s8[8388608]{0:T(1024)(128)(4,1)} %bitcast.67), calls=%async_computation.1 | async-start | bytes 8388608
  33.5 3.9 %copy-start.4 = (bf16[2,2048,4]{1,2,0:T(4,128)(2,1)S(1)}, bf16[2,2048,4]{1,2,0:T(4,128)(2,1)}, u32[]{:S(2)}) copy-start(bf16[2,2048,4]{1,2,0:T(4,128)(2,1)} %param.25) | copy-start | bytes 98308
  33.5 4.9 %copy-start.3 = (bf16[2048,2,256]{2,1,0:T(2,128)(2,1)S(1)}, bf16[2048,2,256]{2,1,0:T(2,128)(2,1)}, u32[]{:S(2)}) copy-start(bf16[2048,2,256]{2,1,0:T(2,128)(2,1)} %param.20) | copy-start | bytes 6291460
